TPU v7x, 512 devices: a whole 4x8x8 slice. The times are simulated.
512 devices in a mesh: grp: 4 (over x), node: 128 (over z, y, core).
Axes of the slice: x: 4, y: 8, z: 8, core: 2. Of those that a mesh axis runs over, the one named last changes fastest.
Arguments:
- start_block: float32 [64, 65536], P(None, ('grp', 'node')), may hold values from -24 to 24
- weight_tiles: bfloat16 [512, 12, 128, 128], P(('grp', 'node')), may hold values from -0.15625 to 0.15625
- tile_scales: float32 [512, 12], P(('grp', 'node')), may hold values from 0.5 to 2
- neighbour_ids: int32 [512, 12], P(('grp', 'node')), may hold values from 0 to 511, as said below
- live_counts: int32 [512], P(('grp', 'node')), may hold values from 1 to 12
- row_order: int32 [512, 128], P(('grp', 'node')), may hold values from 0 to 127, each once within a row
Outputs:
- embedding: float32 [64, 65536], P(None, ('grp', 'node'))
- ritz: float32 [64, 64], replicated
- start_theta: float32 [64, 64], replicated
Inputs may be any that keep to these rules, and one draw needn't show every extreme that they name: `neighbour_ids`: row tile t belongs to device t in group-major order. Every id names a row tile of a device of any group whose node index differs from that of row tile t by at most 2, around the cycle of 128. Ids may repeat within a row tile; unused slots also hold such ids.
All inputs are finite; a program needn't handle non-finite values.
Results may differ from a plain program's by a relative error of at most 0.002.
The roundings to bfloat16 on the way count: a program that leaves them out, or rounds other values in their place, can miss the bound.
Values may be sent and summed in bfloat16 or wider, within the bound.
No kernel may reach another device: no remote copies, remote signals or barrier semaphores. Data moves between devices by JAX's collectives and lax.ppermute only.
A program may use at most 64 MiB of HBM per device.

v0:
```python
import jax
import jax.numpy as jnp
from jax import lax
from jax.sharding import PartitionSpec as P

REACH = 2
NSUB = 4
STEPS = 2


def shifted(value, axis, steps):
    count = lax.axis_size(axis)
    pairs = [(source, (source + steps) % count) for source in range(count)]
    return lax.ppermute(value, axis, pairs)


def symmetric(matrix):
    return 0.5 * (matrix + matrix.T)


def exact_dot(left, right):
    return jnp.dot(left, right, precision=lax.Precision.HIGHEST, preferred_element_type=jnp.float32)


def lower_solve(factor, rhs, transposed):
    return lax.linalg.triangular_solve(
        factor, rhs, left_side=True, lower=True, transpose_a=transposed
    )


def rayleigh(gram_basis, gram_operator, columns):
    order = gram_basis.shape[0]
    chol_basis = jnp.linalg.cholesky(gram_basis)
    half = lower_solve(chol_basis, symmetric(gram_operator), False)
    projected = symmetric(lower_solve(chol_basis, half.T, False))
    scale = jnp.sqrt(jnp.sum(projected * projected) + 1e-06)
    filtered = projected / scale + 1.25 * jnp.eye(order, dtype=jnp.float32)
    square = exact_dot(filtered, filtered)
    fourth = exact_dot(square, square)
    basis = jnp.eye(order, dtype=jnp.float32)[:, :columns]
    for sweep in range(NSUB):
        image = exact_dot(fourth, basis)
        chol_image = jnp.linalg.cholesky(exact_dot(image.T, image))
        basis = lower_solve(chol_image, image.T, False).T
    coeffs = lower_solve(chol_basis, basis, True)
    ritz_now = symmetric(exact_dot(basis.T, exact_dot(projected, basis)))
    return (coeffs, ritz_now)


def local(start_block, weight_tiles, tile_scales, neighbour_ids, live_counts, row_order):
    columns = start_block.shape[0]
    rows_dev = start_block.shape[1]
    tiles_dev = weight_tiles.shape[0]
    tile = weight_tiles.shape[2]
    groups = lax.axis_size("grp")
    nodes = lax.axis_size("node")
    here = lax.axis_index("node")
    width = 2 * REACH + 1
    group_index = neighbour_ids // (nodes * tiles_dev)
    node_index = neighbour_ids // tiles_dev % nodes
    tile_index = neighbour_ids % tiles_dev
    offset_index = (node_index - here + REACH + nodes) % nodes
    slot_iota = jnp.arange(neighbour_ids.shape[1], dtype=jnp.int32)[None, :]
    weights = jnp.where(slot_iota < live_counts[:, None], tile_scales, jnp.float32(0.0))

    def operate(values):
        rounded = values.astype(jnp.bfloat16)
        grouped = lax.all_gather(rounded[None], "grp", axis=0, tiled=True)
        blocks = []
        for offset in range(-REACH, REACH + 1):
            if offset == 0:
                blocks.append(grouped)
            else:
                blocks.append(shifted(grouped, "node", -offset))
        stacked = jnp.stack(blocks)
        window = stacked.reshape(width, groups, columns, tiles_dev, tile)
        picked = window[offset_index, group_index, :, tile_index, :]
        product = jnp.einsum(
            "tscj,tsij->ctsi", picked, weight_tiles, preferred_element_type=jnp.float32
        )
        summed = jnp.sum(product * weights[None, :, :, None], axis=2)
        return summed.reshape(columns, rows_dev)

    total_rows = rows_dev * groups * nodes
    start_gram = lax.psum(exact_dot(start_block, start_block.T), ("grp", "node"))
    start_chol = jnp.linalg.cholesky(start_gram)
    block = lower_solve(start_chol, start_block, False)
    applied = operate(block)
    theta = symmetric(lax.psum(exact_dot(block, applied.T), ("grp", "node")))
    start_theta = jnp.sqrt(jnp.float32(total_rows)) * theta
    momentum = None
    applied_momentum = None
    ritz = theta
    for step in range(STEPS):
        residual = applied - exact_dot(theta, block)
        applied_residual = operate(residual)
        if momentum is None:
            trial = jnp.concatenate([block, residual], axis=0)
            applied_trial = jnp.concatenate([applied, applied_residual], axis=0)
        else:
            trial = jnp.concatenate([block, residual, momentum], axis=0)
            applied_trial = jnp.concatenate([applied, applied_residual, applied_momentum], axis=0)
        gram_basis, gram_operator = lax.psum(
            (exact_dot(trial, trial.T), exact_dot(trial, applied_trial.T)), ("grp", "node")
        )
        coeffs, ritz = rayleigh(gram_basis, gram_operator, columns)
        lower_coeffs = coeffs[columns:]
        block = exact_dot(coeffs.T, trial)
        applied = exact_dot(coeffs.T, applied_trial)
        momentum = exact_dot(lower_coeffs.T, trial[columns:])
        applied_momentum = exact_dot(lower_coeffs.T, applied_trial[columns:])
        theta = ritz
    scaled = jnp.sqrt(jnp.float32(total_rows)) * block
    permuted = scaled[:, row_order[0]]
    pieces = permuted.reshape(columns, nodes, rows_dev // nodes)
    arrived = lax.all_to_all(pieces, "node", split_axis=1, concat_axis=1, tiled=True)
    embedding = arrived.reshape(columns, rows_dev)
    return (embedding, ritz, start_theta)


def solution(mesh):
    return jax.shard_map(
        local,
        mesh=mesh,
        in_specs=(
            P(None, ("grp", "node")),
            P(("grp", "node"), None, None, None),
            P(("grp", "node"), None),
            P(("grp", "node"), None),
            P(("grp", "node")),
            P(("grp", "node"), None),
        ),
        out_specs=(P(None, ("grp", "node")), P(), P()),
        check_vma=False,
    )
```

profile of v0, /device:TPU:1, one launch (start us, length us, event | category | flops | bytes accessed | tf_op | source)
XLA Modules:
  0.0 1052.9 jit_solution(10396621836252823110)
XLA Ops:
  8.2 106.2 %psum.42 = f32[64,64]{0,1:T(8,128)S(1)} all-reduce(f32[64,64]{0,1:T(8,128)S(1)} %fusion.157), channel_id=1, replica_groups=mesh['grp'=4,'node'=128] {'grp','node'}, use_global_device_ids=true, to_apply=%region_0.1 | all-reduce | flops 4096 | bytes 32768 | tf_op jit(solution)/shard_map/psum | solution.py:85
  114.5 5.8 cholesky.328
  126.9 9.0 all-gather
  138.3 6.0 collective-permute-start.1
  146.3 6.3 collective-permute-start.3
  156.8 96.0 %psum.43 = f32[64,64]{1,0:T(8,128)S(1)} all-reduce(f32[64,64]{1,0:T(8,128)S(1)} %fusion.158), channel_id=1, replica_groups=mesh['grp'=4,'node'=128] {'grp','node'}, use_global_device_ids=true, to_apply=%region_4.7 | all-reduce | flops 4096 | bytes 32768 | tf_op jit(solution)/shard_map/psum | solution.py:89
  253.1 9.0 all-gather.1
  264.3 5.5 collective-permute-start.5
  272.0 6.6 collective-permute-start.7
  282.1 259.4 %all-reduce.12.cloned.1.call-done = (f32[128,128]{0,1:T(8,128)}, f32[128,128]{0,1:T(8,128)}) async-done(((f32[128,128]{0,1:T(8,128)}, f32[128,128]{0,1:T(8,128)}), (f32[128,128]{0,1:T(8,128)}, f32[128,128]{0,1:T(8,128)})) %all-reduce.12.cloned.1.call-update) | async-done | bytes 131088 | tf_op jit(solution)/shard_map/psum | solution.py:103
  542.5 11.7 %cholesky.105 = f32[128,128]{1,0:T(8,128)S(1)} custom-call(f32[128,128]{1,0:T(8,128)S(1)} %fusion.54), custom_call_target="Cholesky" | custom-call | tf_op jit(solution)/shard_map/jit(cholesky)/cholesky | solution.py:33
  555.6 9.8 custom-call.34
  568.4 5.8 cholesky.339
  581.3 5.8 cholesky.350
  594.2 6.2 cholesky.361
  601.8 4.9 custom-call.57
  607.4 5.8 cholesky.372
  614.6 4.9 custom-call.58
  621.3 9.0 all-gather.2
  633.5 6.6 collective-permute-start.9
  642.0 5.5 collective-permute-start.11
  651.5 262.4 %all-reduce.10.cloned.1.call-done = (f32[192,192]{0,1:T(8,128)}, f32[192,192]{0,1:T(8,128)}) async-done(((f32[192,192]{0,1:T(8,128)}, f32[192,192]{0,1:T(8,128)}), (f32[192,192]{0,1:T(8,128)}, f32[192,192]{0,1:T(8,128)})) %all-reduce.10.cloned.1.call-update) | async-done | bytes 294928 | tf_op jit(solution)/shard_map/psum | solution.py:103
  916.0 11.7 %cholesky.175 = f32[128,128]{1,0:T(8,128)S(1)} custom-call(f32[128,128]{1,0:T(8,128)S(1)} %cholesky.425), custom_call_target="Cholesky" | custom-call | tf_op jit(solution)/shard_map/jit(cholesky)/cholesky | solution.py:33
  927.8 9.8 custom-call.35
  938.0 5.8 cholesky.191
  946.6 19.8 %custom-call.36 = f32[2,128,128]{1,2,0:T(8,128)S(1)} custom-call(f32[2,128,128]{2,1,0:T(8,128)S(1)} %pad_maximum_fusion.1), custom_call_target="InvertDiagBlocksLowerTriangular" | custom-call | tf_op jit(solution)/shard_map/triangular_solve | solution.py:26
  971.3 5.8 cholesky.383
  984.3 5.8 cholesky.394
  997.3 5.8 cholesky.405
  1010.3 5.8 cholesky.416
  1025.7 8.0 all-to-all-start
  1034.3 10.8 %all-to-all-done = f32[64,128,1]{0,2,1:T(1,128)S(1)} async-done(((f32[64,128,1]{0,2,1:T(1,128)}), f32[64,128,1]{0,2,1:T(1,128)S(1)}, u32[]{:S(2)}, u32[]{:S(2)}) %all-to-all-start) | async-done | bytes 32800 | tf_op jit(solution)/shard_map/all_to_all | solution.py:116
  (219 shorter events, 96.4 us)
Async XLA Ops:
  7.2 149.1 %copy-start = (bf16[1,12,128,128]{3,2,1,0:T(8,128)(2,1)S(1)}, bf16[1,12,128,128]{3,2,1,0:T(8,128)(2,1)}, u32[]{:S(2)}) copy-start(bf16[1,12,128,128]{3,2,1,0:T(8,128)(2,1)} %param.16) | copy-start | bytes 1179652
  7.2 534.3 %all-reduce.12.cloned.1.call-start = ((), (), s32[]{:S(2)}) async-start(), calls=%async_computation.2 | async-start | bytes 262144 | tf_op jit(solution)/shard_map/psum | solution.py:103
  121.0 5.6 copy-start.3
  135.8 19.6 %collective-permute-start = (bf16[4,64,128]{2,1,0:T(8,128)(2,1)S(1)}, bf16[4,64,128]{2,1,0:T(8,128)(2,1)S(1)}, u32[]{:S(2)}, u32[]{:S(2)}) collective-permute-start(bf16[4,64,128]{2,1,0:T(8,128)(2,1)S(1)} %bitcast.372), channel_id=1, source_target_pairs={{0,2},{1,3},{2,4},{3,5},{4,6},{5,7},{6,8},{7,9},{8,10},{9,11},{10,... | collective-permute-start | bytes 196616 | tf_op jit(solution)/shard_map/ppermute | solution.py:14
  138.3 17.2 %collective-permute-start.1 = (bf16[4,64,128]{2,1,0:T(8,128)(2,1)S(1)}, bf16[4,64,128]{2,1,0:T(8,128)(2,1)S(1)}, u32[]{:S(2)}, u32[]{:S(2)}) collective-permute-start(bf16[4,64,128]{2,1,0:T(8,128)(2,1)S(1)} %bitcast.373), channel_id=1, source_target_pairs={{0,1},{1,2},{2,3},{3,4},{4,5},{5,6},{6,7},{7,8},{8,9},{9,10},{10,1... | collective-permute-start | bytes 196616 | tf_op jit(solution)/shard_map/ppermute | solution.py:14
  144.4 11.2 %collective-permute-start.2 = (bf16[4,64,128]{2,1,0:T(8,128)(2,1)S(1)}, bf16[4,64,128]{2,1,0:T(8,128)(2,1)S(1)}, u32[]{:S(2)}, u32[]{:S(2)}) collective-permute-start(bf16[4,64,128]{2,1,0:T(8,128)(2,1)S(1)} %bitcast.374), channel_id=1, source_target_pairs={{0,127},{1,0},{2,1},{3,2},{4,3},{5,4},{6,5},{7,6},{8,7},{9,8},{10,... | collective-permute-start | bytes 196616 | tf_op jit(solution)/shard_map/ppermute | solution.py:14
  146.3 9.3 collective-permute-start.3
  152.7 0.7 copy-start.6
  154.1 0.7 copy-start.7
  154.8 0.7 copy-start.8
  262.1 17.4 %collective-permute-start.4 = (bf16[4,64,128]{2,1,0:T(8,128)(2,1)S(1)}, bf16[4,64,128]{2,1,0:T(8,128)(2,1)S(1)}, u32[]{:S(2)}, u32[]{:S(2)}) collective-permute-start(bf16[4,64,128]{2,1,0:T(8,128)(2,1)S(1)} %bitcast.382), channel_id=1, source_target_pairs={{0,2},{1,3},{2,4},{3,5},{4,6},{5,7},{6,8},{7,9},{8,10},{9,11},{10,... | collective-permute-start | bytes 196616 | tf_op jit(solution)/shard_map/ppermute | solution.py:14
  264.3 15.2 %collective-permute-start.5 = (bf16[4,64,128]{2,1,0:T(8,128)(2,1)S(1)}, bf16[4,64,128]{2,1,0:T(8,128)(2,1)S(1)}, u32[]{:S(2)}, u32[]{:S(2)}) collective-permute-start(bf16[4,64,128]{2,1,0:T(8,128)(2,1)S(1)} %bitcast.383), channel_id=1, source_target_pairs={{0,1},{1,2},{2,3},{3,4},{4,5},{5,6},{6,7},{7,8},{8,9},{9,10},{10,1... | collective-permute-start | bytes 196616 | tf_op jit(solution)/shard_map/ppermute | solution.py:14
  269.8 9.7 collective-permute-start.6
  272.0 7.9 collective-permute-start.7
  281.8 632.1 %all-reduce.10.cloned.1.call-start = ((), (), s32[]{:S(2)}) async-start(), calls=%async_computation.1 | async-start | bytes 786432 | tf_op jit(solution)/shard_map/psum | solution.py:103
  541.4 1.0 copy-start.4
  554.9 10.5 copy-start.5
  630.3 18.5 %collective-permute-start.8 = (bf16[4,64,128]{2,1,0:T(8,128)(2,1)S(1)}, bf16[4,64,128]{2,1,0:T(8,128)(2,1)S(1)}, u32[]{:S(2)}, u32[]{:S(2)}) collective-permute-start(bf16[4,64,128]{2,1,0:T(8,128)(2,1)S(1)} %bitcast.377), channel_id=1, source_target_pairs={{0,2},{1,3},{2,4},{3,5},{4,6},{5,7},{6,8},{7,9},{8,10},{9,11},{10,... | collective-permute-start | bytes 196616 | tf_op jit(solution)/shard_map/ppermute | solution.py:14
  633.5 15.3 %collective-permute-start.9 = (bf16[4,64,128]{2,1,0:T(8,128)(2,1)S(1)}, bf16[4,64,128]{2,1,0:T(8,128)(2,1)S(1)}, u32[]{:S(2)}, u32[]{:S(2)}) collective-permute-start(bf16[4,64,128]{2,1,0:T(8,128)(2,1)S(1)} %bitcast.378), channel_id=1, source_target_pairs={{0,1},{1,2},{2,3},{3,4},{4,5},{5,6},{6,7},{7,8},{8,9},{9,10},{10,1... | collective-permute-start | bytes 196616 | tf_op jit(solution)/shard_map/ppermute | solution.py:14
  640.1 8.7 collective-permute-start.10
  642.0 6.8 collective-permute-start.11
  913.9 1.1 copy-start.1
  915.0 0.9 copy-start.2
  1025.7 19.5 %all-to-all-start = ((f32[64,128,1]{0,2,1:T(1,128)}), f32[64,128,1]{0,2,1:T(1,128)S(1)}, u32[]{:S(2)}, u32[]{:S(2)}) async-start(f32[64,128,1]{0,2,1:T(1,128)} %bitcast.107), calls=%async_computation | async-start | bytes 131072 | tf_op jit(solution)/shard_map/all_to_all | solution.py:116
Sparse Core Ops, SparseCore 0:
  282.0 259.4 all-reduce.11
  651.0 262.8 all-reduce.9
where the time goes:
time: 1060 us; the launch traced here: 1050 us
  waiting for transfers between devices  533 us (50%)
  blocking collectives  229 us (22%)
  other arithmetic  183 us (17%)
  starting transfers between devices  58.7 us (6%)
  matrix products  19.6 us (2%)
  between operations  18.7 us (2%)
    psum x2, waiting for transfers between devices, local(): lax.psum((exact_dot(trial, trial.T), exact_dot(trial, applied_trial.T)),...  522 us
    psum x1, blocking collectives, local(): lax.psum(exact_dot(start_block, start_block.T), ('grp', 'node'))  106 us
    psum x1, blocking collectives, local(): theta = symmetric(lax.psum(exact_dot(block, applied.T), ('grp', 'node')))  96 us
    another operation x27, other arithmetic, lower_solve(): lax.linalg.triangular_solve(factor, rhs, left_side=True, lower=True, tran...  80.4 us
    another operation x24, other arithmetic, rayleigh(): chol_image = jnp.linalg.cholesky(exact_dot(image.T, image))  52.5 us
    ppermute x12, starting transfers between devices, shifted(): return lax.ppermute(value, axis, pairs)  50.4 us
    another operation x11, other arithmetic, rayleigh(): chol_basis = jnp.linalg.cholesky(gram_basis)  41.1 us
    all_gather x3, blocking collectives, operate(): grouped = lax.all_gather(rounded[None], 'grp', axis=0, tiled=True)  26.9 us
  transfers between devices with their start and end apart: 15, of which 4 were waited for; matrix products, arithmetic and copies ran while one was open for 0% of the time, Pallas kernels for 0%

commit v1 on v0

v1 whole, which is shorter than its diff:
```python
import jax
import jax.numpy as jnp
from jax import lax
from jax.experimental import pallas as pl
from jax.experimental.pallas import tpu as pltpu
from jax.sharding import PartitionSpec as P

REACH = 2
NSUB = 4
STEPS = 2
BOTH = ("grp", "node")
CORE_Y = (1, 2, 4, 8)
Z_X = (16, 32, 64, 128, 256)
CORE_X = (1, 128, 256)


def groups_over(bits):
    mask = sum(bits)
    groups = []
    for base in range(512):
        if base & mask:
            continue
        members = [base]
        for bit in bits:
            members = members + [member | bit for member in members]
        groups.append(members)
    return groups


def swap(values, bits):
    return lax.all_to_all(
        values, BOTH, split_axis=0, concat_axis=0, tiled=True, axis_index_groups=groups_over(bits)
    )


def copies(value, count):
    return jnp.broadcast_to(value[None], (count,) + value.shape)


def total(part):
    rows = part.shape[0]
    scattered = jnp.sum(swap(part.reshape(16, rows // 16, 128), CORE_Y), axis=0)
    summed = jnp.sum(swap(copies(scattered, 32), Z_X), axis=0)
    return swap(copies(summed, 16), CORE_Y).reshape(rows, 128)


def total_square(matrix):
    half = matrix.shape[0] // 2
    packed = total(jnp.concatenate([matrix[:half], matrix[half:]], axis=1))
    width = matrix.shape[1]
    return jnp.concatenate([packed[:, :width], packed[:, width:]], axis=0)


def symmetric(matrix):
    return 0.5 * (matrix + matrix.T)


def exact_dot(left, right):
    return jnp.dot(left, right, precision=lax.Precision.HIGHEST, preferred_element_type=jnp.float32)


def lower_solve(factor, rhs, transposed):
    return lax.linalg.triangular_solve(
        factor, rhs, left_side=True, lower=True, transpose_a=transposed
    )


def rayleigh(gram_basis, gram_operator, columns):
    order = gram_basis.shape[0]
    chol_basis = jnp.linalg.cholesky(gram_basis)
    half = lower_solve(chol_basis, symmetric(gram_operator), False)
    projected = symmetric(lower_solve(chol_basis, half.T, False))
    scale = jnp.sqrt(jnp.sum(projected * projected) + 1e-06)
    filtered = projected / scale + 1.25 * jnp.eye(order, dtype=jnp.float32)
    square = exact_dot(filtered, filtered)
    fourth = exact_dot(square, square)
    basis = jnp.eye(order, dtype=jnp.float32)[:, :columns]
    for sweep in range(NSUB):
        image = exact_dot(fourth, basis)
        chol_image = jnp.linalg.cholesky(exact_dot(image.T, image))
        basis = lower_solve(chol_image, image.T, False).T
    coeffs = lower_solve(chol_basis, basis, True)
    ritz_now = symmetric(exact_dot(basis.T, exact_dot(projected, basis)))
    return (coeffs, ritz_now)


def tiles_kernel(index_ref, weight_ref, own_ref, up_ref, down_ref, tiles_ref, out_ref, window_ref):
    window_ref[0:8] = down_ref[...]
    window_ref[8:16] = own_ref[...]
    window_ref[16:24] = up_ref[...]
    acc = jnp.zeros(out_ref.shape, jnp.float32)
    for slot in range(tiles_ref.shape[0]):
        product = lax.dot_general(
            window_ref[index_ref[slot]],
            tiles_ref[slot],
            (((1,), (1,)), ((), ())),
            preferred_element_type=jnp.float32,
        )
        acc = acc + weight_ref[slot] * product
    out_ref[...] = acc


def apply_tiles(index, weights, own, up, down, tiles):
    smem = pl.BlockSpec(memory_space=pltpu.SMEM)
    vmem = pl.BlockSpec(memory_space=pltpu.VMEM)
    return pl.pallas_call(
        tiles_kernel,
        out_shape=jax.ShapeDtypeStruct(own.shape[1:], jnp.float32),
        in_specs=[smem, smem, vmem, vmem, vmem, vmem],
        out_specs=vmem,
        scratch_shapes=[pltpu.VMEM((24,) + own.shape[1:], jnp.bfloat16)],
        compiler_params=pltpu.CompilerParams(vmem_limit_bytes=16 << 20),
        name="apply_tiles",
    )(index, weights, own, up, down, tiles)


def local(start_block, weight_tiles, tile_scales, neighbour_ids, live_counts, row_order):
    columns = start_block.shape[0]
    rows_dev = start_block.shape[1]
    groups = lax.axis_size("grp")
    nodes = lax.axis_size("node")
    here = lax.axis_index("node")
    ids = neighbour_ids[0]
    slots = ids.shape[0]
    group_index = ids // nodes
    node_index = ids % nodes
    chips = nodes // 2
    chip_offset = (node_index // 2 - here // 2 + 1 + chips) % chips
    index = jnp.clip(chip_offset * 8 + node_index % 2 + 2 * group_index, 0, 23).astype(jnp.int32)
    slot_iota = jnp.arange(slots, dtype=jnp.int32)
    weights = jnp.where(slot_iota < live_counts[0], tile_scales[0], jnp.float32(0.0))
    tiles = weight_tiles[0]
    to_next = [(source, (source + 2) % nodes) for source in range(nodes)]
    to_last = [(source, (source - 2) % nodes) for source in range(nodes)]

    def operate(values):
        rounded = values.astype(jnp.bfloat16)
        own = swap(copies(rounded, 8), CORE_X)
        down = lax.ppermute(own, "node", to_next)
        up = lax.ppermute(own, "node", to_last)
        return apply_tiles(index, weights, own, up, down, tiles)

    total_rows = rows_dev * groups * nodes
    start_gram = total_square(exact_dot(start_block, start_block.T))
    start_chol = jnp.linalg.cholesky(start_gram)
    block = lower_solve(start_chol, start_block, False)
    applied = operate(block)
    theta = symmetric(total_square(exact_dot(block, applied.T)))
    start_theta = jnp.sqrt(jnp.float32(total_rows)) * theta
    momentum = None
    applied_momentum = None
    ritz = theta
    for step in range(STEPS):
        residual = applied - exact_dot(theta, block)
        applied_residual = operate(residual)
        if momentum is None:
            trial = jnp.concatenate([block, residual], axis=0)
            applied_trial = jnp.concatenate([applied, applied_residual], axis=0)
        else:
            trial = jnp.concatenate([block, residual, momentum], axis=0)
            applied_trial = jnp.concatenate([applied, applied_residual, applied_momentum], axis=0)
        order = trial.shape[0]
        grams = jnp.concatenate([exact_dot(trial, trial.T), exact_dot(trial, applied_trial.T)], axis=0)
        grams = total(grams.reshape(-1, 128)).reshape(2 * order, order)
        coeffs, ritz = rayleigh(grams[:order], grams[order:], columns)
        lower_coeffs = coeffs[columns:]
        block = exact_dot(coeffs.T, trial)
        applied = exact_dot(coeffs.T, applied_trial)
        momentum = exact_dot(lower_coeffs.T, trial[columns:])
        applied_momentum = exact_dot(lower_coeffs.T, applied_trial[columns:])
        theta = ritz
    scaled = jnp.sqrt(jnp.float32(total_rows)) * block
    pick = (row_order[0][None, :] == jnp.arange(rows_dev, dtype=jnp.int32)[:, None]).astype(jnp.float32)
    permuted = exact_dot(scaled, pick)
    pieces = permuted.reshape(columns, nodes, rows_dev // nodes)
    arrived = lax.all_to_all(pieces, "node", split_axis=1, concat_axis=1, tiled=True)
    embedding = arrived.reshape(columns, rows_dev)
    return (embedding, ritz, start_theta)


def solution(mesh):
    return jax.shard_map(
        local,
        mesh=mesh,
        in_specs=(
            P(None, BOTH),
            P(BOTH, None, None, None),
            P(BOTH, None),
            P(BOTH, None),
            P(BOTH),
            P(BOTH, None),
        ),
        out_specs=(P(None, BOTH), P(), P()),
        check_vma=False,
    )
```

time: 1060 us -> 488 us (0.46)
  waiting for transfers between devices: 533 us -> 65.7 us
  blocking collectives: 229 us -> 154 us
  starting transfers between devices: 58.7 us -> 45.2 us
  between operations: 18.7 us -> 5.4 us
    psum x2 -> x0, waiting for transfers between devices: 522 us -> none  [local(): lax.psum((exact_dot(trial, trial.T), exact_dot(trial, applied_trial.T)),...]
    psum x2 -> x0, blocking collectives: 202 us -> none  [the longest x1 106 us: local(): lax.psum(exact_dot(start_block, start_block.T), ('grp', 'node'))]
    all_to_all x0 -> x10, blocking collectives: none -> 154 us  [swap(): lax.all_to_all(values, BOTH, split_axis=0, concat_axis=0, tiled=True, axi...]
    all_to_all x0 -> x5, waiting for transfers between devices: none -> 38.1 us  [swap(): lax.all_to_all(values, BOTH, split_axis=0, concat_axis=0, tiled=True, axi...]
    ppermute x12 -> x6, starting transfers between devices: 50.4 us -> 15.8 us  [the longest x3 9.34 us: operate(): down = lax.ppermute(own, 'node', to_next)]
    all_gather x3 -> x0, blocking collectives: 26.9 us -> none  [operate(): grouped = lax.all_gather(rounded[None], 'grp', axis=0, tiled=True)]
    all_to_all x0 -> x5, starting transfers between devices: none -> 22.7 us  [swap(): lax.all_to_all(values, BOTH, split_axis=0, concat_axis=0, tiled=True, axi...]
    ppermute x12 -> x6, waiting for transfers between devices: 0.36 us -> 16.9 us  [the longest x3 15.5 us: operate(): down = lax.ppermute(own, 'node', to_next)]
  transfers between devices with their start and end apart: 15 -> 12, of which waited for: 4 -> 12; matrix products, arithmetic and copies ran while one was open for 0% -> 1% of each run, Pallas kernels for 0% -> 0%
where the time goes in v1:
time: 488 us; the launch traced here: 481 us
  other arithmetic  184 us (38%)
  blocking collectives  154 us (32%)
  waiting for transfers between devices  65.7 us (13%)
  starting transfers between devices  45.2 us (9%)
  matrix products  15.9 us (3%)
  local copies, waits for them, and re-layouts  8.15 us (2%)
  between operations  5.4 us (1%)
    all_to_all x10, blocking collectives, swap(): lax.all_to_all(values, BOTH, split_axis=0, concat_axis=0, tiled=True, axi...  154 us
    another operation x27, other arithmetic, lower_solve(): lax.linalg.triangular_solve(factor, rhs, left_side=True, lower=True, tran...  80.4 us
    another operation x24, other arithmetic, rayleigh(): chol_image = jnp.linalg.cholesky(exact_dot(image.T, image))  52.3 us
    another operation x11, other arithmetic, rayleigh(): chol_basis = jnp.linalg.cholesky(gram_basis)  41.1 us
    all_to_all x5, waiting for transfers between devices, swap(): lax.all_to_all(values, BOTH, split_axis=0, concat_axis=0, tiled=True, axi...  38.1 us
    all_to_all x5, starting transfers between devices, swap(): lax.all_to_all(values, BOTH, split_axis=0, concat_axis=0, tiled=True, axi...  22.7 us
    ppermute x3, waiting for transfers between devices, operate(): down = lax.ppermute(own, 'node', to_next)  15.5 us
    all_to_all x1, waiting for transfers between devices, local(): lax.all_to_all(pieces, 'node', split_axis=1, concat_axis=1, tiled=True)  10.8 us
  transfers between devices with their start and end apart: 12, of which 12 were waited for; matrix products, arithmetic and copies ran while one was open for 1% of the time, Pallas kernels for 0%

profile of v1, /device:TPU:1, one launch (start us, length us, event | category | flops | bytes accessed | tf_op | source)
XLA Modules:
  0.0 481.4 jit_solution(11629693124371527373)
XLA Ops:
  1.7 16.7 %all_to_all.80 = f32[16,2,128]{2,1,0:T(2,128)S(1)} all-to-all(f32[16,2,128]{2,1,0:T(2,128)S(1)} %bitcast.317), channel_id=1, replica_groups={{0,1,2,3,4,5,6,7,8,9,10,11,12,13,14,15},{16,17,18,19,20,21,22,23,24,25,..., dimensions={0} | all-to-all | bytes 32768 | tf_op jit(solution)/shard_map/all_to_all | solution.py:31
  18.4 20.5 %all_to_all.81 = f32[32,2,128]{2,1,0:T(2,128)S(1)} all-to-all(f32[32,2,128]{2,1,0:T(2,128)S(1)} %broadcast_in_dim.29), channel_id=1, replica_groups={{0,16,32,48,64,80,96,112,128,144,160,176,192,208,224,240,256,272,288,30..., dimensions={0} | all-to-all | bytes 65536 | tf_op jit(solution)/shard_map/all_to_all | solution.py:31
  45.3 6.8 %all-to-all-done.2 = f32[16,2,128]{2,1,0:T(2,128)S(1)} async-done(((f32[16,2,128]{2,1,0:T(2,128)}), f32[16,2,128]{2,1,0:T(2,128)S(1)}, u32[]{:S(2)}, u32[]{:S(2)}) %all-to-all-start.2) | async-done | bytes 16416 | tf_op jit(solution)/shard_map/all_to_all | solution.py:31
  52.5 5.9 %cholesky.325 = f32[64,64]{1,0:T(8,128)S(1)} custom-call(f32[64,64]{1,0:T(8,128)S(1)} %fusion.100), custom_call_target="Cholesky" | custom-call | tf_op jit(solution)/shard_map/jit(cholesky)/cholesky | solution.py:145
  87.0 12.1 %all_to_all.82 = f32[16,2,128]{2,1,0:T(2,128)S(1)} all-to-all(f32[16,2,128]{2,1,0:T(2,128)S(1)} %bitcast.318), channel_id=1, replica_groups={{0,1,2,3,4,5,6,7,8,9,10,11,12,13,14,15},{16,17,18,19,20,21,22,23,24,25,..., dimensions={0} | all-to-all | bytes 32768 | tf_op jit(solution)/shard_map/all_to_all | solution.py:31
  99.1 13.4 %all_to_all.83 = f32[32,2,128]{2,1,0:T(2,128)S(1)} all-to-all(f32[32,2,128]{2,1,0:T(2,128)S(1)} %broadcast_in_dim.33), channel_id=1, replica_groups={{0,16,32,48,64,80,96,112,128,144,160,176,192,208,224,240,256,272,288,30..., dimensions={0} | all-to-all | bytes 65536 | tf_op jit(solution)/shard_map/all_to_all | solution.py:31
  112.5 11.6 %all_to_all.84 = f32[16,2,128]{2,1,0:T(2,128)S(1)} all-to-all(f32[16,2,128]{2,1,0:T(2,128)S(1)} %broadcast_in_dim.34), channel_id=1, replica_groups={{0,1,2,3,4,5,6,7,8,9,10,11,12,13,14,15},{16,17,18,19,20,21,22,23,24,25,..., dimensions={0} | all-to-all | bytes 32768 | tf_op jit(solution)/shard_map/all_to_all | solution.py:31
  124.7 8.1 %all_to_all.85.own_ref = bf16[8,64,128]{2,1,0:T(8,128)(2,1)S(1)} all-to-all(bf16[8,64,128]{2,1,0:T(8,128)(2,1)S(1)} %broadcast_in_dim.35), channel_id=1, replica_groups={{0,1,128,129,256,257,384,385},{2,3,130,131,258,259,386,387},{4,5,132,13..., dimensions={0} | all-to-all | bytes 262144 | tf_op jit(solution)/shard_map/all_to_all | solution.py:31
  145.1 13.9 %all_to_all.86 = f32[16,16,128]{2,1,0:T(8,128)S(1)} all-to-all(f32[16,16,128]{2,1,0:T(8,128)S(1)} %bitcast.313), channel_id=1, replica_groups={{0,1,2,3,4,5,6,7,8,9,10,11,12,13,14,15},{16,17,18,19,20,21,22,23,24,25,..., dimensions={0} | all-to-all | bytes 262144 | tf_op jit(solution)/shard_map/all_to_all | solution.py:31
  159.1 15.4 %all_to_all.87 = f32[32,16,128]{2,1,0:T(8,128)S(1)} all-to-all(f32[32,16,128]{2,1,0:T(8,128)S(1)} %broadcast_in_dim.36), channel_id=1, replica_groups={{0,16,32,48,64,80,96,112,128,144,160,176,192,208,224,240,256,272,288,30..., dimensions={0} | all-to-all | bytes 524288 | tf_op jit(solution)/shard_map/all_to_all | solution.py:31
  175.1 5.4 %all-to-all-start.10 = ((f32[16,16,128]{2,1,0:T(8,128)}), f32[16,16,128]{2,1,0:T(8,128)S(1)}, u32[]{:S(2)}, u32[]{:S(2)}) async-start(f32[16,16,128]{2,1,0:T(8,128)} %broadcast_in_dim.38), calls=%async_computation.10 | async-start | bytes 262144 | tf_op jit(solution)/shard_map/all_to_all | solution.py:31
  180.6 8.7 %all-to-all-done.10 = f32[16,16,128]{2,1,0:T(8,128)S(1)} async-done(((f32[16,16,128]{2,1,0:T(8,128)}), f32[16,16,128]{2,1,0:T(8,128)S(1)}, u32[]{:S(2)}, u32[]{:S(2)}) %all-to-all-start.10) | async-done | bytes 131104 | tf_op jit(solution)/shard_map/all_to_all | solution.py:31
  189.5 11.7 %cholesky.104 = f32[128,128]{1,0:T(8,128)S(1)} custom-call(f32[128,128]{1,0:T(8,128)S(1)} %fusion.45), custom_call_target="Cholesky" | custom-call | tf_op jit(solution)/shard_map/jit(cholesky)/cholesky | solution.py:70
  202.5 9.8 %custom-call.34 = f32[1,128,128]{1,2,0:T(8,128)S(1)} custom-call(f32[1,128,128]{2,1,0:T(8,128)S(1)} %fusion.22), custom_call_target="InvertDiagBlocksLowerTriangular" | custom-call | tf_op jit(solution)/shard_map/triangular_solve | solution.py:63
  215.4 5.8 %cholesky.336 = f32[64,64]{1,0:T(8,128)S(1)} custom-call(f32[64,64]{1,0:T(8,128)S(1)} %fusion.97), custom_call_target="Cholesky" | custom-call | tf_op jit(solution)/shard_map/jit(cholesky)/cholesky | solution.py:80
  228.3 5.8 %cholesky.347 = f32[64,64]{1,0:T(8,128)S(1)} custom-call(f32[64,64]{1,0:T(8,128)S(1)} %fusion.93), custom_call_target="Cholesky" | custom-call | tf_op jit(solution)/shard_map/jit(cholesky)/cholesky | solution.py:80
  241.1 5.9 %cholesky.358 = f32[64,64]{1,0:T(8,128)S(1)} custom-call(f32[64,64]{1,0:T(8,128)S(1)} %fusion.89), custom_call_target="Cholesky" | custom-call | tf_op jit(solution)/shard_map/jit(cholesky)/cholesky | solution.py:80
  254.1 5.8 %cholesky.369 = f32[64,64]{1,0:T(8,128)S(1)} custom-call(f32[64,64]{1,0:T(8,128)S(1)} %fusion.85), custom_call_target="Cholesky" | custom-call | tf_op jit(solution)/shard_map/jit(cholesky)/cholesky | solution.py:80
  283.5 5.3 %collective-permute-done.5.down_ref = bf16[8,64,128]{2,1,0:T(8,128)(2,1)S(1)} collective-permute-done((bf16[8,64,128]{2,1,0:T(8,128)(2,1)S(1)}, bf16[8,64,128]{2,1,0:T(8,128)(2,1)S(1)}, u32[]{:S(2)}, u32[]{:S(2)}) %collective-permute-start.5) | collective-permute-done | bytes 131104 | tf_op jit(solution)/shard_map/ppermute | solution.py:139
  290.6 17.8 %all_to_all.88 = f32[16,36,128]{2,1,0:T(8,128)S(1)} all-to-all(f32[16,36,128]{2,1,0:T(8,128)S(1)} %reshape_reshape.4), channel_id=1, replica_groups={{0,1,2,3,4,5,6,7,8,9,10,11,12,13,14,15},{16,17,18,19,20,21,22,23,24,25,..., dimensions={0} | all-to-all | bytes 589824 | tf_op jit(solution)/shard_map/all_to_all | solution.py:31
  308.4 25.0 %all_to_all.89 = f32[32,36,128]{2,1,0:T(8,128)S(1)} all-to-all(f32[32,36,128]{2,1,0:T(8,128)S(1)} %broadcast_in_dim.40), channel_id=1, replica_groups={{0,16,32,48,64,80,96,112,128,144,160,176,192,208,224,240,256,272,288,30..., dimensions={0} | all-to-all | bytes 1179648 | tf_op jit(solution)/shard_map/all_to_all | solution.py:31
  339.6 12.3 %all-to-all-done.14 = f32[16,36,128]{2,1,0:T(8,128)S(1)} async-done(((f32[16,36,128]{2,1,0:T(8,128)}), f32[16,36,128]{2,1,0:T(8,128)S(1)}, u32[]{:S(2)}, u32[]{:S(2)}) %all-to-all-start.14) | async-done | bytes 294944 | tf_op jit(solution)/shard_map/all_to_all | solution.py:31
  352.1 11.7 %cholesky.173 = f32[128,128]{1,0:T(8,128)S(1)} custom-call(f32[128,128]{1,0:T(8,128)S(1)} %cholesky.422), custom_call_target="Cholesky" | custom-call | tf_op jit(solution)/shard_map/jit(cholesky)/cholesky | solution.py:70
  363.9 9.8 %custom-call.35 = f32[1,128,128]{1,2,0:T(8,128)S(1)} custom-call(f32[1,128,128]{2,1,0:T(8,128)S(1)} %get-tuple-element.68), custom_call_target="InvertDiagBlocksLowerTriangular" | custom-call | tf_op jit(solution)/shard_map/jit(cholesky)/cholesky | solution.py:70
  374.1 5.8 %cholesky.189 = f32[64,64]{1,0:T(8,128)S(1)} custom-call(f32[64,64]{1,0:T(8,128)S(1)} %convolution_subtract_fusion.3), custom_call_target="Cholesky" | custom-call | tf_op jit(solution)/shard_map/jit(cholesky)/cholesky | solution.py:70
  382.7 19.9 %custom-call.36 = f32[2,128,128]{1,2,0:T(8,128)S(1)} custom-call(f32[2,128,128]{2,1,0:T(8,128)S(1)} %pad_maximum_fusion.3), custom_call_target="InvertDiagBlocksLowerTriangular" | custom-call | tf_op jit(solution)/shard_map/triangular_solve | solution.py:63
  407.7 5.8 %cholesky.380 = f32[64,64]{1,0:T(8,128)S(1)} custom-call(f32[64,64]{1,0:T(8,128)S(1)} %fusion.79), custom_call_target="Cholesky" | custom-call | tf_op jit(solution)/shard_map/jit(cholesky)/cholesky | solution.py:80
  420.7 5.8 %cholesky.391 = f32[64,64]{1,0:T(8,128)S(1)} custom-call(f32[64,64]{1,0:T(8,128)S(1)} %fusion.77), custom_call_target="Cholesky" | custom-call | tf_op jit(solution)/shard_map/jit(cholesky)/cholesky | solution.py:80
  433.7 5.8 %cholesky.402 = f32[64,64]{1,0:T(8,128)S(1)} custom-call(f32[64,64]{1,0:T(8,128)S(1)} %fusion.75), custom_call_target="Cholesky" | custom-call | tf_op jit(solution)/shard_map/jit(cholesky)/cholesky | solution.py:80
  446.7 5.8 %cholesky.413 = f32[64,64]{1,0:T(8,128)S(1)} custom-call(f32[64,64]{1,0:T(8,128)S(1)} %fusion.73), custom_call_target="Cholesky" | custom-call | tf_op jit(solution)/shard_map/jit(cholesky)/cholesky | solution.py:80
  462.1 6.7 %all-to-all-start.15 = ((f32[64,128,1]{0,2,1:T(1,128)}), f32[64,128,1]{0,2,1:T(1,128)S(1)}, u32[]{:S(2)}, u32[]{:S(2)}) async-start(f32[64,128,1]{0,2,1:T(1,128)} %bitcast.81), calls=%async_computation.15 | async-start | bytes 131072 | tf_op jit(solution)/shard_map/all_to_all | solution.py:176
  469.5 10.8 %all-to-all-done.15 = f32[64,128,1]{0,2,1:T(1,128)S(1)} async-done(((f32[64,128,1]{0,2,1:T(1,128)}), f32[64,128,1]{0,2,1:T(1,128)S(1)}, u32[]{:S(2)}, u32[]{:S(2)}) %all-to-all-start.15) | async-done | bytes 32800 | tf_op jit(solution)/shard_map/all_to_all | solution.py:176
  (222 shorter events, 144.2 us)
Async XLA Ops:
  0.6 0.8 copy-start
  39.6 12.5 %all-to-all-start.2 = ((f32[16,2,128]{2,1,0:T(2,128)}), f32[16,2,128]{2,1,0:T(2,128)S(1)}, u32[]{:S(2)}, u32[]{:S(2)}) async-start(f32[16,2,128]{2,1,0:T(2,128)} %broadcast_in_dim.30), calls=%async_computation.2 | async-start | bytes 32768 | tf_op jit(solution)/shard_map/all_to_all | solution.py:31
  52.4 33.4 %copy-start.1 = (bf16[1,12,128,128]{3,2,1,0:T(8,128)(2,1)S(1)}, bf16[1,12,128,128]{3,2,1,0:T(8,128)(2,1)}, u32[]{:S(2)}) copy-start(bf16[1,12,128,128]{3,2,1,0:T(8,128)(2,1)} %param.16) | copy-start | bytes 1179652
  65.5 3.8 copy-start.3
  65.5 9.1 %all-to-all-start.3 = ((bf16[8,64,128]{2,1,0:T(8,128)(2,1)}), bf16[8,64,128]{2,1,0:T(8,128)(2,1)S(1)}, u32[]{:S(2)}, u32[]{:S(2)}) async-start(bf16[8,64,128]{2,1,0:T(8,128)(2,1)} %broadcast_in_dim.32), calls=%async_computation.3 | async-start | bytes 262144 | tf_op jit(solution)/shard_map/all_to_all | solution.py:31
  69.4 10.5 %copy-start.4 = (f32[1,12]{1,0:T(1,128)S(1)}, f32[1,12]{1,0:T(1,128)}, u32[]{:S(2)}) copy-start(f32[1,12]{1,0:T(1,128)} %param.17) | copy-start | bytes 148
  74.6 6.0 %collective-permute-start = (bf16[8,64,128]{2,1,0:T(8,128)(2,1)S(1)}, bf16[8,64,128]{2,1,0:T(8,128)(2,1)S(1)}, u32[]{:S(2)}, u32[]{:S(2)}) collective-permute-start(bf16[8,64,128]{2,1,0:T(8,128)(2,1)S(1)} %all-to-all-done.3.own_ref), channel_id=1, source_target_pairs={{0,126},{1,127},{2,0},{3,1},{4,2},{5,3},{6,4},{7,5},{8,6},{9,7},{1... | collective-permute-start | bytes 393224 | tf_op jit(solution)/shard_map/ppermute | solution.py:140
  76.7 9.0 %collective-permute-start.1 = (bf16[8,64,128]{2,1,0:T(8,128)(2,1)S(1)}, bf16[8,64,128]{2,1,0:T(8,128)(2,1)S(1)}, u32[]{:S(2)}, u32[]{:S(2)}) collective-permute-start(bf16[8,64,128]{2,1,0:T(8,128)(2,1)S(1)} %all-to-all-done.3.own_ref), channel_id=1, source_target_pairs={{0,2},{1,3},{2,4},{3,5},{4,6},{5,7},{6,8},{7,9},{8,10},{9,11},{10,... | collective-permute-start | bytes 393224 | tf_op jit(solution)/shard_map/ppermute | solution.py:139
  132.8 6.0 %collective-permute-start.2 = (bf16[8,64,128]{2,1,0:T(8,128)(2,1)S(1)}, bf16[8,64,128]{2,1,0:T(8,128)(2,1)S(1)}, u32[]{:S(2)}, u32[]{:S(2)}) collective-permute-start(bf16[8,64,128]{2,1,0:T(8,128)(2,1)S(1)} %all_to_all.85.own_ref), channel_id=1, source_target_pairs={{0,126},{1,127},{2,0},{3,1},{4,2},{5,3},{6,4},{7,5},{8,6},{9,7},{1... | collective-permute-start | bytes 393224 | tf_op jit(solution)/shard_map/ppermute | solution.py:140
  134.9 9.0 %collective-permute-start.3 = (bf16[8,64,128]{2,1,0:T(8,128)(2,1)S(1)}, bf16[8,64,128]{2,1,0:T(8,128)(2,1)S(1)}, u32[]{:S(2)}, u32[]{:S(2)}) collective-permute-start(bf16[8,64,128]{2,1,0:T(8,128)(2,1)S(1)} %all_to_all.85.own_ref), channel_id=1, source_target_pairs={{0,2},{1,3},{2,4},{3,5},{4,6},{5,7},{6,8},{7,9},{8,10},{9,11},{10,... | collective-permute-start | bytes 393224 | tf_op jit(solution)/shard_map/ppermute | solution.py:139
  175.1 14.2 %all-to-all-start.10 = ((f32[16,16,128]{2,1,0:T(8,128)}), f32[16,16,128]{2,1,0:T(8,128)S(1)}, u32[]{:S(2)}, u32[]{:S(2)}) async-start(f32[16,16,128]{2,1,0:T(8,128)} %broadcast_in_dim.38), calls=%async_computation.10 | async-start | bytes 262144 | tf_op jit(solution)/shard_map/all_to_all | solution.py:31
  268.4 9.0 %all-to-all-start.11 = ((bf16[8,64,128]{2,1,0:T(8,128)(2,1)}), bf16[8,64,128]{2,1,0:T(8,128)(2,1)S(1)}, u32[]{:S(2)}, u32[]{:S(2)}) async-start(bf16[8,64,128]{2,1,0:T(8,128)(2,1)} %broadcast_in_dim.39), calls=%async_computation.11 | async-start | bytes 262144 | tf_op jit(solution)/shard_map/all_to_all | solution.py:31
  277.5 6.0 %collective-permute-start.4 = (bf16[8,64,128]{2,1,0:T(8,128)(2,1)S(1)}, bf16[8,64,128]{2,1,0:T(8,128)(2,1)S(1)}, u32[]{:S(2)}, u32[]{:S(2)}) collective-permute-start(bf16[8,64,128]{2,1,0:T(8,128)(2,1)S(1)} %all-to-all-done.11.own_ref), channel_id=1, source_target_pairs={{0,126},{1,127},{2,0},{3,1},{4,2},{5,3},{6,4},{7,5},{8,6},{9,7},{1... | collective-permute-start | bytes 393224 | tf_op jit(solution)/shard_map/ppermute | solution.py:140
  279.7 9.0 %collective-permute-start.5 = (bf16[8,64,128]{2,1,0:T(8,128)(2,1)S(1)}, bf16[8,64,128]{2,1,0:T(8,128)(2,1)S(1)}, u32[]{:S(2)}, u32[]{:S(2)}) collective-permute-start(bf16[8,64,128]{2,1,0:T(8,128)(2,1)S(1)} %all-to-all-done.11.own_ref), channel_id=1, source_target_pairs={{0,2},{1,3},{2,4},{3,5},{4,6},{5,7},{6,8},{7,9},{8,10},{9,11},{10,... | collective-permute-start | bytes 393224 | tf_op jit(solution)/shard_map/ppermute | solution.py:139
  334.1 17.7 %all-to-all-start.14 = ((f32[16,36,128]{2,1,0:T(8,128)}), f32[16,36,128]{2,1,0:T(8,128)S(1)}, u32[]{:S(2)}, u32[]{:S(2)}) async-start(f32[16,36,128]{2,1,0:T(8,128)} %broadcast_in_dim.41), calls=%async_computation.14 | async-start | bytes 655360 | tf_op jit(solution)/shard_map/all_to_all | solution.py:31
  460.6 0.7 copy-start.2
  462.1 18.2 %all-to-all-start.15 = ((f32[64,128,1]{0,2,1:T(1,128)}), f32[64,128,1]{0,2,1:T(1,128)S(1)}, u32[]{:S(2)}, u32[]{:S(2)}) async-start(f32[64,128,1]{0,2,1:T(1,128)} %bitcast.81), calls=%async_computation.15 | async-start | bytes 131072 | tf_op jit(solution)/shard_map/all_to_all | solution.py:176

commit v2 on v1

v2 whole, which is shorter than its diff:
```python
import jax
import jax.numpy as jnp
from jax import lax
from jax.experimental import pallas as pl
from jax.experimental.pallas import tpu as pltpu
from jax.sharding import PartitionSpec as P

REACH = 2
NSUB = 4
BLOCK = 4
RADIUS = 0.18
BOTH = ("grp", "node")
CORE_Y = (1, 2, 4, 8)
Z_X = (16, 32, 64, 128, 256)
CORE_X = (1, 128, 256)


def groups_over(bits):
    mask = sum(bits)
    groups = []
    for base in range(512):
        if base & mask:
            continue
        members = [base]
        for bit in bits:
            members = members + [member | bit for member in members]
        groups.append(members)
    return groups


def swap(values, bits):
    return lax.all_to_all(
        values, BOTH, split_axis=0, concat_axis=0, tiled=True, axis_index_groups=groups_over(bits)
    )


def run(kernel, name, results, *operands, scalars=0, scratch=()):
    smem = pl.BlockSpec(memory_space=pltpu.SMEM)
    vmem = pl.BlockSpec(memory_space=pltpu.VMEM)
    return pl.pallas_call(
        kernel,
        out_shape=[jax.ShapeDtypeStruct(shape, dtype) for shape, dtype in results],
        in_specs=[smem] * scalars + [vmem] * (len(operands) - scalars),
        out_specs=[vmem] * len(results),
        scratch_shapes=list(scratch),
        compiler_params=pltpu.CompilerParams(vmem_limit_bytes=32 << 20),
        name=name,
    )(*operands)


F32 = jnp.float32
BF16 = jnp.bfloat16


def sum_kernel(parts_ref, out_ref):
    parts = [parts_ref[i] for i in range(parts_ref.shape[0])]
    while len(parts) > 1:
        parts = [parts[i] + parts[i + 1] for i in range(0, len(parts), 2)]
    for i in range(out_ref.shape[0]):
        out_ref[i] = parts[0]


def sum_copies(parts, count):
    return run(sum_kernel, "sum_copies", [((count,) + parts.shape[1:], F32)], parts)[0]


def total(part):
    rows = part.shape[0]
    scattered = swap(part.reshape(16, rows // 16, 128), CORE_Y)
    shared = swap(sum_copies(scattered, 32), Z_X)
    return swap(sum_copies(shared, 16), CORE_Y).reshape(rows, 128)


def mm(left, right, contract):
    return lax.dot_general(
        left,
        right,
        ((contract[:1], contract[1:]), ((), ())),
        precision=lax.Precision.HIGHEST,
        preferred_element_type=jnp.float32,
    )


def nn(left, right):
    return mm(left, right, (1, 0))


def nt(left, right):
    return mm(left, right, (1, 1))


def tn(left, right):
    return mm(left, right, (0, 0))


def eye(order):
    row = lax.broadcasted_iota(jnp.int32, (order, order), 0)
    column = lax.broadcasted_iota(jnp.int32, (order, order), 1)
    return jnp.where(row == column, jnp.float32(1.0), jnp.float32(0.0))


def inverse_root(value):
    guess = lax.rsqrt(value)
    return guess * (1.5 - 0.5 * value * guess * guess)


def inverse_factor(matrix):
    order = matrix.shape[0]
    lanes = 2 * order
    both = jnp.concatenate([matrix, eye(order)], axis=1)
    bands = [both[8 * i : 8 * i + 8] for i in range(order // 8)]
    sublane = lax.broadcasted_iota(jnp.int32, (8, lanes), 0)
    done = [None] * len(bands)
    for first in range(0, order, BLOCK):
        band = first // 8
        base = first % 8
        last_of_band = base + BLOCK == 8
        live = range(band, len(bands))
        column = [
            [jnp.broadcast_to(bands[i][:, first + k : first + k + 1], (8, lanes)) for i in live]
            for k in range(BLOCK)
        ]
        row = [
            jnp.broadcast_to(bands[band][base + k : base + k + 1], (8, lanes)) for k in range(BLOCK)
        ]
        entry = [
            [
                jnp.broadcast_to(column[l][0][base + k : base + k + 1], (8, lanes))
                for l in range(k + 1)
            ]
            for k in range(BLOCK)
        ]
        inverse = []
        factor = [[None] * BLOCK for _ in range(BLOCK)]
        for l in range(BLOCK):
            inverse.append(1.0 / entry[l][l])
            for k in range(l + 1, BLOCK):
                factor[k][l] = entry[k][l] * inverse[l]
                for m in range(l + 1, k + 1):
                    entry[k][m] = entry[k][m] - factor[k][l] * entry[m][l]
        start = 1 if last_of_band else 0
        for k in range(BLOCK):
            for l in range(k):
                row[k] = row[k] - factor[k][l] * row[l]
                for i in range(start, len(live)):
                    column[k][i] = column[k][i] - factor[k][l] * column[l][i]
        for k in range(BLOCK):
            scaled = row[k] * inverse_root(entry[k][k])
            if done[band] is None:
                done[band] = scaled
            else:
                done[band] = jnp.where(sublane == base + k, scaled, done[band])
            left = row[k] * inverse[k]
            for i in range(start, len(live)):
                bands[band + i] = bands[band + i] - column[k][i] * left
    return jnp.concatenate(done, axis=0)[:, order:]


def half_sum(matrix):
    return 0.5 * (matrix + matrix.T)


def orthonormal(image):
    return nt(image, inverse_factor(tn(image, image)))


def project(linv, gram, basis_ref):
    order = linv.shape[0]
    columns = basis_ref.shape[1]
    projected = half_sum(nt(nn(linv, gram), linv))
    scale = jnp.sqrt(jnp.sum(projected * projected, keepdims=True) + 1e-06)
    unit = projected / scale
    identity = eye(order)
    filtered = unit + 1.25 * identity
    square = nn(filtered, filtered)
    fourth = nn(square, square)
    eighth = nn(fourth, fourth)
    unit2 = square - 2.5 * unit - 1.5625 * identity
    unit4 = nn(unit2, unit2)
    bound = jnp.sum(unit4 * unit4)
    basis_ref[...] = orthonormal(nn(eighth, eighth[:, :columns]))

    @pl.when(jnp.logical_not(bound < RADIUS**8))
    def _():
        basis_ref[...] = identity[:, :columns]

        def sweep(_, carry):
            basis_ref[...] = orthonormal(nn(fourth, basis_ref[...]))
            return carry

        lax.fori_loop(0, NSUB, sweep, 0)

    basis = basis_ref[...]
    coeffs = tn(linv, basis)
    theta = half_sum(tn(basis, nn(projected, basis)))
    return coeffs, theta


def store_packed(ref, matrix):
    half = matrix.shape[0] // 2
    ref[...] = jnp.concatenate([matrix[:half], matrix[half:]], axis=1)


def load_packed(ref):
    width = ref.shape[1] // 2
    return jnp.concatenate([ref[:, :width], ref[:, width:]], axis=0)


def store_copies(ref, value):
    rounded = value.astype(BF16)
    for i in range(ref.shape[0]):
        ref[i] = rounded


def gram_kernel(start_ref, gram_ref):
    start = start_ref[...]
    store_packed(gram_ref, nt(start, start))


def start_kernel(gram_ref, start_ref, block_ref, rounded_ref):
    block = nn(inverse_factor(load_packed(gram_ref)), start_ref[...])
    block_ref[...] = block
    store_copies(rounded_ref, block)


def multiply_tiles(index_ref, weight_ref, own_ref, up_ref, down_ref, tiles_ref, window_ref):
    window_ref[0:8] = down_ref[...]
    window_ref[8:16] = own_ref[...]
    window_ref[16:24] = up_ref[...]
    acc = jnp.zeros(own_ref.shape[1:], F32)
    for slot in range(tiles_ref.shape[0]):
        product = lax.dot_general(
            window_ref[index_ref[slot]],
            tiles_ref[slot],
            (((1,), (1,)), ((), ())),
            preferred_element_type=F32,
        )
        acc = acc + weight_ref[slot] * product
    return acc


def first_kernel(index_ref, weight_ref, own_ref, up_ref, down_ref, tiles_ref, block_ref, applied_ref, theta_ref, window_ref):
    block = block_ref[...]
    applied = multiply_tiles(index_ref, weight_ref, own_ref, up_ref, down_ref, tiles_ref, window_ref)
    applied_ref[...] = applied
    store_packed(theta_ref, 0.5 * (nt(block, applied) + nt(applied, block)))


def residual_kernel(root, theta_in_ref, block_ref, applied_ref, theta_ref, start_theta_ref, residual_ref, rounded_ref):
    theta = half_sum(load_packed(theta_in_ref))
    theta_ref[...] = theta
    start_theta_ref[...] = root * theta
    residual = applied_ref[...] - nn(theta, block_ref[...])
    residual_ref[...] = residual
    store_copies(rounded_ref, residual)


def trial_kernel(index_ref, weight_ref, own_ref, up_ref, down_ref, tiles_ref, trial_ref, applied_ref, image_ref, grams_ref, window_ref):
    columns = image_ref.shape[0]
    image = multiply_tiles(index_ref, weight_ref, own_ref, up_ref, down_ref, tiles_ref, window_ref)
    image_ref[...] = image
    trial = trial_ref[...]
    residual = trial[columns : 2 * columns]
    applied = applied_ref[...]
    bands = [applied[i : i + columns] for i in range(0, applied.shape[0], columns)]
    applied_trial = jnp.concatenate(bands[:1] + [image] + bands[1:], axis=0)
    cross = 0.5 * (nt(trial, image) + nt(applied_trial, residual))
    grams_ref[...] = jnp.concatenate([nt(trial, residual), cross], axis=1)


def assemble_first(grams, theta):
    columns = theta.shape[0]
    cross = grams[:columns, columns:]
    overlap = grams[:columns, :columns]
    own = half_sum(grams[columns:, columns:])
    basis = (overlap, grams[columns:, :columns])
    gram = jnp.concatenate(
        [jnp.concatenate([theta, cross], axis=1), jnp.concatenate([cross.T, own], axis=1)], axis=0
    )
    return basis, gram


def first_step_kernel(grams_ref, theta_ref, trial_ref, applied_ref, image_ref, coeffs_ref, theta_out_ref, trial_out_ref, applied_out_ref, rounded_ref, basis_ref):
    columns = theta_ref.shape[0]
    (overlap, own), gram = assemble_first(grams_ref[...], theta_ref[...])
    factor = inverse_factor(own - tn(overlap, overlap))
    linv = jnp.concatenate(
        [
            jnp.concatenate([eye(columns), jnp.zeros((columns, columns), F32)], axis=1),
            jnp.concatenate([-nt(factor, overlap), factor], axis=1),
        ],
        axis=0,
    )
    coeffs, theta = project(linv, gram, basis_ref)
    theta_out_ref[...] = theta
    lower = jnp.concatenate([jnp.zeros((columns, columns), F32), coeffs[columns:]], axis=0)
    both = jnp.concatenate([coeffs, lower], axis=1)
    coeffs_ref[...] = both
    applied_trial = jnp.concatenate([applied_ref[...], image_ref[...]], axis=0)
    fresh = tn(both, jnp.concatenate([trial_ref[...], applied_trial], axis=1))
    width = trial_ref.shape[1]
    block = fresh[:columns, :width]
    applied = fresh[:columns, width:]
    residual = applied - nn(theta, block)
    store_copies(rounded_ref, residual)
    trial_out_ref[...] = jnp.concatenate([block, residual, fresh[columns:, :width]], axis=0)
    applied_out_ref[...] = jnp.concatenate([applied, fresh[columns:, width:]], axis=0)


def carry_kernel(coeffs_ref, grams_ref, theta_ref, trial_ref, order_ref, carried_ref, pieces_ref):
    columns = theta_ref.shape[0]
    coeffs = coeffs_ref[...]
    (overlap, own), gram = assemble_first(grams_ref[...], theta_ref[...])
    basis = jnp.concatenate(
        [
            jnp.concatenate([eye(columns), overlap], axis=1),
            jnp.concatenate([overlap.T, own], axis=1),
        ],
        axis=0,
    )
    carried_ref[...] = jnp.concatenate(
        [tn(coeffs, nn(basis, coeffs)), tn(coeffs, nn(gram, coeffs))], axis=0
    )
    width = trial_ref.shape[1]
    place = lax.broadcasted_iota(jnp.int32, (width, width), 0)
    pick = jnp.where(place == order_ref[...], F32(1.0), F32(0.0))
    pieces_ref[...] = mm(pick, trial_ref[...], (0, 1))


def last_step_kernel(root, grams_ref, carried_ref, theta_ref, arrived_ref, theta_out_ref, embedding_ref, basis_ref):
    columns = theta_ref.shape[0]
    grams = grams_ref[...]
    carried = carried_ref[...]
    wide = 2 * columns
    overlap = jnp.concatenate([grams[:columns, :columns], carried[:columns, columns:wide]], axis=1)
    mixed = grams[wide:, :columns]
    spread = tn(overlap, overlap)
    first = grams[columns:wide, :columns] - spread[:columns, :columns]
    corner = mixed.T - spread[:columns, columns:]
    second = carried[columns:wide, columns:wide] - spread[columns:, columns:]
    factor = inverse_factor(first)
    middle = nn(factor, corner)
    other = inverse_factor(second - tn(middle, middle))
    zero = jnp.zeros((columns, columns), F32)
    lower = jnp.concatenate(
        [
            jnp.concatenate([factor, zero], axis=1),
            jnp.concatenate([-nn(other, tn(middle, factor)), other], axis=1),
        ],
        axis=0,
    )
    linv = jnp.concatenate(
        [
            jnp.concatenate([eye(columns), zero, zero], axis=1),
            jnp.concatenate([-nt(lower, overlap), lower], axis=1),
        ],
        axis=0,
    )
    cross = grams[:columns, columns:]
    own = half_sum(grams[columns:wide, columns:])
    momentum_cross = grams[wide:, columns:]
    block_momentum = carried[wide : wide + columns, columns:wide]
    momentum = half_sum(carried[wide + columns :, columns:wide])
    gram = jnp.concatenate(
        [
            jnp.concatenate([theta_ref[...], cross, block_momentum], axis=1),
            jnp.concatenate([cross.T, own, momentum_cross.T], axis=1),
            jnp.concatenate([block_momentum.T, momentum_cross, momentum], axis=1),
        ],
        axis=0,
    )
    coeffs, theta = project(linv, gram, basis_ref)
    theta_out_ref[...] = theta
    embedding_ref[...] = root * mm(coeffs, arrived_ref[...], (0, 1))


def local(start_block, weight_tiles, tile_scales, neighbour_ids, live_counts, row_order):
    columns = start_block.shape[0]
    rows_dev = start_block.shape[1]
    groups = lax.axis_size("grp")
    nodes = lax.axis_size("node")
    here = lax.axis_index("node")
    ids = neighbour_ids[0]
    slots = ids.shape[0]
    group_index = ids // nodes
    node_index = ids % nodes
    chips = nodes // 2
    chip_offset = (node_index // 2 - here // 2 + 1 + chips) % chips
    index = jnp.clip(chip_offset * 8 + node_index % 2 + 2 * group_index, 0, 23).astype(jnp.int32)
    slot_iota = jnp.arange(slots, dtype=jnp.int32)
    weights = jnp.where(slot_iota < live_counts[0], tile_scales[0], F32(0.0))
    tiles = weight_tiles[0]
    to_next = [(source, (source + 2) % nodes) for source in range(nodes)]
    to_last = [(source, (source - 2) % nodes) for source in range(nodes)]
    root = float(rows_dev * groups * nodes) ** 0.5
    slab = (columns, rows_dev)
    square = (columns, columns)
    packed = (columns // 2, 2 * columns)
    rounded_copies = ((2 * groups,) + slab, BF16)
    window = [pltpu.VMEM((6 * groups,) + slab, BF16)]

    def halo(rounded):
        own = swap(rounded, CORE_X)
        down = lax.ppermute(own, "node", to_next)
        up = lax.ppermute(own, "node", to_last)
        return index, weights, own, up, down, tiles

    gram = total(run(gram_kernel, "start_gram", [(packed, F32)], start_block)[0])
    block, rounded = run(
        start_kernel, "start_basis", [(slab, F32), rounded_copies], gram, start_block
    )
    applied, theta_part = run(
        first_kernel,
        "apply_start",
        [(slab, F32), (packed, F32)],
        *halo(rounded),
        block,
        scalars=2,
        scratch=window,
    )
    theta, start_theta, residual, rounded = run(
        lambda *refs: residual_kernel(root, *refs),
        "residual",
        [(square, F32), (square, F32), (slab, F32), rounded_copies],
        total(theta_part),
        block,
        applied,
    )
    trial = jnp.concatenate([block, residual], axis=0)
    image, grams = run(
        trial_kernel,
        "apply_first",
        [(slab, F32), ((2 * columns, 2 * columns), F32)],
        *halo(rounded),
        trial,
        applied,
        scalars=2,
        scratch=window,
    )
    grams = total(grams)
    coeffs, next_theta, next_trial, next_applied, rounded = run(
        first_step_kernel,
        "first_step",
        [
            ((2 * columns, 2 * columns), F32),
            (square, F32),
            ((3 * columns, rows_dev), F32),
            ((2 * columns, rows_dev), F32),
            rounded_copies,
        ],
        grams,
        theta,
        trial,
        applied,
        image,
        scratch=[pltpu.VMEM((2 * columns, columns), F32)],
    )
    carried, pieces = run(
        carry_kernel,
        "carry",
        [((4 * columns, 2 * columns), F32), ((rows_dev, 3 * columns), F32)],
        coeffs,
        grams,
        theta,
        next_trial,
        row_order,
    )
    arrived = lax.all_to_all(pieces, "node", split_axis=0, concat_axis=0, tiled=True)
    _, last_grams = run(
        trial_kernel,
        "apply_last",
        [(slab, F32), ((3 * columns, 2 * columns), F32)],
        *halo(rounded),
        next_trial,
        next_applied,
        scalars=2,
        scratch=window,
    )
    ritz, embedding = run(
        lambda *refs: last_step_kernel(root, *refs),
        "last_step",
        [(square, F32), (slab, F32)],
        total(last_grams),
        carried,
        next_theta,
        arrived,
        scratch=[pltpu.VMEM((3 * columns, columns), F32)],
    )
    return (embedding, ritz, start_theta)


def solution(mesh):
    return jax.shard_map(
        local,
        mesh=mesh,
        in_specs=(
            P(None, BOTH),
            P(BOTH, None, None, None),
            P(BOTH, None),
            P(BOTH, None),
            P(BOTH),
            P(BOTH, None),
        ),
        out_specs=(P(None, BOTH), P(), P()),
        check_vma=False,
    )
```

time: 488 us -> 288 us (0.59); the launches traced: 481 us -> 286 us
  other arithmetic: 184 us -> 0.04 us
  Pallas kernels: 2.74 us -> 35.5 us
  waiting for transfers between devices: 65.7 us -> 47.2 us
  matrix products: 15.9 us -> 0 us
  starting transfers between devices: 45.2 us -> 51.5 us
  blocking collectives: 154 us -> 148 us
  local copies, waits for them, and re-layouts: 8.15 us -> 3.04 us
    another operation x65 -> x0, other arithmetic: 180 us -> none  [the longest x27 80.4 us: lower_solve(): lax.linalg.triangular_solve(factor, rhs, left_side=True, lower=True, tran...]
    pallas_call x3 -> x17, Pallas kernels: 2.74 us -> 35.5 us  [run(): pl.pallas_call(kernel, out_shape=[jax.ShapeDtypeStruct(shape, dtype) for...]
    ppermute x6, waiting for transfers between devices: 16.9 us -> 5.55 us  [the longest x3 3.55 us: halo(): up = lax.ppermute(own, 'node', to_last)]
    ppermute x6, starting transfers between devices: 15.8 us -> 26 us  [the longest x3 19.5 us: halo(): up = lax.ppermute(own, 'node', to_last)]
    dot_general x38 -> x0, matrix products: 9.69 us -> none  [exact_dot(): jnp.dot(left, right, precision=lax.Precision.HIGHEST, preferred_element_t...]
    all_to_all x5 -> x4, waiting for transfers between devices: 38.1 us -> 29.6 us  [swap(): lax.all_to_all(values, BOTH, split_axis=0, concat_axis=0, tiled=True, axi...]
    all_to_all x10 -> x11, blocking collectives: 154 us -> 148 us  [swap(): lax.all_to_all(values, BOTH, split_axis=0, concat_axis=0, tiled=True, axi...]
    another operation x23 -> x0, matrix products: 6.19 us -> none  [the longest x21 5.82 us: lower_solve(): lax.linalg.triangular_solve(factor, rhs, left_side=True, lower=True, tran...]
  transfers between devices with their start and end apart: 12 -> 11, of which waited for: 12 -> 11; matrix products, arithmetic and copies ran while one was open for 1% -> 0% of each run, Pallas kernels for 0% -> 1%
where the time goes in v2:
time: 288 us; the launch traced here: 286 us
  blocking collectives  148 us (51%)
  starting transfers between devices  51.5 us (18%)
  waiting for transfers between devices  47.2 us (16%)
  Pallas kernels  35.5 us (12%)
  local copies, waits for them, and re-layouts  3.04 us (1%)
    all_to_all x11, blocking collectives, swap(): lax.all_to_all(values, BOTH, split_axis=0, concat_axis=0, tiled=True, axi...  148 us
    pallas_call x17, Pallas kernels, run(): pl.pallas_call(kernel, out_shape=[jax.ShapeDtypeStruct(shape, dtype) for...  35.5 us
    all_to_all x4, waiting for transfers between devices, swap(): lax.all_to_all(values, BOTH, split_axis=0, concat_axis=0, tiled=True, axi...  29.6 us
    ppermute x3, starting transfers between devices, halo(): up = lax.ppermute(own, 'node', to_last)  19.5 us
    all_to_all x4, starting transfers between devices, swap(): lax.all_to_all(values, BOTH, split_axis=0, concat_axis=0, tiled=True, axi...  18 us
    all_to_all x1, waiting for transfers between devices, local(): lax.all_to_all(pieces, 'node', split_axis=0, concat_axis=0, tiled=True)  12 us
    all_to_all x1, starting transfers between devices, local(): lax.all_to_all(pieces, 'node', split_axis=0, concat_axis=0, tiled=True)  7.59 us
    ppermute x3, starting transfers between devices, halo(): down = lax.ppermute(own, 'node', to_next)  6.49 us
  transfers between devices with their start and end apart: 11, of which 11 were waited for; matrix products, arithmetic and copies ran while one was open for 0% of the time, Pallas kernels for 1%

profile of v2, /device:TPU:1, one launch (start us, length us, event | category | flops | bytes accessed | tf_op | source)
XLA Modules:
  0.0 286.4 jit_solution(9239600918562217413)
XLA Ops:
  1.7 16.7 %all_to_all.86.parts_ref = f32[16,2,128]{2,1,0:T(2,128)S(1)} all-to-all(f32[16,2,128]{2,1,0:T(2,128)S(1)} %bitcast.40), channel_id=1, replica_groups={{0,1,2,3,4,5,6,7,8,9,10,11,12,13,14,15},{16,17,18,19,20,21,22,23,24,25,..., dimensions={0} | all-to-all | bytes 32768 | tf_op jit(solution)/shard_map/all_to_all | solution.py:32
  18.4 20.5 %all_to_all.87.parts_ref = f32[32,2,128]{2,1,0:T(2,128)S(1)} all-to-all(f32[32,2,128]{2,1,0:T(2,128)S(1)} %sum_copies.8), channel_id=1, replica_groups={{0,16,32,48,64,80,96,112,128,144,160,176,192,208,224,240,256,272,288,30..., dimensions={0} | all-to-all | bytes 65536 | tf_op jit(solution)/shard_map/all_to_all | solution.py:32
  39.5 5.1 %all-to-all-start.2 = ((f32[16,2,128]{2,1,0:T(2,128)}), f32[16,2,128]{2,1,0:T(2,128)S(1)}, u32[]{:S(2)}, u32[]{:S(2)}) async-start(f32[16,2,128]{2,1,0:T(2,128)} %sum_copies.9), calls=%async_computation.2 | async-start | bytes 32768 | tf_op jit(solution)/shard_map/all_to_all | solution.py:32
  45.2 6.8 %all-to-all-done.2 = f32[16,2,128]{2,1,0:T(2,128)S(1)} async-done(((f32[16,2,128]{2,1,0:T(2,128)}), f32[16,2,128]{2,1,0:T(2,128)S(1)}, u32[]{:S(2)}, u32[]{:S(2)}) %all-to-all-start.2) | async-done | bytes 16416 | tf_op jit(solution)/shard_map/all_to_all | solution.py:32
  52.8 3.7 %start_basis.1 = (f32[64,128]{1,0:T(8,128)S(1)}, bf16[8,64,128]{2,1,0:T(8,128)(2,1)}) custom-call(f32[32,128]{1,0:T(8,128)S(1)} %bitcast.38, f32[64,128]{1,0:T(8,128)S(1)} %copy-done.2), custom_call_target="tpu_custom_call" | custom-call | tf_op jit(solution)/shard_map/start_basis/pallas_call | solution.py:40
  56.4 3.8 %all-to-all-start.3 = ((bf16[8,64,128]{2,1,0:T(8,128)(2,1)}), bf16[8,64,128]{2,1,0:T(8,128)(2,1)S(1)}, u32[]{:S(2)}, u32[]{:S(2)}) async-start(bf16[8,64,128]{2,1,0:T(8,128)(2,1)} %get-tuple-element.23), calls=%async_computation.3 | async-start | bytes 262144 | tf_op jit(solution)/shard_map/all_to_all | solution.py:32
  60.3 5.2 %all-to-all-done.3.own_ref = bf16[8,64,128]{2,1,0:T(8,128)(2,1)S(1)} async-done(((bf16[8,64,128]{2,1,0:T(8,128)(2,1)}), bf16[8,64,128]{2,1,0:T(8,128)(2,1)S(1)}, u32[]{:S(2)}, u32[]{:S(2)}) %all-to-all-start.3) | async-done | bytes 131104 | tf_op jit(solution)/shard_map/all_to_all | solution.py:32
  65.5 2.1 collective-permute-start.1
  67.7 6.5 %collective-permute-start = (bf16[8,64,128]{2,1,0:T(8,128)(2,1)S(1)}, bf16[8,64,128]{2,1,0:T(8,128)(2,1)S(1)}, u32[]{:S(2)}, u32[]{:S(2)}) collective-permute-start(bf16[8,64,128]{2,1,0:T(8,128)(2,1)S(1)} %all-to-all-done.3.own_ref), channel_id=1, source_target_pairs={{0,126},{1,127},{2,0},{3,1},{4,2},{5,3},{6,4},{7,5},{8,6},{9,7},{1... | collective-permute-start | bytes 393224 | tf_op jit(solution)/shard_map/ppermute | solution.py:405
  76.1 1.3 apply_start.1
  77.4 13.0 %all_to_all.88.parts_ref = f32[16,2,128]{2,1,0:T(2,128)S(1)} all-to-all(f32[16,2,128]{2,1,0:T(2,128)S(1)} %bitcast.42), channel_id=1, replica_groups={{0,1,2,3,4,5,6,7,8,9,10,11,12,13,14,15},{16,17,18,19,20,21,22,23,24,25,..., dimensions={0} | all-to-all | bytes 32768 | tf_op jit(solution)/shard_map/all_to_all | solution.py:32
  90.5 14.2 %all_to_all.89.parts_ref = f32[32,2,128]{2,1,0:T(2,128)S(1)} all-to-all(f32[32,2,128]{2,1,0:T(2,128)S(1)} %sum_copies.10), channel_id=1, replica_groups={{0,16,32,48,64,80,96,112,128,144,160,176,192,208,224,240,256,272,288,30..., dimensions={0} | all-to-all | bytes 65536 | tf_op jit(solution)/shard_map/all_to_all | solution.py:32
  104.7 11.6 %all_to_all.90 = f32[16,2,128]{2,1,0:T(2,128)S(1)} all-to-all(f32[16,2,128]{2,1,0:T(2,128)S(1)} %sum_copies.11), channel_id=1, replica_groups={{0,1,2,3,4,5,6,7,8,9,10,11,12,13,14,15},{16,17,18,19,20,21,22,23,24,25,..., dimensions={0} | all-to-all | bytes 32768 | tf_op jit(solution)/shard_map/all_to_all | solution.py:32
  117.1 8.0 %all_to_all.91.own_ref = bf16[8,64,128]{2,1,0:T(8,128)(2,1)S(1)} all-to-all(bf16[8,64,128]{2,1,0:T(8,128)(2,1)S(1)} %get-tuple-element.27), channel_id=1, replica_groups={{0,1,128,129,256,257,384,385},{2,3,130,131,258,259,386,387},{4,5,132,13..., dimensions={0} | all-to-all | bytes 262144 | tf_op jit(solution)/shard_map/all_to_all | solution.py:32
  125.1 2.1 collective-permute-start.3
  127.3 6.5 %collective-permute-start.2 = (bf16[8,64,128]{2,1,0:T(8,128)(2,1)S(1)}, bf16[8,64,128]{2,1,0:T(8,128)(2,1)S(1)}, u32[]{:S(2)}, u32[]{:S(2)}) collective-permute-start(bf16[8,64,128]{2,1,0:T(8,128)(2,1)S(1)} %all_to_all.91.own_ref), channel_id=1, source_target_pairs={{0,126},{1,127},{2,0},{3,1},{4,2},{5,3},{6,4},{7,5},{8,6},{9,7},{1... | collective-permute-start | bytes 393224 | tf_op jit(solution)/shard_map/ppermute | solution.py:405
  137.0 13.5 %all_to_all.92.parts_ref = f32[16,8,128]{2,1,0:T(8,128)S(1)} all-to-all(f32[16,8,128]{2,1,0:T(8,128)S(1)} %bitcast.41), channel_id=1, replica_groups={{0,1,2,3,4,5,6,7,8,9,10,11,12,13,14,15},{16,17,18,19,20,21,22,23,24,25,..., dimensions={0} | all-to-all | bytes 131072 | tf_op jit(solution)/shard_map/all_to_all | solution.py:32
  150.5 14.6 %all_to_all.93.parts_ref = f32[32,8,128]{2,1,0:T(8,128)S(1)} all-to-all(f32[32,8,128]{2,1,0:T(8,128)S(1)} %sum_copies.12), channel_id=1, replica_groups={{0,16,32,48,64,80,96,112,128,144,160,176,192,208,224,240,256,272,288,30..., dimensions={0} | all-to-all | bytes 262144 | tf_op jit(solution)/shard_map/all_to_all | solution.py:32
  165.1 12.3 %all_to_all.94 = f32[16,8,128]{2,1,0:T(8,128)S(1)} all-to-all(f32[16,8,128]{2,1,0:T(8,128)S(1)} %sum_copies.13), channel_id=1, replica_groups={{0,1,2,3,4,5,6,7,8,9,10,11,12,13,14,15},{16,17,18,19,20,21,22,23,24,25,..., dimensions={0} | all-to-all | bytes 131072 | tf_op jit(solution)/shard_map/all_to_all | solution.py:32
  177.5 9.0 %first_step.1 = (f32[128,128]{1,0:T(8,128)S(1)}, f32[64,64]{1,0:T(8,128)S(1)}, f32[192,128]{1,0:T(8,128)S(1)}, f32[128,128]{1,0:T(8,128)S(1)}, bf16[8,64,128]{2,1,0:T(8,128)(2,1)S(1)}) custom-call(f32[128,128]{1,0:T(8,128)S(1)} %bitcast.34, f32[64,64]{1,0:T(8,128)S(1)} %get-tuple-element.30.theta_ref, ...), custom_call_target="tpu_custom_call" | custom-call | tf_op jit(solution)/shard_map/first_step/pallas_call | solution.py:40
  186.5 8.0 %all_to_all.95.own_ref = bf16[8,64,128]{2,1,0:T(8,128)(2,1)S(1)} all-to-all(bf16[8,64,128]{2,1,0:T(8,128)(2,1)S(1)} %get-tuple-element.32), channel_id=1, replica_groups={{0,1,128,129,256,257,384,385},{2,3,130,131,258,259,386,387},{4,5,132,13..., dimensions={0} | all-to-all | bytes 262144 | tf_op jit(solution)/shard_map/all_to_all | solution.py:32
  194.4 2.3 collective-permute-start.5
  196.7 6.5 %collective-permute-start.4 = (bf16[8,64,128]{2,1,0:T(8,128)(2,1)S(1)}, bf16[8,64,128]{2,1,0:T(8,128)(2,1)S(1)}, u32[]{:S(2)}, u32[]{:S(2)}) collective-permute-start(bf16[8,64,128]{2,1,0:T(8,128)(2,1)S(1)} %all_to_all.95.own_ref), channel_id=1, source_target_pairs={{0,126},{1,127},{2,0},{3,1},{4,2},{5,3},{6,4},{7,5},{8,6},{9,7},{1... | collective-permute-start | bytes 393224 | tf_op jit(solution)/shard_map/ppermute | solution.py:405
  205.0 1.6 apply_last.1
  206.5 15.2 %all_to_all.96.parts_ref = f32[16,12,128]{2,1,0:T(8,128)S(1)} all-to-all(f32[16,12,128]{2,1,0:T(8,128)S(1)} %reshape.38), channel_id=1, replica_groups={{0,1,2,3,4,5,6,7,8,9,10,11,12,13,14,15},{16,17,18,19,20,21,22,23,24,25,..., dimensions={0} | all-to-all | bytes 196608 | tf_op jit(solution)/shard_map/all_to_all | solution.py:32
  222.4 5.4 %all-to-all-start.13 = ((f32[32,12,128]{2,1,0:T(8,128)}), f32[32,12,128]{2,1,0:T(8,128)S(1)}, u32[]{:S(2)}, u32[]{:S(2)}) async-start(f32[32,12,128]{2,1,0:T(8,128)} %sum_copies.14), calls=%async_computation.13 | async-start | bytes 524288 | tf_op jit(solution)/shard_map/all_to_all | solution.py:32
  230.2 8.4 %all-to-all-done.13.parts_ref = f32[32,12,128]{2,1,0:T(8,128)S(1)} async-done(((f32[32,12,128]{2,1,0:T(8,128)}), f32[32,12,128]{2,1,0:T(8,128)S(1)}, u32[]{:S(2)}, u32[]{:S(2)}) %all-to-all-start.13) | async-done | bytes 196640 | tf_op jit(solution)/shard_map/all_to_all | solution.py:32
  238.6 7.6 %all-to-all-start.15 = ((f32[128,1,192]{2,1,0:T(1,128)}), f32[128,1,192]{2,1,0:T(1,128)S(1)}, u32[]{:S(2)}, u32[]{:S(2)}) async-start(f32[128,1,192]{2,1,0:T(1,128)} %copy.10), calls=%async_computation.15 | async-start | bytes 262144 | tf_op jit(solution)/shard_map/all_to_all | solution.py:468
  246.8 12.0 %all-to-all-done.15 = f32[128,1,192]{2,1,0:T(1,128)S(1)} async-done(((f32[128,1,192]{2,1,0:T(1,128)}), f32[128,1,192]{2,1,0:T(1,128)S(1)}, u32[]{:S(2)}, u32[]{:S(2)}) %all-to-all-start.15) | async-done | bytes 98336 | tf_op jit(solution)/shard_map/all_to_all | solution.py:468
  258.9 3.7 %all-to-all-start.14 = ((f32[16,12,128]{2,1,0:T(8,128)}), f32[16,12,128]{2,1,0:T(8,128)S(1)}, u32[]{:S(2)}, u32[]{:S(2)}) async-start(f32[16,12,128]{2,1,0:T(8,128)} %sum_copies.15), calls=%async_computation.14 | async-start | bytes 262144 | tf_op jit(solution)/shard_map/all_to_all | solution.py:32
  262.6 9.2 %all-to-all-done.14 = f32[16,12,128]{2,1,0:T(8,128)S(1)} async-done(((f32[16,12,128]{2,1,0:T(8,128)}), f32[16,12,128]{2,1,0:T(8,128)S(1)}, u32[]{:S(2)}, u32[]{:S(2)}) %all-to-all-start.14) | async-done | bytes 98336 | tf_op jit(solution)/shard_map/all_to_all | solution.py:32
  271.8 14.7 %last_step.1 = (f32[64,64]{1,0:T(8,128)}, f32[64,128]{1,0:T(8,128)}) custom-call(f32[192,128]{1,0:T(8,128)S(1)} %reshape.39.refs_0_, f32[256,128]{1,0:T(8,128)S(1)} %get-tuple-element.37.refs_1_, f32[64,64]{1,0:T(8,128)S(1)} %get-tuple-element.38.refs_2_, f32[128,192]{1,0:T(8,128)S(1)} %bitcast.36), custom_call_target="tpu_custom_call" | custom-call | tf_op jit(solution)/shard_map/last_step/pallas_call | solution.py:40
  (38 shorter events, 13.9 us)
Async XLA Ops:
  0.6 75.4 %copy-start = (bf16[1,12,128,128]{3,2,1,0:T(8,128)(2,1)S(1)}, bf16[1,12,128,128]{3,2,1,0:T(8,128)(2,1)}, u32[]{:S(2)}) copy-start(bf16[1,12,128,128]{3,2,1,0:T(8,128)(2,1)} %param.7) | copy-start | bytes 1179652
  0.6 0.8 copy-start.1
  39.5 12.5 %all-to-all-start.2 = ((f32[16,2,128]{2,1,0:T(2,128)}), f32[16,2,128]{2,1,0:T(2,128)S(1)}, u32[]{:S(2)}, u32[]{:S(2)}) async-start(f32[16,2,128]{2,1,0:T(2,128)} %sum_copies.9), calls=%async_computation.2 | async-start | bytes 32768 | tf_op jit(solution)/shard_map/all_to_all | solution.py:32
  52.0 0.8 copy-start.2
  56.4 3.8 %copy-start.4 = (s32[1,12]{1,0:T(1,128)S(1)}, s32[1,12]{1,0:T(1,128)}, u32[]{:S(2)}) copy-start(s32[1,12]{1,0:T(1,128)} %param.9) | copy-start | bytes 148
  56.4 9.1 %all-to-all-start.3 = ((bf16[8,64,128]{2,1,0:T(8,128)(2,1)}), bf16[8,64,128]{2,1,0:T(8,128)(2,1)S(1)}, u32[]{:S(2)}, u32[]{:S(2)}) async-start(bf16[8,64,128]{2,1,0:T(8,128)(2,1)} %get-tuple-element.23), calls=%async_computation.3 | async-start | bytes 262144 | tf_op jit(solution)/shard_map/all_to_all | solution.py:32
  60.3 13.9 %copy-start.5 = (f32[1,12]{1,0:T(1,128)S(1)}, f32[1,12]{1,0:T(1,128)}, u32[]{:S(2)}) copy-start(f32[1,12]{1,0:T(1,128)} %param.8) | copy-start | bytes 148
  65.5 9.3 %collective-permute-start.1 = (bf16[8,64,128]{2,1,0:T(8,128)(2,1)S(1)}, bf16[8,64,128]{2,1,0:T(8,128)(2,1)S(1)}, u32[]{:S(2)}, u32[]{:S(2)}) collective-permute-start(bf16[8,64,128]{2,1,0:T(8,128)(2,1)S(1)} %all-to-all-done.3.own_ref), channel_id=1, source_target_pairs={{0,2},{1,3},{2,4},{3,5},{4,6},{5,7},{6,8},{7,9},{8,10},{9,11},{10,... | collective-permute-start | bytes 393224 | tf_op jit(solution)/shard_map/ppermute | solution.py:404
  67.7 8.4 %collective-permute-start = (bf16[8,64,128]{2,1,0:T(8,128)(2,1)S(1)}, bf16[8,64,128]{2,1,0:T(8,128)(2,1)S(1)}, u32[]{:S(2)}, u32[]{:S(2)}) collective-permute-start(bf16[8,64,128]{2,1,0:T(8,128)(2,1)S(1)} %all-to-all-done.3.own_ref), channel_id=1, source_target_pairs={{0,126},{1,127},{2,0},{3,1},{4,2},{5,3},{6,4},{7,5},{8,6},{9,7},{1... | collective-permute-start | bytes 393224 | tf_op jit(solution)/shard_map/ppermute | solution.py:405
  125.1 9.3 %collective-permute-start.3 = (bf16[8,64,128]{2,1,0:T(8,128)(2,1)S(1)}, bf16[8,64,128]{2,1,0:T(8,128)(2,1)S(1)}, u32[]{:S(2)}, u32[]{:S(2)}) collective-permute-start(bf16[8,64,128]{2,1,0:T(8,128)(2,1)S(1)} %all_to_all.91.own_ref), channel_id=1, source_target_pairs={{0,2},{1,3},{2,4},{3,5},{4,6},{5,7},{6,8},{7,9},{8,10},{9,11},{10,... | collective-permute-start | bytes 393224 | tf_op jit(solution)/shard_map/ppermute | solution.py:404
  127.3 8.4 %collective-permute-start.2 = (bf16[8,64,128]{2,1,0:T(8,128)(2,1)S(1)}, bf16[8,64,128]{2,1,0:T(8,128)(2,1)S(1)}, u32[]{:S(2)}, u32[]{:S(2)}) collective-permute-start(bf16[8,64,128]{2,1,0:T(8,128)(2,1)S(1)} %all_to_all.91.own_ref), channel_id=1, source_target_pairs={{0,126},{1,127},{2,0},{3,1},{4,2},{5,3},{6,4},{7,5},{8,6},{9,7},{1... | collective-permute-start | bytes 393224 | tf_op jit(solution)/shard_map/ppermute | solution.py:405
  194.4 9.3 %collective-permute-start.5 = (bf16[8,64,128]{2,1,0:T(8,128)(2,1)S(1)}, bf16[8,64,128]{2,1,0:T(8,128)(2,1)S(1)}, u32[]{:S(2)}, u32[]{:S(2)}) collective-permute-start(bf16[8,64,128]{2,1,0:T(8,128)(2,1)S(1)} %all_to_all.95.own_ref), channel_id=1, source_target_pairs={{0,2},{1,3},{2,4},{3,5},{4,6},{5,7},{6,8},{7,9},{8,10},{9,11},{10,... | collective-permute-start | bytes 393224 | tf_op jit(solution)/shard_map/ppermute | solution.py:404
  196.7 8.3 %collective-permute-start.4 = (bf16[8,64,128]{2,1,0:T(8,128)(2,1)S(1)}, bf16[8,64,128]{2,1,0:T(8,128)(2,1)S(1)}, u32[]{:S(2)}, u32[]{:S(2)}) collective-permute-start(bf16[8,64,128]{2,1,0:T(8,128)(2,1)S(1)} %all_to_all.95.own_ref), channel_id=1, source_target_pairs={{0,126},{1,127},{2,0},{3,1},{4,2},{5,3},{6,4},{7,5},{8,6},{9,7},{1... | collective-permute-start | bytes 393224 | tf_op jit(solution)/shard_map/ppermute | solution.py:405
  222.4 16.1 %all-to-all-start.13 = ((f32[32,12,128]{2,1,0:T(8,128)}), f32[32,12,128]{2,1,0:T(8,128)S(1)}, u32[]{:S(2)}, u32[]{:S(2)}) async-start(f32[32,12,128]{2,1,0:T(8,128)} %sum_copies.14), calls=%async_computation.13 | async-start | bytes 524288 | tf_op jit(solution)/shard_map/all_to_all | solution.py:32
  227.9 0.7 copy-start.3
  238.6 20.3 %all-to-all-start.15 = ((f32[128,1,192]{2,1,0:T(1,128)}), f32[128,1,192]{2,1,0:T(1,128)S(1)}, u32[]{:S(2)}, u32[]{:S(2)}) async-start(f32[128,1,192]{2,1,0:T(1,128)} %copy.10), calls=%async_computation.15 | async-start | bytes 262144 | tf_op jit(solution)/shard_map/all_to_all | solution.py:468
  258.9 12.9 %all-to-all-start.14 = ((f32[16,12,128]{2,1,0:T(8,128)}), f32[16,12,128]{2,1,0:T(8,128)S(1)}, u32[]{:S(2)}, u32[]{:S(2)}) async-start(f32[16,12,128]{2,1,0:T(8,128)} %sum_copies.15), calls=%async_computation.14 | async-start | bytes 262144 | tf_op jit(solution)/shard_map/all_to_all | solution.py:32

commit v3 on v2

--- a/solution.py
+++ b/solution.py
@@ -13,6 +13,7 @@
 CORE_Y = (1, 2, 4, 8)
 Z_X = (16, 32, 64, 128, 256)
 CORE_X = (1, 128, 256)
+Y_Z = (2, 4, 8, 16, 32, 64)
 
 
 def groups_over(bits):
@@ -64,11 +65,12 @@
     return run(sum_kernel, "sum_copies", [((count,) + parts.shape[1:], F32)], parts)[0]
 
 
-def total(part):
+def total(part, inner, outer):
     rows = part.shape[0]
-    scattered = swap(part.reshape(16, rows // 16, 128), CORE_Y)
-    shared = swap(sum_copies(scattered, 32), Z_X)
-    return swap(sum_copies(shared, 16), CORE_Y).reshape(rows, 128)
+    count = 2 ** len(inner)
+    scattered = swap(part.reshape(count, rows // count, 128), inner)
+    shared = swap(sum_copies(scattered, 2 ** len(outer)), outer)
+    return swap(sum_copies(shared, count), inner).reshape(rows, 128)
 
 
 def mm(left, right, contract):
@@ -207,63 +209,76 @@
 
 
 def store_copies(ref, value):
-    rounded = value.astype(BF16)
     for i in range(ref.shape[0]):
-        ref[i] = rounded
-
-
-def gram_kernel(start_ref, gram_ref):
+        ref[i] = value
+
+
+def gram_kernel(start_ref, gram_ref, copies_ref):
     start = start_ref[...]
     store_packed(gram_ref, nt(start, start))
-
-
-def start_kernel(gram_ref, start_ref, block_ref, rounded_ref):
-    block = nn(inverse_factor(load_packed(gram_ref)), start_ref[...])
-    block_ref[...] = block
-    store_copies(rounded_ref, block)
-
-
-def multiply_tiles(index_ref, weight_ref, own_ref, up_ref, down_ref, tiles_ref, window_ref):
-    window_ref[0:8] = down_ref[...]
-    window_ref[8:16] = own_ref[...]
-    window_ref[16:24] = up_ref[...]
-    acc = jnp.zeros(own_ref.shape[1:], F32)
+    store_copies(copies_ref, start)
+
+
+def pick_kernel(index_ref, own_ref, up_ref, down_ref, slots_ref):
+    count = own_ref.shape[0]
+    for slot in range(slots_ref.shape[0]):
+        chosen = index_ref[slot]
+        for side, ref in enumerate((down_ref, own_ref, up_ref)):
+
+            @pl.when(chosen // count == side)
+            def _(ref=ref, slot=slot, chosen=chosen):
+                slots_ref[slot] = ref[chosen % count]
+
+
+def multiply_tiles(weight_ref, tiles_ref, slot_values):
+    acc = None
     for slot in range(tiles_ref.shape[0]):
         product = lax.dot_general(
-            window_ref[index_ref[slot]],
+            slot_values(slot).astype(BF16),
             tiles_ref[slot],
             (((1,), (1,)), ((), ())),
             preferred_element_type=F32,
         )
-        acc = acc + weight_ref[slot] * product
+        product = weight_ref[slot] * product
+        acc = product if acc is None else acc + product
     return acc
 
 
-def first_kernel(index_ref, weight_ref, own_ref, up_ref, down_ref, tiles_ref, block_ref, applied_ref, theta_ref, window_ref):
-    block = block_ref[...]
-    applied = multiply_tiles(index_ref, weight_ref, own_ref, up_ref, down_ref, tiles_ref, window_ref)
+def start_kernel(weight_ref, gram_ref, start_ref, slots_ref, tiles_ref, block_ref, block_slots_ref, applied_ref, copies_ref, theta_ref):
+    inverse = inverse_factor(load_packed(gram_ref))
+    block = nn(inverse, start_ref[...])
+    block_ref[...] = block
+
+    def values(slot):
+        there = nn(inverse, slots_ref[slot])
+        block_slots_ref[slot] = there
+        return there
+
+    applied = multiply_tiles(weight_ref, tiles_ref, values)
     applied_ref[...] = applied
+    store_copies(copies_ref, applied)
     store_packed(theta_ref, 0.5 * (nt(block, applied) + nt(applied, block)))
 
 
-def residual_kernel(root, theta_in_ref, block_ref, applied_ref, theta_ref, start_theta_ref, residual_ref, rounded_ref):
-    theta = half_sum(load_packed(theta_in_ref))
+def first_kernel(root, weight_ref, sum_ref, block_ref, applied_ref, block_slots_ref, applied_slots_ref, tiles_ref, theta_ref, start_theta_ref, residual_ref, residual_slots_ref, image_ref, copies_ref, grams_ref):
+    theta = half_sum(load_packed(sum_ref))
     theta_ref[...] = theta
     start_theta_ref[...] = root * theta
-    residual = applied_ref[...] - nn(theta, block_ref[...])
+    block = block_ref[...]
+    applied = applied_ref[...]
+    residual = applied - nn(theta, block)
     residual_ref[...] = residual
-    store_copies(rounded_ref, residual)
-
-
-def trial_kernel(index_ref, weight_ref, own_ref, up_ref, down_ref, tiles_ref, trial_ref, applied_ref, image_ref, grams_ref, window_ref):
-    columns = image_ref.shape[0]
-    image = multiply_tiles(index_ref, weight_ref, own_ref, up_ref, down_ref, tiles_ref, window_ref)
+
+    def values(slot):
+        there = applied_slots_ref[slot] - nn(theta, block_slots_ref[slot])
+        residual_slots_ref[slot] = there
+        return there
+
+    image = multiply_tiles(weight_ref, tiles_ref, values)
     image_ref[...] = image
-    trial = trial_ref[...]
-    residual = trial[columns : 2 * columns]
-    applied = applied_ref[...]
-    bands = [applied[i : i + columns] for i in range(0, applied.shape[0], columns)]
-    applied_trial = jnp.concatenate(bands[:1] + [image] + bands[1:], axis=0)
+    store_copies(copies_ref, image)
+    trial = jnp.concatenate([block, residual], axis=0)
+    applied_trial = jnp.concatenate([applied, image], axis=0)
     cross = 0.5 * (nt(trial, image) + nt(applied_trial, residual))
     grams_ref[...] = jnp.concatenate([nt(trial, residual), cross], axis=1)
 
@@ -280,8 +295,9 @@
     return basis, gram
 
 
-def first_step_kernel(grams_ref, theta_ref, trial_ref, applied_ref, image_ref, coeffs_ref, theta_out_ref, trial_out_ref, applied_out_ref, rounded_ref, basis_ref):
+def second_kernel(weight_ref, grams_ref, theta_ref, block_ref, residual_ref, applied_ref, image_ref, block_slots_ref, residual_slots_ref, applied_slots_ref, image_slots_ref, tiles_ref, coeffs_ref, theta_out_ref, trial_ref, grams_out_ref, basis_ref):
     columns = theta_ref.shape[0]
+    width = block_ref.shape[1]
     (overlap, own), gram = assemble_first(grams_ref[...], theta_ref[...])
     factor = inverse_factor(own - tn(overlap, overlap))
     linv = jnp.concatenate(
@@ -296,15 +312,24 @@
     lower = jnp.concatenate([jnp.zeros((columns, columns), F32), coeffs[columns:]], axis=0)
     both = jnp.concatenate([coeffs, lower], axis=1)
     coeffs_ref[...] = both
-    applied_trial = jnp.concatenate([applied_ref[...], image_ref[...]], axis=0)
-    fresh = tn(both, jnp.concatenate([trial_ref[...], applied_trial], axis=1))
-    width = trial_ref.shape[1]
-    block = fresh[:columns, :width]
-    applied = fresh[:columns, width:]
-    residual = applied - nn(theta, block)
-    store_copies(rounded_ref, residual)
-    trial_out_ref[...] = jnp.concatenate([block, residual, fresh[columns:, :width]], axis=0)
-    applied_out_ref[...] = jnp.concatenate([applied, fresh[columns:, width:]], axis=0)
+    mix = jnp.concatenate([coeffs, -nn(coeffs, theta)], axis=0).T
+
+    def values(slot):
+        parts = (applied_slots_ref, image_slots_ref, block_slots_ref, residual_slots_ref)
+        return nn(mix, jnp.concatenate([ref[slot] for ref in parts], axis=0))
+
+    image = multiply_tiles(weight_ref, tiles_ref, values)
+    block, applied = block_ref[...], applied_ref[...]
+    previous, previous_image = residual_ref[...], image_ref[...]
+    residual = nn(mix, jnp.concatenate([applied, previous_image, block, previous], axis=0))
+    old_trial = jnp.concatenate([block, previous], axis=0)
+    old_applied = jnp.concatenate([applied, previous_image], axis=0)
+    fresh = tn(both, jnp.concatenate([old_trial, old_applied], axis=1))
+    trial = jnp.concatenate([fresh[:columns, :width], residual, fresh[columns:, :width]], axis=0)
+    trial_ref[...] = trial
+    applied_trial = jnp.concatenate([fresh[:columns, width:], image, fresh[columns:, width:]], axis=0)
+    cross = 0.5 * (nt(trial, image) + nt(applied_trial, residual))
+    grams_out_ref[...] = jnp.concatenate([nt(trial, residual), cross], axis=1)
 
 
 def carry_kernel(coeffs_ref, grams_ref, theta_ref, trial_ref, order_ref, carried_ref, pieces_ref):
@@ -396,63 +421,74 @@
     slab = (columns, rows_dev)
     square = (columns, columns)
     packed = (columns // 2, 2 * columns)
-    rounded_copies = ((2 * groups,) + slab, BF16)
-    window = [pltpu.VMEM((6 * groups,) + slab, BF16)]
-
-    def halo(rounded):
-        own = swap(rounded, CORE_X)
+    slab_copies = ((2 * groups,) + slab, F32)
+    slab_slots = ((slots,) + slab, F32)
+
+    def slot_rows(copied):
+        own = swap(copied, CORE_X)
         down = lax.ppermute(own, "node", to_next)
         up = lax.ppermute(own, "node", to_last)
-        return index, weights, own, up, down, tiles
-
-    gram = total(run(gram_kernel, "start_gram", [(packed, F32)], start_block)[0])
-    block, rounded = run(
-        start_kernel, "start_basis", [(slab, F32), rounded_copies], gram, start_block
-    )
-    applied, theta_part = run(
-        first_kernel,
-        "apply_start",
-        [(slab, F32), (packed, F32)],
-        *halo(rounded),
-        block,
-        scalars=2,
-        scratch=window,
-    )
-    theta, start_theta, residual, rounded = run(
-        lambda *refs: residual_kernel(root, *refs),
-        "residual",
-        [(square, F32), (square, F32), (slab, F32), rounded_copies],
-        total(theta_part),
+        return run(pick_kernel, "pick_slots", [slab_slots], index, own, up, down, scalars=1)[0]
+
+    gram, copied = run(gram_kernel, "start_gram", [(packed, F32), slab_copies], start_block)
+    start_slots = slot_rows(copied)
+    block, block_slots, applied, copied, theta_part = run(
+        start_kernel,
+        "start_step",
+        [(slab, F32), slab_slots, (slab, F32), slab_copies, (packed, F32)],
+        weights,
+        total(gram, CORE_X, Y_Z),
+        start_block,
+        start_slots,
+        tiles,
+        scalars=1,
+    )
+    applied_slots = slot_rows(copied)
+    theta, start_theta, residual, residual_slots, image, copied, grams = run(
+        lambda *refs: first_kernel(root, *refs),
+        "first_residual",
+        [
+            (square, F32),
+            (square, F32),
+            (slab, F32),
+            slab_slots,
+            (slab, F32),
+            slab_copies,
+            ((2 * columns, 2 * columns), F32),
+        ],
+        weights,
+        total(theta_part, CORE_X, Y_Z),
         block,
         applied,
-    )
-    trial = jnp.concatenate([block, residual], axis=0)
-    image, grams = run(
-        trial_kernel,
-        "apply_first",
-        [(slab, F32), ((2 * columns, 2 * columns), F32)],
-        *halo(rounded),
-        trial,
-        applied,
-        scalars=2,
-        scratch=window,
-    )
-    grams = total(grams)
-    coeffs, next_theta, next_trial, next_applied, rounded = run(
-        first_step_kernel,
-        "first_step",
+        block_slots,
+        applied_slots,
+        tiles,
+        scalars=1,
+    )
+    image_slots = slot_rows(copied)
+    grams = total(grams, CORE_Y, Z_X)
+    coeffs, next_theta, trial, last_grams = run(
+        second_kernel,
+        "second_step",
         [
             ((2 * columns, 2 * columns), F32),
             (square, F32),
             ((3 * columns, rows_dev), F32),
-            ((2 * columns, rows_dev), F32),
-            rounded_copies,
-        ],
+            ((3 * columns, 2 * columns), F32),
+        ],
+        weights,
         grams,
         theta,
-        trial,
+        block,
+        residual,
         applied,
         image,
+        block_slots,
+        residual_slots,
+        applied_slots,
+        image_slots,
+        tiles,
+        scalars=1,
         scratch=[pltpu.VMEM((2 * columns, columns), F32)],
     )
     carried, pieces = run(
@@ -462,25 +498,15 @@
         coeffs,
         grams,
         theta,
-        next_trial,
+        trial,
         row_order,
     )
     arrived = lax.all_to_all(pieces, "node", split_axis=0, concat_axis=0, tiled=True)
-    _, last_grams = run(
-        trial_kernel,
-        "apply_last",
-        [(slab, F32), ((3 * columns, 2 * columns), F32)],
-        *halo(rounded),
-        next_trial,
-        next_applied,
-        scalars=2,
-        scratch=window,
-    )
     ritz, embedding = run(
         lambda *refs: last_step_kernel(root, *refs),
         "last_step",
         [(square, F32), (slab, F32)],
-        total(last_grams),
+        total(last_grams, CORE_Y, Z_X),
         carried,
         next_theta,
         arrived,

time: 288 us -> 262 us (0.910)
  blocking collectives: 148 us -> 44.3 us
  starting transfers between devices: 51.5 us -> 99.6 us
  waiting for transfers between devices: 47.2 us -> 67.2 us
  Pallas kernels: 35.5 us -> 45.2 us
    all_to_all x11 -> x4, blocking collectives: 148 us -> 44.3 us  [swap(): lax.all_to_all(values, BOTH, split_axis=0, concat_axis=0, tiled=True, axi...]
    all_to_all x4 -> x11, starting transfers between devices: 18 us -> 66.3 us  [swap(): lax.all_to_all(values, BOTH, split_axis=0, concat_axis=0, tiled=True, axi...]
    all_to_all x4 -> x11, waiting for transfers between devices: 29.6 us -> 55.1 us  [swap(): lax.all_to_all(values, BOTH, split_axis=0, concat_axis=0, tiled=True, axi...]
    pallas_call x17, Pallas kernels: 35.5 us -> 45.2 us  [run(): pl.pallas_call(kernel, out_shape=[jax.ShapeDtypeStruct(shape, dtype) for...]
    ppermute x6, waiting for transfers between devices: 5.55 us -> 0.02 us  [the longest x3 0.01 us: slot_rows(): up = lax.ppermute(own, 'node', to_last)]
  transfers between devices with their start and end apart: 11 -> 18, of which waited for: 11 -> 12; matrix products, arithmetic and copies ran while one was open for 0% -> 0% of each run, Pallas kernels for 1% -> 3%
where the time goes in v3:
time: 262 us; the launch traced here: 261 us
  starting transfers between devices  99.6 us (38%)
  waiting for transfers between devices  67.2 us (26%)
  Pallas kernels  45.2 us (17%)
  blocking collectives  44.3 us (17%)
  local copies, waits for them, and re-layouts  2.89 us (1%)
    all_to_all x11, starting transfers between devices, swap(): lax.all_to_all(values, BOTH, split_axis=0, concat_axis=0, tiled=True, axi...  66.3 us
    all_to_all x11, waiting for transfers between devices, swap(): lax.all_to_all(values, BOTH, split_axis=0, concat_axis=0, tiled=True, axi...  55.1 us
    pallas_call x17, Pallas kernels, run(): pl.pallas_call(kernel, out_shape=[jax.ShapeDtypeStruct(shape, dtype) for...  45.2 us
    all_to_all x4, blocking collectives, swap(): lax.all_to_all(values, BOTH, split_axis=0, concat_axis=0, tiled=True, axi...  44.3 us
    ppermute x3, starting transfers between devices, slot_rows(): up = lax.ppermute(own, 'node', to_last)  17.8 us
    all_to_all x1, waiting for transfers between devices, local(): lax.all_to_all(pieces, 'node', split_axis=0, concat_axis=0, tiled=True)  12 us
    ppermute x3, starting transfers between devices, slot_rows(): down = lax.ppermute(own, 'node', to_next)  8.05 us
    all_to_all x1, starting transfers between devices, local(): lax.all_to_all(pieces, 'node', split_axis=0, concat_axis=0, tiled=True)  7.5 us
  transfers between devices with their start and end apart: 18, of which 12 were waited for; matrix products, arithmetic and copies ran while one was open for 0% of the time, Pallas kernels for 3%

profile of v3, /device:TPU:1, one launch (start us, length us, event | category | flops | bytes accessed | tf_op | source)
XLA Modules:
  0.0 260.7 jit_solution(10704024901360147819)
XLA Ops:
  2.1 13.9 %all_to_all.86.parts_ref = f32[8,4,128]{2,1,0:T(4,128)S(1)} all-to-all(f32[8,4,128]{2,1,0:T(4,128)S(1)} %bitcast.42), channel_id=1, replica_groups={{0,1,128,129,256,257,384,385},{2,3,130,131,258,259,386,387},{4,5,132,13..., dimensions={0} | all-to-all | bytes 32768 | tf_op jit(solution)/shard_map/all_to_all | solution.py:33
  16.0 4.0 %all-to-all-start.3 = ((f32[8,64,128]{2,1,0:T(8,128)}), f32[8,64,128]{2,1,0:T(8,128)S(1)}, u32[]{:S(2)}, u32[]{:S(2)}) async-start(f32[8,64,128]{2,1,0:T(8,128)} %get-tuple-element.26), calls=%async_computation.3 | async-start | bytes 524288 | tf_op jit(solution)/shard_map/all_to_all | solution.py:33
  20.7 5.8 %all-to-all-done.3.own_ref = f32[8,64,128]{2,1,0:T(8,128)S(1)} async-done(((f32[8,64,128]{2,1,0:T(8,128)}), f32[8,64,128]{2,1,0:T(8,128)S(1)}, u32[]{:S(2)}, u32[]{:S(2)}) %all-to-all-start.3) | async-done | bytes 262176 | tf_op jit(solution)/shard_map/all_to_all | solution.py:33
  26.5 12.7 %all-to-all-start.1 = ((f32[64,4,128]{2,1,0:T(4,128)}), f32[64,4,128]{2,1,0:T(4,128)S(1)}, u32[]{:S(2)}, u32[]{:S(2)}) async-start(f32[64,4,128]{2,1,0:T(4,128)} %sum_copies.8), calls=%async_computation.1 | async-start | bytes 262144 | tf_op jit(solution)/shard_map/all_to_all | solution.py:33
  42.2 5.7 %collective-permute-start = (f32[8,64,128]{2,1,0:T(8,128)S(1)}, f32[8,64,128]{2,1,0:T(8,128)S(1)}, u32[]{:S(2)}, u32[]{:S(2)}) collective-permute-start(f32[8,64,128]{2,1,0:T(8,128)S(1)} %all-to-all-done.3.own_ref), channel_id=1, source_target_pairs={{0,126},{1,127},{2,0},{3,1},{4,2},{5,3},{6,4},{7,5},{8,6},{9,7},{1... | collective-permute-start | bytes 786440 | tf_op jit(solution)/shard_map/ppermute | solution.py:430
  51.7 6.2 %all-to-all-start.2 = ((f32[8,4,128]{2,1,0:T(4,128)}), f32[8,4,128]{2,1,0:T(4,128)S(1)}, u32[]{:S(2)}, u32[]{:S(2)}) async-start(f32[8,4,128]{2,1,0:T(4,128)} %sum_copies.9), calls=%async_computation.2 | async-start | bytes 32768 | tf_op jit(solution)/shard_map/all_to_all | solution.py:33
  62.5 5.7 %start_step.1 = (f32[64,128]{1,0:T(8,128)S(1)}, f32[12,64,128]{2,1,0:T(8,128)S(1)}, f32[64,128]{1,0:T(8,128)S(1)}, f32[8,64,128]{2,1,0:T(8,128)}, f32[32,128]{1,0:T(8,128)S(1)}) custom-call(f32[12]{0:T(128)S(1)} %compare_select_fusion.2.weight_ref.refs_0_, f32[32,128]{1,0:T(8,128)S(1)} %bitcast.39, f32[64,128]{1,0:T(8,128)S(1)} %copy-done.2, ...), custom_call_target="tpu_custom_call" | custom-call | tf_op jit(solution)/shard_map/start_step/pallas_call | solution.py:41
  68.2 7.7 %all_to_all.87.parts_ref = f32[8,4,128]{2,1,0:T(4,128)S(1)} all-to-all(f32[8,4,128]{2,1,0:T(4,128)S(1)} %bitcast.41), channel_id=1, replica_groups={{0,1,128,129,256,257,384,385},{2,3,130,131,258,259,386,387},{4,5,132,13..., dimensions={0} | all-to-all | bytes 32768 | tf_op jit(solution)/shard_map/all_to_all | solution.py:33
  75.9 4.0 %all-to-all-start.7 = ((f32[8,64,128]{2,1,0:T(8,128)}), f32[8,64,128]{2,1,0:T(8,128)S(1)}, u32[]{:S(2)}, u32[]{:S(2)}) async-start(f32[8,64,128]{2,1,0:T(8,128)} %get-tuple-element.31), calls=%async_computation.7 | async-start | bytes 524288 | tf_op jit(solution)/shard_map/all_to_all | solution.py:33
  80.6 5.8 %all-to-all-done.7.own_ref = f32[8,64,128]{2,1,0:T(8,128)S(1)} async-done(((f32[8,64,128]{2,1,0:T(8,128)}), f32[8,64,128]{2,1,0:T(8,128)S(1)}, u32[]{:S(2)}, u32[]{:S(2)}) %all-to-all-start.7) | async-done | bytes 262176 | tf_op jit(solution)/shard_map/all_to_all | solution.py:33
  86.4 6.8 %all-to-all-start.5 = ((f32[64,4,128]{2,1,0:T(4,128)}), f32[64,4,128]{2,1,0:T(4,128)S(1)}, u32[]{:S(2)}, u32[]{:S(2)}) async-start(f32[64,4,128]{2,1,0:T(4,128)} %sum_copies.10), calls=%async_computation.5 | async-start | bytes 262144 | tf_op jit(solution)/shard_map/all_to_all | solution.py:33
  96.1 5.7 %collective-permute-start.2 = (f32[8,64,128]{2,1,0:T(8,128)S(1)}, f32[8,64,128]{2,1,0:T(8,128)S(1)}, u32[]{:S(2)}, u32[]{:S(2)}) collective-permute-start(f32[8,64,128]{2,1,0:T(8,128)S(1)} %all-to-all-done.7.own_ref), channel_id=1, source_target_pairs={{0,126},{1,127},{2,0},{3,1},{4,2},{5,3},{6,4},{7,5},{8,6},{9,7},{1... | collective-permute-start | bytes 786440 | tf_op jit(solution)/shard_map/ppermute | solution.py:430
  101.8 3.2 %all-to-all-done.5.parts_ref = f32[64,4,128]{2,1,0:T(4,128)S(1)} async-done(((f32[64,4,128]{2,1,0:T(4,128)}), f32[64,4,128]{2,1,0:T(4,128)S(1)}, u32[]{:S(2)}, u32[]{:S(2)}) %all-to-all-start.5) | async-done | bytes 131104 | tf_op jit(solution)/shard_map/all_to_all | solution.py:33
  105.7 6.2 %all-to-all-start.6 = ((f32[8,4,128]{2,1,0:T(4,128)}), f32[8,4,128]{2,1,0:T(4,128)S(1)}, u32[]{:S(2)}, u32[]{:S(2)}) async-start(f32[8,4,128]{2,1,0:T(4,128)} %sum_copies.11), calls=%async_computation.6 | async-start | bytes 32768 | tf_op jit(solution)/shard_map/all_to_all | solution.py:33
  112.8 3.8 %all-to-all-done.6 = f32[8,4,128]{2,1,0:T(4,128)S(1)} async-done(((f32[8,4,128]{2,1,0:T(4,128)}), f32[8,4,128]{2,1,0:T(4,128)S(1)}, u32[]{:S(2)}, u32[]{:S(2)}) %all-to-all-start.6) | async-done | bytes 16416 | tf_op jit(solution)/shard_map/all_to_all | solution.py:33
  116.6 3.2 %first_residual.1 = (f32[64,64]{1,0:T(8,128)S(1)}, f32[64,64]{1,0:T(8,128)}, f32[64,128]{1,0:T(8,128)S(1)}, f32[12,64,128]{2,1,0:T(8,128)S(1)}, f32[64,128]{1,0:...) custom-call(f32[12]{0:T(128)S(1)} %compare_select_fusion.2.weight_ref.refs_0_, f32[32,128]{1,0:T(8,128)S(1)} %bitcast.38, ...), custom_call_target="tpu_custom_call" | custom-call | tf_op jit(solution)/shard_map/first_residual/pallas_call | solution.py:41
  119.8 10.9 %all_to_all.88.parts_ref = f32[16,8,128]{2,1,0:T(8,128)S(1)} all-to-all(f32[16,8,128]{2,1,0:T(8,128)S(1)} %bitcast.40), channel_id=1, replica_groups={{0,1,2,3,4,5,6,7,8,9,10,11,12,13,14,15},{16,17,18,19,20,21,22,23,24,25,..., dimensions={0} | all-to-all | bytes 131072 | tf_op jit(solution)/shard_map/all_to_all | solution.py:33
  130.7 3.5 %all-to-all-start.11 = ((f32[8,64,128]{2,1,0:T(8,128)}), f32[8,64,128]{2,1,0:T(8,128)S(1)}, u32[]{:S(2)}, u32[]{:S(2)}) async-start(f32[8,64,128]{2,1,0:T(8,128)} %get-tuple-element.37), calls=%async_computation.11 | async-start | bytes 524288 | tf_op jit(solution)/shard_map/all_to_all | solution.py:33
  134.8 5.9 %all-to-all-done.11.own_ref = f32[8,64,128]{2,1,0:T(8,128)S(1)} async-done(((f32[8,64,128]{2,1,0:T(8,128)}), f32[8,64,128]{2,1,0:T(8,128)S(1)}, u32[]{:S(2)}, u32[]{:S(2)}) %all-to-all-start.11) | async-done | bytes 262176 | tf_op jit(solution)/shard_map/all_to_all | solution.py:33
  140.7 5.2 %all-to-all-start.9 = ((f32[32,8,128]{2,1,0:T(8,128)}), f32[32,8,128]{2,1,0:T(8,128)S(1)}, u32[]{:S(2)}, u32[]{:S(2)}) async-start(f32[32,8,128]{2,1,0:T(8,128)} %sum_copies.12), calls=%async_computation.9 | async-start | bytes 262144 | tf_op jit(solution)/shard_map/all_to_all | solution.py:33
  148.1 6.4 %collective-permute-start.4 = (f32[8,64,128]{2,1,0:T(8,128)S(1)}, f32[8,64,128]{2,1,0:T(8,128)S(1)}, u32[]{:S(2)}, u32[]{:S(2)}) collective-permute-start(f32[8,64,128]{2,1,0:T(8,128)S(1)} %all-to-all-done.11.own_ref), channel_id=1, source_target_pairs={{0,126},{1,127},{2,0},{3,1},{4,2},{5,3},{6,4},{7,5},{8,6},{9,7},{1... | collective-permute-start | bytes 786440 | tf_op jit(solution)/shard_map/ppermute | solution.py:430
  155.7 5.9 %all-to-all-start.10 = ((f32[16,8,128]{2,1,0:T(8,128)}), f32[16,8,128]{2,1,0:T(8,128)S(1)}, u32[]{:S(2)}, u32[]{:S(2)}) async-start(f32[16,8,128]{2,1,0:T(8,128)} %sum_copies.13), calls=%async_computation.10 | async-start | bytes 131072 | tf_op jit(solution)/shard_map/all_to_all | solution.py:33
  162.7 6.8 %all-to-all-done.10 = f32[16,8,128]{2,1,0:T(8,128)S(1)} async-done(((f32[16,8,128]{2,1,0:T(8,128)}), f32[16,8,128]{2,1,0:T(8,128)S(1)}, u32[]{:S(2)}, u32[]{:S(2)}) %all-to-all-start.10) | async-done | bytes 65568 | tf_op jit(solution)/shard_map/all_to_all | solution.py:33
  169.5 12.2 %second_step.1 = (f32[128,128]{1,0:T(8,128)S(1)}, f32[64,64]{1,0:T(8,128)S(1)}, f32[192,128]{1,0:T(8,128)S(1)}, f32[192,128]{1,0:T(8,128)S(1)}) custom-call(f32[12]{0:T(128)S(1)} %compare_select_fusion.2.weight_ref.refs_0_, f32[128,128]{1,0:T(8,128)S(1)} %bitcast.34, f32[64,64]{1,0:T(8,128)S(1)} %get-tuple-element.33.theta_ref, ...), custom_call_target="tpu_custom_call" | custom-call | tf_op jit(solution)/shard_map/second_step/pallas_call | solution.py:41
  181.7 11.8 %all_to_all.89.parts_ref = f32[16,12,128]{2,1,0:T(8,128)S(1)} all-to-all(f32[16,12,128]{2,1,0:T(8,128)S(1)} %reshape.38), channel_id=1, replica_groups={{0,1,2,3,4,5,6,7,8,9,10,11,12,13,14,15},{16,17,18,19,20,21,22,23,24,25,..., dimensions={0} | all-to-all | bytes 196608 | tf_op jit(solution)/shard_map/all_to_all | solution.py:33
  194.2 8.2 %all-to-all-start.13 = ((f32[32,12,128]{2,1,0:T(8,128)}), f32[32,12,128]{2,1,0:T(8,128)S(1)}, u32[]{:S(2)}, u32[]{:S(2)}) async-start(f32[32,12,128]{2,1,0:T(8,128)} %sum_copies.14), calls=%async_computation.13 | async-start | bytes 524288 | tf_op jit(solution)/shard_map/all_to_all | solution.py:33
  204.8 8.4 %all-to-all-done.13.parts_ref = f32[32,12,128]{2,1,0:T(8,128)S(1)} async-done(((f32[32,12,128]{2,1,0:T(8,128)}), f32[32,12,128]{2,1,0:T(8,128)S(1)}, u32[]{:S(2)}, u32[]{:S(2)}) %all-to-all-start.13) | async-done | bytes 196640 | tf_op jit(solution)/shard_map/all_to_all | solution.py:33
  213.2 7.5 %all-to-all-start.15 = ((f32[128,1,192]{2,1,0:T(1,128)}), f32[128,1,192]{2,1,0:T(1,128)S(1)}, u32[]{:S(2)}, u32[]{:S(2)}) async-start(f32[128,1,192]{2,1,0:T(1,128)} %copy.10), calls=%async_computation.15 | async-start | bytes 262144 | tf_op jit(solution)/shard_map/all_to_all | solution.py:504
  221.3 12.0 %all-to-all-done.15 = f32[128,1,192]{2,1,0:T(1,128)S(1)} async-done(((f32[128,1,192]{2,1,0:T(1,128)}), f32[128,1,192]{2,1,0:T(1,128)S(1)}, u32[]{:S(2)}, u32[]{:S(2)}) %all-to-all-start.15) | async-done | bytes 98336 | tf_op jit(solution)/shard_map/all_to_all | solution.py:504
  233.3 3.7 %all-to-all-start.14 = ((f32[16,12,128]{2,1,0:T(8,128)}), f32[16,12,128]{2,1,0:T(8,128)S(1)}, u32[]{:S(2)}, u32[]{:S(2)}) async-start(f32[16,12,128]{2,1,0:T(8,128)} %sum_copies.15), calls=%async_computation.14 | async-start | bytes 262144 | tf_op jit(solution)/shard_map/all_to_all | solution.py:33
  237.0 9.2 %all-to-all-done.14 = f32[16,12,128]{2,1,0:T(8,128)S(1)} async-done(((f32[16,12,128]{2,1,0:T(8,128)}), f32[16,12,128]{2,1,0:T(8,128)S(1)}, u32[]{:S(2)}, u32[]{:S(2)}) %all-to-all-start.14) | async-done | bytes 98336 | tf_op jit(solution)/shard_map/all_to_all | solution.py:33
  246.3 14.5 %last_step.1 = (f32[64,64]{1,0:T(8,128)}, f32[64,128]{1,0:T(8,128)}) custom-call(f32[192,128]{1,0:T(8,128)S(1)} %reshape.39.refs_0_, f32[256,128]{1,0:T(8,128)S(1)} %get-tuple-element.41.refs_1_, f32[64,64]{1,0:T(8,128)S(1)} %get-tuple-element.42.refs_2_, f32[128,192]{1,0:T(8,128)S(1)} %bitcast.36), custom_call_target="tpu_custom_call" | custom-call | tf_op jit(solution)/shard_map/last_step/pallas_call | solution.py:41
  (43 shorter events, 26.8 us)
Async XLA Ops:
  0.6 0.8 copy-start.1
  16.0 10.5 %all-to-all-start.3 = ((f32[8,64,128]{2,1,0:T(8,128)}), f32[8,64,128]{2,1,0:T(8,128)S(1)}, u32[]{:S(2)}, u32[]{:S(2)}) async-start(f32[8,64,128]{2,1,0:T(8,128)} %get-tuple-element.26), calls=%async_computation.3 | async-start | bytes 524288 | tf_op jit(solution)/shard_map/all_to_all | solution.py:33
  26.5 24.5 %all-to-all-start.1 = ((f32[64,4,128]{2,1,0:T(4,128)}), f32[64,4,128]{2,1,0:T(4,128)S(1)}, u32[]{:S(2)}, u32[]{:S(2)}) async-start(f32[64,4,128]{2,1,0:T(4,128)} %sum_copies.8), calls=%async_computation.1 | async-start | bytes 262144 | tf_op jit(solution)/shard_map/all_to_all | solution.py:33
  39.2 8.6 %copy-start.4 = (s32[1,12]{1,0:T(1,128)S(1)}, s32[1,12]{1,0:T(1,128)}, u32[]{:S(2)}) copy-start(s32[1,12]{1,0:T(1,128)} %param.9) | copy-start | bytes 148
  39.2 19.3 %collective-permute-start.1 = (f32[8,64,128]{2,1,0:T(8,128)S(1)}, f32[8,64,128]{2,1,0:T(8,128)S(1)}, u32[]{:S(2)}, u32[]{:S(2)}) collective-permute-start(f32[8,64,128]{2,1,0:T(8,128)S(1)} %all-to-all-done.3.own_ref), channel_id=1, source_target_pairs={{0,2},{1,3},{2,4},{3,5},{4,6},{5,7},{6,8},{7,9},{8,10},{9,11},{10,... | collective-permute-start | bytes 786440 | tf_op jit(solution)/shard_map/ppermute | solution.py:429
  42.2 16.4 %collective-permute-start = (f32[8,64,128]{2,1,0:T(8,128)S(1)}, f32[8,64,128]{2,1,0:T(8,128)S(1)}, u32[]{:S(2)}, u32[]{:S(2)}) collective-permute-start(f32[8,64,128]{2,1,0:T(8,128)S(1)} %all-to-all-done.3.own_ref), channel_id=1, source_target_pairs={{0,126},{1,127},{2,0},{3,1},{4,2},{5,3},{6,4},{7,5},{8,6},{9,7},{1... | collective-permute-start | bytes 786440 | tf_op jit(solution)/shard_map/ppermute | solution.py:430
  51.7 10.8 %all-to-all-start.2 = ((f32[8,4,128]{2,1,0:T(4,128)}), f32[8,4,128]{2,1,0:T(4,128)S(1)}, u32[]{:S(2)}, u32[]{:S(2)}) async-start(f32[8,4,128]{2,1,0:T(4,128)} %sum_copies.9), calls=%async_computation.2 | async-start | bytes 32768 | tf_op jit(solution)/shard_map/all_to_all | solution.py:33
  57.9 0.7 copy-start.5
  58.5 4.0 %copy-start = (bf16[1,12,128,128]{3,2,1,0:T(8,128)(2,1)S(1)}, bf16[1,12,128,128]{3,2,1,0:T(8,128)(2,1)}, u32[]{:S(2)}) copy-start(bf16[1,12,128,128]{3,2,1,0:T(8,128)(2,1)} %param.7) | copy-start | bytes 1179652
  58.5 4.0 %copy-start.2 = (f32[64,128]{1,0:T(8,128)S(1)}, f32[64,128]{1,0:T(8,128)}, u32[]{:S(2)}) copy-start(f32[64,128]{1,0:T(8,128)} %start_ref.3) | copy-start | bytes 98308
  75.9 10.5 %all-to-all-start.7 = ((f32[8,64,128]{2,1,0:T(8,128)}), f32[8,64,128]{2,1,0:T(8,128)S(1)}, u32[]{:S(2)}, u32[]{:S(2)}) async-start(f32[8,64,128]{2,1,0:T(8,128)} %get-tuple-element.31), calls=%async_computation.7 | async-start | bytes 524288 | tf_op jit(solution)/shard_map/all_to_all | solution.py:33
  86.4 18.6 %all-to-all-start.5 = ((f32[64,4,128]{2,1,0:T(4,128)}), f32[64,4,128]{2,1,0:T(4,128)S(1)}, u32[]{:S(2)}, u32[]{:S(2)}) async-start(f32[64,4,128]{2,1,0:T(4,128)} %sum_copies.10), calls=%async_computation.5 | async-start | bytes 262144 | tf_op jit(solution)/shard_map/all_to_all | solution.py:33
  93.2 18.7 %collective-permute-start.3 = (f32[8,64,128]{2,1,0:T(8,128)S(1)}, f32[8,64,128]{2,1,0:T(8,128)S(1)}, u32[]{:S(2)}, u32[]{:S(2)}) collective-permute-start(f32[8,64,128]{2,1,0:T(8,128)S(1)} %all-to-all-done.7.own_ref), channel_id=1, source_target_pairs={{0,2},{1,3},{2,4},{3,5},{4,6},{5,7},{6,8},{7,9},{8,10},{9,11},{10,... | collective-permute-start | bytes 786440 | tf_op jit(solution)/shard_map/ppermute | solution.py:429
  96.1 15.8 %collective-permute-start.2 = (f32[8,64,128]{2,1,0:T(8,128)S(1)}, f32[8,64,128]{2,1,0:T(8,128)S(1)}, u32[]{:S(2)}, u32[]{:S(2)}) collective-permute-start(f32[8,64,128]{2,1,0:T(8,128)S(1)} %all-to-all-done.7.own_ref), channel_id=1, source_target_pairs={{0,126},{1,127},{2,0},{3,1},{4,2},{5,3},{6,4},{7,5},{8,6},{9,7},{1... | collective-permute-start | bytes 786440 | tf_op jit(solution)/shard_map/ppermute | solution.py:430
  105.7 10.9 %all-to-all-start.6 = ((f32[8,4,128]{2,1,0:T(4,128)}), f32[8,4,128]{2,1,0:T(4,128)S(1)}, u32[]{:S(2)}, u32[]{:S(2)}) async-start(f32[8,4,128]{2,1,0:T(4,128)} %sum_copies.11), calls=%async_computation.6 | async-start | bytes 32768 | tf_op jit(solution)/shard_map/all_to_all | solution.py:33
  130.7 10.0 %all-to-all-start.11 = ((f32[8,64,128]{2,1,0:T(8,128)}), f32[8,64,128]{2,1,0:T(8,128)S(1)}, u32[]{:S(2)}, u32[]{:S(2)}) async-start(f32[8,64,128]{2,1,0:T(8,128)} %get-tuple-element.37), calls=%async_computation.11 | async-start | bytes 524288 | tf_op jit(solution)/shard_map/all_to_all | solution.py:33
  140.7 14.4 %all-to-all-start.9 = ((f32[32,8,128]{2,1,0:T(8,128)}), f32[32,8,128]{2,1,0:T(8,128)S(1)}, u32[]{:S(2)}, u32[]{:S(2)}) async-start(f32[32,8,128]{2,1,0:T(8,128)} %sum_copies.12), calls=%async_computation.9 | async-start | bytes 262144 | tf_op jit(solution)/shard_map/all_to_all | solution.py:33
  145.9 15.7 %collective-permute-start.5 = (f32[8,64,128]{2,1,0:T(8,128)S(1)}, f32[8,64,128]{2,1,0:T(8,128)S(1)}, u32[]{:S(2)}, u32[]{:S(2)}) collective-permute-start(f32[8,64,128]{2,1,0:T(8,128)S(1)} %all-to-all-done.11.own_ref), channel_id=1, source_target_pairs={{0,2},{1,3},{2,4},{3,5},{4,6},{5,7},{6,8},{7,9},{8,10},{9,11},{10,... | collective-permute-start | bytes 786440 | tf_op jit(solution)/shard_map/ppermute | solution.py:429
  148.1 13.5 %collective-permute-start.4 = (f32[8,64,128]{2,1,0:T(8,128)S(1)}, f32[8,64,128]{2,1,0:T(8,128)S(1)}, u32[]{:S(2)}, u32[]{:S(2)}) collective-permute-start(f32[8,64,128]{2,1,0:T(8,128)S(1)} %all-to-all-done.11.own_ref), channel_id=1, source_target_pairs={{0,126},{1,127},{2,0},{3,1},{4,2},{5,3},{6,4},{7,5},{8,6},{9,7},{1... | collective-permute-start | bytes 786440 | tf_op jit(solution)/shard_map/ppermute | solution.py:430
  155.7 13.8 %all-to-all-start.10 = ((f32[16,8,128]{2,1,0:T(8,128)}), f32[16,8,128]{2,1,0:T(8,128)S(1)}, u32[]{:S(2)}, u32[]{:S(2)}) async-start(f32[16,8,128]{2,1,0:T(8,128)} %sum_copies.13), calls=%async_computation.10 | async-start | bytes 131072 | tf_op jit(solution)/shard_map/all_to_all | solution.py:33
  194.2 18.9 %all-to-all-start.13 = ((f32[32,12,128]{2,1,0:T(8,128)}), f32[32,12,128]{2,1,0:T(8,128)S(1)}, u32[]{:S(2)}, u32[]{:S(2)}) async-start(f32[32,12,128]{2,1,0:T(8,128)} %sum_copies.14), calls=%async_computation.13 | async-start | bytes 524288 | tf_op jit(solution)/shard_map/all_to_all | solution.py:33
  202.4 0.7 copy-start.3
  213.2 20.2 %all-to-all-start.15 = ((f32[128,1,192]{2,1,0:T(1,128)}), f32[128,1,192]{2,1,0:T(1,128)S(1)}, u32[]{:S(2)}, u32[]{:S(2)}) async-start(f32[128,1,192]{2,1,0:T(1,128)} %copy.10), calls=%async_computation.15 | async-start | bytes 262144 | tf_op jit(solution)/shard_map/all_to_all | solution.py:504
  233.3 12.9 %all-to-all-start.14 = ((f32[16,12,128]{2,1,0:T(8,128)}), f32[16,12,128]{2,1,0:T(8,128)S(1)}, u32[]{:S(2)}, u32[]{:S(2)}) async-start(f32[16,12,128]{2,1,0:T(8,128)} %sum_copies.15), calls=%async_computation.14 | async-start | bytes 262144 | tf_op jit(solution)/shard_map/all_to_all | solution.py:33

commit v4 on v3

--- a/solution.py
+++ b/solution.py
@@ -10,8 +10,6 @@
 BLOCK = 4
 RADIUS = 0.18
 BOTH = ("grp", "node")
-CORE_Y = (1, 2, 4, 8)
-Z_X = (16, 32, 64, 128, 256)
 CORE_X = (1, 128, 256)
 Y_Z = (2, 4, 8, 16, 32, 64)
 
@@ -53,24 +51,37 @@
 BF16 = jnp.bfloat16
 
 
-def sum_kernel(parts_ref, out_ref):
-    parts = [parts_ref[i] for i in range(parts_ref.shape[0])]
+def tree_sum(parts):
     while len(parts) > 1:
         parts = [parts[i] + parts[i + 1] for i in range(0, len(parts), 2)]
+    return parts[0]
+
+
+def sum_kernel(first, parts_ref, out_ref):
+    summed = tree_sum([parts_ref[i, first:] for i in range(parts_ref.shape[0])])
     for i in range(out_ref.shape[0]):
-        out_ref[i] = parts[0]
-
-
-def sum_copies(parts, count):
-    return run(sum_kernel, "sum_copies", [((count,) + parts.shape[1:], F32)], parts)[0]
-
-
-def total(part, inner, outer):
-    rows = part.shape[0]
-    count = 2 ** len(inner)
-    scattered = swap(part.reshape(count, rows // count, 128), inner)
-    shared = swap(sum_copies(scattered, 2 ** len(outer)), outer)
-    return swap(sum_copies(shared, count), inner).reshape(rows, 128)
+        out_ref[i] = summed
+
+
+def sum_copies(parts, count, first=0):
+    return run(
+        lambda *refs: sum_kernel(first, *refs),
+        "sum_copies",
+        [((count, parts.shape[1] - first, parts.shape[2]), F32)],
+        parts,
+    )[0]
+
+
+def row_sum_kernel(parts_ref, out_ref):
+    summed = jnp.sum(parts_ref[...], axis=0, keepdims=True)
+    out_ref[...] = jnp.broadcast_to(summed, out_ref.shape)
+
+
+def gather_kernel(parts_ref, pieces_ref, out_ref):
+    summed = tree_sum([parts_ref[i : i + 1] for i in range(parts_ref.shape[0])])
+    rows, width = pieces_ref.shape
+    out_ref[:, :width] = jnp.broadcast_to(summed, (rows, width))
+    out_ref[:, width:] = pieces_ref[...]
 
 
 def mm(left, right, contract):
@@ -198,25 +209,27 @@
     return coeffs, theta
 
 
-def store_packed(ref, matrix):
-    half = matrix.shape[0] // 2
-    ref[...] = jnp.concatenate([matrix[:half], matrix[half:]], axis=1)
-
-
 def load_packed(ref):
     width = ref.shape[1] // 2
     return jnp.concatenate([ref[:, :width], ref[:, width:]], axis=0)
 
 
-def store_copies(ref, value):
-    for i in range(ref.shape[0]):
-        ref[i] = value
-
-
-def gram_kernel(start_ref, gram_ref, copies_ref):
+def store_parcel(ref, value, partial):
+    members, rows = ref.shape[0], value.shape[0]
+    share = partial.shape[0] // members
+    for i in range(members):
+        ref[i, :rows] = value
+        ref[i, rows:] = partial[share * i : share * (i + 1)]
+
+
+def pack(matrix):
+    half = matrix.shape[0] // 2
+    return jnp.concatenate([matrix[:half], matrix[half:]], axis=1)
+
+
+def gram_kernel(start_ref, parcel_ref):
     start = start_ref[...]
-    store_packed(gram_ref, nt(start, start))
-    store_copies(copies_ref, start)
+    store_parcel(parcel_ref, start, pack(nt(start, start)))
 
 
 def pick_kernel(index_ref, own_ref, up_ref, down_ref, slots_ref):
@@ -227,7 +240,7 @@
 
             @pl.when(chosen // count == side)
             def _(ref=ref, slot=slot, chosen=chosen):
-                slots_ref[slot] = ref[chosen % count]
+                slots_ref[slot] = ref[chosen % count, : slots_ref.shape[1]]
 
 
 def multiply_tiles(weight_ref, tiles_ref, slot_values):
@@ -244,7 +257,7 @@
     return acc
 
 
-def start_kernel(weight_ref, gram_ref, start_ref, slots_ref, tiles_ref, block_ref, block_slots_ref, applied_ref, copies_ref, theta_ref):
+def start_kernel(weight_ref, gram_ref, start_ref, slots_ref, tiles_ref, block_ref, block_slots_ref, applied_ref, parcel_ref):
     inverse = inverse_factor(load_packed(gram_ref))
     block = nn(inverse, start_ref[...])
     block_ref[...] = block
@@ -256,11 +269,10 @@
 
     applied = multiply_tiles(weight_ref, tiles_ref, values)
     applied_ref[...] = applied
-    store_copies(copies_ref, applied)
-    store_packed(theta_ref, 0.5 * (nt(block, applied) + nt(applied, block)))
-
-
-def first_kernel(root, weight_ref, sum_ref, block_ref, applied_ref, block_slots_ref, applied_slots_ref, tiles_ref, theta_ref, start_theta_ref, residual_ref, residual_slots_ref, image_ref, copies_ref, grams_ref):
+    store_parcel(parcel_ref, applied, pack(0.5 * (nt(block, applied) + nt(applied, block))))
+
+
+def first_kernel(root, weight_ref, sum_ref, block_ref, applied_ref, block_slots_ref, applied_slots_ref, tiles_ref, theta_ref, start_theta_ref, residual_ref, residual_slots_ref, image_ref, parcel_ref):
     theta = half_sum(load_packed(sum_ref))
     theta_ref[...] = theta
     start_theta_ref[...] = root * theta
@@ -276,11 +288,10 @@
 
     image = multiply_tiles(weight_ref, tiles_ref, values)
     image_ref[...] = image
-    store_copies(copies_ref, image)
     trial = jnp.concatenate([block, residual], axis=0)
     applied_trial = jnp.concatenate([applied, image], axis=0)
     cross = 0.5 * (nt(trial, image) + nt(applied_trial, residual))
-    grams_ref[...] = jnp.concatenate([nt(trial, residual), cross], axis=1)
+    store_parcel(parcel_ref, image, jnp.concatenate([nt(trial, residual), cross], axis=1))
 
 
 def assemble_first(grams, theta):
@@ -328,8 +339,8 @@
     trial = jnp.concatenate([fresh[:columns, :width], residual, fresh[columns:, :width]], axis=0)
     trial_ref[...] = trial
     applied_trial = jnp.concatenate([fresh[:columns, width:], image, fresh[columns:, width:]], axis=0)
-    cross = 0.5 * (nt(trial, image) + nt(applied_trial, residual))
-    grams_out_ref[...] = jnp.concatenate([nt(trial, residual), cross], axis=1)
+    cross = 0.5 * (nt(image, trial) + nt(residual, applied_trial))
+    grams_out_ref[...] = jnp.concatenate([nt(residual, trial), cross], axis=0)
 
 
 def carry_kernel(coeffs_ref, grams_ref, theta_ref, trial_ref, order_ref, carried_ref, pieces_ref):
@@ -352,9 +363,11 @@
     pieces_ref[...] = mm(pick, trial_ref[...], (0, 1))
 
 
-def last_step_kernel(root, grams_ref, carried_ref, theta_ref, arrived_ref, theta_out_ref, embedding_ref, basis_ref):
+def last_step_kernel(root, gathered_ref, carried_ref, theta_ref, theta_out_ref, embedding_ref, basis_ref):
     columns = theta_ref.shape[0]
-    grams = grams_ref[...]
+    width = gathered_ref.shape[1] // 2
+    grams = gathered_ref[:, :width].T
+    arrived = gathered_ref[:, width:]
     carried = carried_ref[...]
     wide = 2 * columns
     overlap = jnp.concatenate([grams[:columns, :columns], carried[:columns, columns:wide]], axis=1)
@@ -396,7 +409,7 @@
     )
     coeffs, theta = project(linv, gram, basis_ref)
     theta_out_ref[...] = theta
-    embedding_ref[...] = root * mm(coeffs, arrived_ref[...], (0, 1))
+    embedding_ref[...] = root * mm(coeffs, arrived, (0, 1))
 
 
 def local(start_block, weight_tiles, tile_scales, neighbour_ids, live_counts, row_order):
@@ -421,30 +434,36 @@
     slab = (columns, rows_dev)
     square = (columns, columns)
     packed = (columns // 2, 2 * columns)
-    slab_copies = ((2 * groups,) + slab, F32)
     slab_slots = ((slots,) + slab, F32)
 
-    def slot_rows(copied):
-        own = swap(copied, CORE_X)
-        down = lax.ppermute(own, "node", to_next)
-        up = lax.ppermute(own, "node", to_last)
-        return run(pick_kernel, "pick_slots", [slab_slots], index, own, up, down, scalars=1)[0]
-
-    gram, copied = run(gram_kernel, "start_gram", [(packed, F32), slab_copies], start_block)
-    start_slots = slot_rows(copied)
-    block, block_slots, applied, copied, theta_part = run(
+    def exchange(parcel):
+        received = swap(parcel, CORE_X)
+        down = lax.ppermute(received, "node", to_next)
+        up = lax.ppermute(received, "node", to_last)
+        rows = run(pick_kernel, "pick_slots", [slab_slots], index, received, up, down, scalars=1)[0]
+        shared = swap(sum_copies(received, 2 ** len(Y_Z), columns), Y_Z)
+        summed = swap(sum_copies(shared, 2 ** len(CORE_X)), CORE_X)
+        return rows, summed.reshape(-1, rows_dev)
+
+    def parcel_of(rows):
+        members = 2 * groups
+        return ((members, columns + rows // members, rows_dev), F32)
+
+    small = parcel_of(columns // 2)
+    start_slots, gram = exchange(run(gram_kernel, "start_gram", [small], start_block)[0])
+    block, block_slots, applied, parcel = run(
         start_kernel,
         "start_step",
-        [(slab, F32), slab_slots, (slab, F32), slab_copies, (packed, F32)],
+        [(slab, F32), slab_slots, (slab, F32), small],
         weights,
-        total(gram, CORE_X, Y_Z),
+        gram,
         start_block,
         start_slots,
         tiles,
         scalars=1,
     )
-    applied_slots = slot_rows(copied)
-    theta, start_theta, residual, residual_slots, image, copied, grams = run(
+    applied_slots, theta_sum = exchange(parcel)
+    theta, start_theta, residual, residual_slots, image, parcel = run(
         lambda *refs: first_kernel(root, *refs),
         "first_residual",
         [
@@ -453,11 +472,10 @@
             (slab, F32),
             slab_slots,
             (slab, F32),
-            slab_copies,
-            ((2 * columns, 2 * columns), F32),
+            parcel_of(2 * columns),
         ],
         weights,
-        total(theta_part, CORE_X, Y_Z),
+        theta_sum,
         block,
         applied,
         block_slots,
@@ -465,8 +483,7 @@
         tiles,
         scalars=1,
     )
-    image_slots = slot_rows(copied)
-    grams = total(grams, CORE_Y, Z_X)
+    image_slots, grams = exchange(parcel)
     coeffs, next_theta, trial, last_grams = run(
         second_kernel,
         "second_step",
@@ -474,7 +491,7 @@
             ((2 * columns, 2 * columns), F32),
             (square, F32),
             ((3 * columns, rows_dev), F32),
-            ((3 * columns, 2 * columns), F32),
+            ((2 * columns, 3 * columns), F32),
         ],
         weights,
         grams,
@@ -501,15 +518,26 @@
         trial,
         row_order,
     )
-    arrived = lax.all_to_all(pieces, "node", split_axis=0, concat_axis=0, tiled=True)
+
+    def over(values, axis):
+        return lax.all_to_all(values, axis, split_axis=0, concat_axis=0, tiled=True)
+
+    row_parts = run(
+        row_sum_kernel, "row_sum", [((groups, 3 * columns), F32)], over(last_grams, "node")
+    )[0]
+    gathered = over(
+        run(
+            gather_kernel, "gather", [((nodes, 6 * columns), F32)], over(row_parts, "grp"), pieces
+        )[0],
+        "node",
+    )
     ritz, embedding = run(
         lambda *refs: last_step_kernel(root, *refs),
         "last_step",
         [(square, F32), (slab, F32)],
-        total(last_grams, CORE_Y, Z_X),
+        gathered,
         carried,
         next_theta,
-        arrived,
         scratch=[pltpu.VMEM((3 * columns, columns), F32)],
     )
     return (embedding, ritz, start_theta)

time: 262 us -> 230 us (0.88)
  blocking collectives: 44.3 us -> 94.9 us
  waiting for transfers between devices: 67.2 us -> 25.2 us
  starting transfers between devices: 99.6 us -> 62.5 us
    all_to_all x0 -> x2, blocking collectives: none -> 38.6 us  [over(): return lax.all_to_all(values, axis, split_axis=0, concat_axis=0, tiled=True)]
    all_to_all x11 -> x5, waiting for transfers between devices: 55.1 us -> 20.7 us  [swap(): lax.all_to_all(values, BOTH, split_axis=0, concat_axis=0, tiled=True, axi...]
    all_to_all x11 -> x5, starting transfers between devices: 66.3 us -> 36.5 us  [swap(): lax.all_to_all(values, BOTH, split_axis=0, concat_axis=0, tiled=True, axi...]
    all_to_all x4, blocking collectives: 44.3 us -> 56.3 us  [swap(): lax.all_to_all(values, BOTH, split_axis=0, concat_axis=0, tiled=True, axi...]
    all_to_all x1, waiting for transfers between devices: 12 us -> 2.57 us  [over(): return lax.all_to_all(values, axis, split_axis=0, concat_axis=0, tiled=True)]
    all_to_all x1, starting transfers between devices: 7.5 us -> 3.25 us  [over(): return lax.all_to_all(values, axis, split_axis=0, concat_axis=0, tiled=True)]
    ppermute x6, starting transfers between devices: 25.8 us -> 22.8 us  [the longest x3 17 us: exchange(): up = lax.ppermute(received, 'node', to_last)]
  transfers between devices with their start and end apart: 18 -> 12, of which waited for: 12 -> 7; matrix products, arithmetic and copies ran while one was open for 0% -> 0% of each run, Pallas kernels for 3% -> 2%
where the time goes in v4:
time: 230 us; the launch traced here: 229 us
  blocking collectives  94.9 us (41%)
  starting transfers between devices  62.5 us (27%)
  Pallas kernels  42.8 us (19%)
  waiting for transfers between devices  25.2 us (11%)
  local copies, waits for them, and re-layouts  2.39 us (1%)
    all_to_all x4, blocking collectives, swap(): lax.all_to_all(values, BOTH, split_axis=0, concat_axis=0, tiled=True, axi...  56.3 us
    pallas_call x17, Pallas kernels, run(): pl.pallas_call(kernel, out_shape=[jax.ShapeDtypeStruct(shape, dtype) for...  42.8 us
    all_to_all x2, blocking collectives, over(): return lax.all_to_all(values, axis, split_axis=0, concat_axis=0, tiled=True)  38.6 us
    all_to_all x5, starting transfers between devices, swap(): lax.all_to_all(values, BOTH, split_axis=0, concat_axis=0, tiled=True, axi...  36.5 us
    all_to_all x5, waiting for transfers between devices, swap(): lax.all_to_all(values, BOTH, split_axis=0, concat_axis=0, tiled=True, axi...  20.7 us
    ppermute x3, starting transfers between devices, exchange(): up = lax.ppermute(received, 'node', to_last)  17 us
    ppermute x3, starting transfers between devices, exchange(): down = lax.ppermute(received, 'node', to_next)  5.76 us
  transfers between devices with their start and end apart: 12, of which 7 were waited for; matrix products, arithmetic and copies ran while one was open for 0% of the time, Pallas kernels for 2%

profile of v4, /device:TPU:1, one launch (start us, length us, event | category | flops | bytes accessed | tf_op | source)
XLA Modules:
  0.0 229.3 jit_solution(10522294182012169689)
XLA Ops:
  1.6 16.6 %all_to_all.78.refs_0_.own_ref = f32[8,68,128]{2,1,0:T(8,128)S(1)} all-to-all(f32[8,68,128]{2,1,0:T(8,128)S(1)} %start_gram.1), channel_id=1, replica_groups={{0,1,128,129,256,257,384,385},{2,3,130,131,258,259,386,387},{4,5,132,13..., dimensions={0} | all-to-all | bytes 557056 | tf_op jit(solution)/shard_map/all_to_all | solution.py:31
  18.9 12.7 %all-to-all-start.1 = ((f32[64,4,128]{2,1,0:T(4,128)}), f32[64,4,128]{2,1,0:T(4,128)S(1)}, u32[]{:S(2)}, u32[]{:S(2)}) async-start(f32[64,4,128]{2,1,0:T(4,128)} %sum_copies.6), calls=%async_computation.1 | async-start | bytes 262144 | tf_op jit(solution)/shard_map/all_to_all | solution.py:31
  32.2 6.6 %collective-permute-start = (f32[8,68,128]{2,1,0:T(8,128)S(1)}, f32[8,68,128]{2,1,0:T(8,128)S(1)}, u32[]{:S(2)}, u32[]{:S(2)}) collective-permute-start(f32[8,68,128]{2,1,0:T(8,128)S(1)} %all_to_all.78.refs_0_.own_ref), channel_id=1, source_target_pairs={{0,126},{1,127},{2,0},{3,1},{4,2},{5,3},{6,4},{7,5},{8,6},{9,7},{1... | collective-permute-start | bytes 835592 | tf_op jit(solution)/shard_map/ppermute | solution.py:442
  38.8 1.9 collective-permute-start.1
  40.7 2.4 %all-to-all-done.1.refs_0_ = f32[64,4,128]{2,1,0:T(4,128)S(1)} async-done(((f32[64,4,128]{2,1,0:T(4,128)}), f32[64,4,128]{2,1,0:T(4,128)S(1)}, u32[]{:S(2)}, u32[]{:S(2)}) %all-to-all-start.1) | async-done | bytes 131104 | tf_op jit(solution)/shard_map/all_to_all | solution.py:31
  43.7 5.4 %all-to-all-start.2 = ((f32[8,4,128]{2,1,0:T(4,128)}), f32[8,4,128]{2,1,0:T(4,128)S(1)}, u32[]{:S(2)}, u32[]{:S(2)}) async-start(f32[8,4,128]{2,1,0:T(4,128)} %sum_copies.7), calls=%async_computation.2 | async-start | bytes 32768 | tf_op jit(solution)/shard_map/all_to_all | solution.py:31
  49.2 1.8 collective-permute-done.1.down_ref
  51.9 1.9 all-to-all-done.2
  53.8 5.3 %start_step.1 = (f32[64,128]{1,0:T(8,128)S(1)}, f32[12,64,128]{2,1,0:T(8,128)S(1)}, f32[64,128]{1,0:T(8,128)S(1)}, f32[8,68,128]{2,1,0:T(8,128)S(1)}) custom-call(f32[12]{0:T(128)S(1)} %compare_select_fusion.2.weight_ref.refs_0_, f32[32,128]{1,0:T(8,128)S(1)} %bitcast.46, f32[64,128]{1,0:T(8,128)S(1)} %copy-done.2, f32[12,64,128]{2,1,0:T(8,128)S(1)} %pick_slots.3.slots_ref, ...), custom_call_target="tpu_custom_call" | custom-call | tf_op jit(solution)/shard_map/start_step/pallas_call | solution.py:39
  59.1 10.4 %all_to_all.79.refs_0_.own_ref = f32[8,68,128]{2,1,0:T(8,128)S(1)} all-to-all(f32[8,68,128]{2,1,0:T(8,128)S(1)} %get-tuple-element.21), channel_id=1, replica_groups={{0,1,128,129,256,257,384,385},{2,3,130,131,258,259,386,387},{4,5,132,13..., dimensions={0} | all-to-all | bytes 557056 | tf_op jit(solution)/shard_map/all_to_all | solution.py:31
  69.6 3.9 %collective-permute-start.2 = (f32[8,68,128]{2,1,0:T(8,128)S(1)}, f32[8,68,128]{2,1,0:T(8,128)S(1)}, u32[]{:S(2)}, u32[]{:S(2)}) collective-permute-start(f32[8,68,128]{2,1,0:T(8,128)S(1)} %all_to_all.79.refs_0_.own_ref), channel_id=1, source_target_pairs={{0,126},{1,127},{2,0},{3,1},{4,2},{5,3},{6,4},{7,5},{8,6},{9,7},{1... | collective-permute-start | bytes 835592 | tf_op jit(solution)/shard_map/ppermute | solution.py:442
  73.5 1.9 collective-permute-start.3
  75.5 18.8 %all_to_all.80.refs_0_ = f32[64,4,128]{2,1,0:T(4,128)S(1)} all-to-all(f32[64,4,128]{2,1,0:T(4,128)S(1)} %sum_copies.8), channel_id=1, replica_groups={{0,2,4,6,8,10,12,14,16,18,20,22,24,26,28,30,32,34,36,38,40,42,44,46,48,..., dimensions={0} | all-to-all | bytes 262144 | tf_op jit(solution)/shard_map/all_to_all | solution.py:31
  94.9 5.8 %all-to-all-start.5 = ((f32[8,4,128]{2,1,0:T(4,128)}), f32[8,4,128]{2,1,0:T(4,128)S(1)}, u32[]{:S(2)}, u32[]{:S(2)}) async-start(f32[8,4,128]{2,1,0:T(4,128)} %sum_copies.9), calls=%async_computation.5 | async-start | bytes 32768 | tf_op jit(solution)/shard_map/all_to_all | solution.py:31
  100.7 0.9 pick_slots.4.refs_5_.applied_slots_ref
  101.6 3.8 %all-to-all-done.5 = f32[8,4,128]{2,1,0:T(4,128)S(1)} async-done(((f32[8,4,128]{2,1,0:T(4,128)}), f32[8,4,128]{2,1,0:T(4,128)S(1)}, u32[]{:S(2)}, u32[]{:S(2)}) %all-to-all-start.5) | async-done | bytes 16416 | tf_op jit(solution)/shard_map/all_to_all | solution.py:31
  105.4 3.0 %first_residual.1 = (f32[64,64]{1,0:T(8,128)S(1)}, f32[64,64]{1,0:T(8,128)}, f32[64,128]{1,0:T(8,128)S(1)}, f32[12,64,128]{2,1,0:T(8,128)S(1)}, f32[64,128]{1,0:T(8,128)S(1)}, /*index=5*/f32[8,80,128]{2,1,0:T(8,128)S(1)}) custom-call(f32[12]{0:T(128)S(1)} %compare_select_fusion.2.weight_ref.refs_0_, f32[32,128]{1,0:T(8,128)S(1)} %bitcast.45, ...), custom_call_target="tpu_custom_call" | custom-call | tf_op jit(solution)/shard_map/first_residual/pallas_call | solution.py:39
  108.3 10.6 %all_to_all.81.refs_0_.own_ref = f32[8,80,128]{2,1,0:T(8,128)S(1)} all-to-all(f32[8,80,128]{2,1,0:T(8,128)S(1)} %get-tuple-element.25), channel_id=1, replica_groups={{0,1,128,129,256,257,384,385},{2,3,130,131,258,259,386,387},{4,5,132,13..., dimensions={0} | all-to-all | bytes 655360 | tf_op jit(solution)/shard_map/all_to_all | solution.py:31
  119.8 4.6 %all-to-all-start.7 = ((f32[64,16,128]{2,1,0:T(8,128)}), f32[64,16,128]{2,1,0:T(8,128)S(1)}, u32[]{:S(2)}, u32[]{:S(2)}) async-start(f32[64,16,128]{2,1,0:T(8,128)} %sum_copies.10), calls=%async_computation.7 | async-start | bytes 1048576 | tf_op jit(solution)/shard_map/all_to_all | solution.py:31
  124.4 6.6 %collective-permute-start.4 = (f32[8,80,128]{2,1,0:T(8,128)S(1)}, f32[8,80,128]{2,1,0:T(8,128)S(1)}, u32[]{:S(2)}, u32[]{:S(2)}) collective-permute-start(f32[8,80,128]{2,1,0:T(8,128)S(1)} %all_to_all.81.refs_0_.own_ref), channel_id=1, source_target_pairs={{0,126},{1,127},{2,0},{3,1},{4,2},{5,3},{6,4},{7,5},{8,6},{9,7},{1... | collective-permute-start | bytes 983048 | tf_op jit(solution)/shard_map/ppermute | solution.py:442
  131.0 1.9 collective-permute-start.5
  132.9 8.9 %all-to-all-done.7.refs_0_ = f32[64,16,128]{2,1,0:T(8,128)S(1)} async-done(((f32[64,16,128]{2,1,0:T(8,128)}), f32[64,16,128]{2,1,0:T(8,128)S(1)}, u32[]{:S(2)}, u32[]{:S(2)}) %all-to-all-start.7) | async-done | bytes 524320 | tf_op jit(solution)/shard_map/all_to_all | solution.py:31
  142.5 7.9 %all-to-all-start.8 = ((f32[8,16,128]{2,1,0:T(8,128)}), f32[8,16,128]{2,1,0:T(8,128)S(1)}, u32[]{:S(2)}, u32[]{:S(2)}) async-start(f32[8,16,128]{2,1,0:T(8,128)} %sum_copies.11), calls=%async_computation.8 | async-start | bytes 131072 | tf_op jit(solution)/shard_map/all_to_all | solution.py:31
  150.4 1.0 pick_slots.5.image_slots_ref
  151.4 3.8 %all-to-all-done.8 = f32[8,16,128]{2,1,0:T(8,128)S(1)} async-done(((f32[8,16,128]{2,1,0:T(8,128)}), f32[8,16,128]{2,1,0:T(8,128)S(1)}, u32[]{:S(2)}, u32[]{:S(2)}) %all-to-all-start.8) | async-done | bytes 65568 | tf_op jit(solution)/shard_map/all_to_all | solution.py:31
  155.3 12.5 %second_step.1 = (f32[128,128]{1,0:T(8,128)S(1)}, f32[64,64]{1,0:T(8,128)S(1)}, f32[192,128]{1,0:T(8,128)S(1)}, f32[128,192]{1,0:T(8,128)S(1)}) custom-call(f32[12]{0:T(128)S(1)} %compare_select_fusion.2.weight_ref.refs_0_, f32[128,128]{1,0:T(8,128)S(1)} %bitcast.41, f32[64,64]{1,0:T(8,128)S(1)} %get-tuple-element.26.theta_ref, ...), custom_call_target="tpu_custom_call" | custom-call | tf_op jit(solution)/shard_map/second_step/pallas_call | solution.py:39
  167.9 18.2 %all_to_all.82 = f32[128,1,192]{2,1,0:T(1,128)S(1)} all-to-all(f32[128,1,192]{2,1,0:T(1,128)S(1)} %copy.12), channel_id=1, replica_groups=mesh['grp'=4,'node'=128] {'node'}, dimensions={0} | all-to-all | bytes 196608 | tf_op jit(solution)/shard_map/all_to_all | solution.py:523
  186.7 3.2 %all-to-all-start.10 = ((f32[4,1,192]{2,1,0:T(1,128)}), f32[4,1,192]{2,1,0:T(1,128)S(1)}, u32[]{:S(2)}, u32[]{:S(2)}) async-start(f32[4,1,192]{2,1,0:T(1,128)} %copy.15), calls=%async_computation.10 | async-start | bytes 8192 | tf_op jit(solution)/shard_map/all_to_all | solution.py:523
  190.6 0.9 carry.1
  191.5 2.6 %all-to-all-done.10 = f32[4,1,192]{2,1,0:T(1,128)S(1)} async-done(((f32[4,1,192]{2,1,0:T(1,128)}), f32[4,1,192]{2,1,0:T(1,128)S(1)}, u32[]{:S(2)}, u32[]{:S(2)}) %all-to-all-start.10) | async-done | bytes 3104 | tf_op jit(solution)/shard_map/all_to_all | solution.py:523
  194.4 20.4 %all_to_all.83 = f32[128,1,384]{2,1,0:T(1,128)S(1)} all-to-all(f32[128,1,384]{2,1,0:T(1,128)S(1)} %copy.16), channel_id=1, replica_groups=mesh['grp'=4,'node'=128] {'node'}, dimensions={0} | all-to-all | bytes 393216 | tf_op jit(solution)/shard_map/all_to_all | solution.py:523
  214.8 14.6 %last_step.1 = (f32[64,64]{1,0:T(8,128)}, f32[64,128]{1,0:T(8,128)}) custom-call(f32[128,384]{1,0:T(8,128)S(1)} %bitcast.39, f32[256,128]{1,0:T(8,128)S(1)} %get-tuple-element.34.refs_1_, f32[64,64]{1,0:T(8,128)S(1)} %get-tuple-element.35.refs_2_), custom_call_target="tpu_custom_call" | custom-call | tf_op jit(solution)/shard_map/last_step/pallas_call | solution.py:39
  (35 shorter events, 7.1 us)
Async XLA Ops:
  0.6 0.8 copy-start.1
  18.9 24.2 %all-to-all-start.1 = ((f32[64,4,128]{2,1,0:T(4,128)}), f32[64,4,128]{2,1,0:T(4,128)S(1)}, u32[]{:S(2)}, u32[]{:S(2)}) async-start(f32[64,4,128]{2,1,0:T(4,128)} %sum_copies.6), calls=%async_computation.1 | async-start | bytes 262144 | tf_op jit(solution)/shard_map/all_to_all | solution.py:31
  32.2 8.5 %copy-start.4 = (f32[1,12]{1,0:T(1,128)S(1)}, f32[1,12]{1,0:T(1,128)}, u32[]{:S(2)}) copy-start(f32[1,12]{1,0:T(1,128)} %param.8) | copy-start | bytes 148
  32.2 17.0 %collective-permute-start = (f32[8,68,128]{2,1,0:T(8,128)S(1)}, f32[8,68,128]{2,1,0:T(8,128)S(1)}, u32[]{:S(2)}, u32[]{:S(2)}) collective-permute-start(f32[8,68,128]{2,1,0:T(8,128)S(1)} %all_to_all.78.refs_0_.own_ref), channel_id=1, source_target_pairs={{0,126},{1,127},{2,0},{3,1},{4,2},{5,3},{6,4},{7,5},{8,6},{9,7},{1... | collective-permute-start | bytes 835592 | tf_op jit(solution)/shard_map/ppermute | solution.py:442
  38.8 12.3 %collective-permute-start.1 = (f32[8,68,128]{2,1,0:T(8,128)S(1)}, f32[8,68,128]{2,1,0:T(8,128)S(1)}, u32[]{:S(2)}, u32[]{:S(2)}) collective-permute-start(f32[8,68,128]{2,1,0:T(8,128)S(1)} %all_to_all.78.refs_0_.own_ref), channel_id=1, source_target_pairs={{0,2},{1,3},{2,4},{3,5},{4,6},{5,7},{6,8},{7,9},{8,10},{9,11},{10,... | collective-permute-start | bytes 835592 | tf_op jit(solution)/shard_map/ppermute | solution.py:441
  43.7 5.4 %copy-start.5 = (s32[1,12]{1,0:T(1,128)S(1)}, s32[1,12]{1,0:T(1,128)}, u32[]{:S(2)}) copy-start(s32[1,12]{1,0:T(1,128)} %param.9) | copy-start | bytes 148
  43.7 10.1 %all-to-all-start.2 = ((f32[8,4,128]{2,1,0:T(4,128)}), f32[8,4,128]{2,1,0:T(4,128)S(1)}, u32[]{:S(2)}, u32[]{:S(2)}) async-start(f32[8,4,128]{2,1,0:T(4,128)} %sum_copies.7), calls=%async_computation.2 | async-start | bytes 32768 | tf_op jit(solution)/shard_map/all_to_all | solution.py:31
  49.2 4.6 %copy-start = (bf16[1,12,128,128]{3,2,1,0:T(8,128)(2,1)S(1)}, bf16[1,12,128,128]{3,2,1,0:T(8,128)(2,1)}, u32[]{:S(2)}) copy-start(bf16[1,12,128,128]{3,2,1,0:T(8,128)(2,1)} %param.7) | copy-start | bytes 1179652
  49.2 4.6 %copy-start.2 = (f32[64,128]{1,0:T(8,128)S(1)}, f32[64,128]{1,0:T(8,128)}, u32[]{:S(2)}) copy-start(f32[64,128]{1,0:T(8,128)} %start_ref.3) | copy-start | bytes 98308
  69.6 31.2 %collective-permute-start.2 = (f32[8,68,128]{2,1,0:T(8,128)S(1)}, f32[8,68,128]{2,1,0:T(8,128)S(1)}, u32[]{:S(2)}, u32[]{:S(2)}) collective-permute-start(f32[8,68,128]{2,1,0:T(8,128)S(1)} %all_to_all.79.refs_0_.own_ref), channel_id=1, source_target_pairs={{0,126},{1,127},{2,0},{3,1},{4,2},{5,3},{6,4},{7,5},{8,6},{9,7},{1... | collective-permute-start | bytes 835592 | tf_op jit(solution)/shard_map/ppermute | solution.py:442
  73.5 27.2 %collective-permute-start.3 = (f32[8,68,128]{2,1,0:T(8,128)S(1)}, f32[8,68,128]{2,1,0:T(8,128)S(1)}, u32[]{:S(2)}, u32[]{:S(2)}) collective-permute-start(f32[8,68,128]{2,1,0:T(8,128)S(1)} %all_to_all.79.refs_0_.own_ref), channel_id=1, source_target_pairs={{0,2},{1,3},{2,4},{3,5},{4,6},{5,7},{6,8},{7,9},{8,10},{9,11},{10,... | collective-permute-start | bytes 835592 | tf_op jit(solution)/shard_map/ppermute | solution.py:441
  94.9 10.5 %all-to-all-start.5 = ((f32[8,4,128]{2,1,0:T(4,128)}), f32[8,4,128]{2,1,0:T(4,128)S(1)}, u32[]{:S(2)}, u32[]{:S(2)}) async-start(f32[8,4,128]{2,1,0:T(4,128)} %sum_copies.9), calls=%async_computation.5 | async-start | bytes 32768 | tf_op jit(solution)/shard_map/all_to_all | solution.py:31
  119.8 22.0 %all-to-all-start.7 = ((f32[64,16,128]{2,1,0:T(8,128)}), f32[64,16,128]{2,1,0:T(8,128)S(1)}, u32[]{:S(2)}, u32[]{:S(2)}) async-start(f32[64,16,128]{2,1,0:T(8,128)} %sum_copies.10), calls=%async_computation.7 | async-start | bytes 1048576 | tf_op jit(solution)/shard_map/all_to_all | solution.py:31
  124.4 26.0 %collective-permute-start.4 = (f32[8,80,128]{2,1,0:T(8,128)S(1)}, f32[8,80,128]{2,1,0:T(8,128)S(1)}, u32[]{:S(2)}, u32[]{:S(2)}) collective-permute-start(f32[8,80,128]{2,1,0:T(8,128)S(1)} %all_to_all.81.refs_0_.own_ref), channel_id=1, source_target_pairs={{0,126},{1,127},{2,0},{3,1},{4,2},{5,3},{6,4},{7,5},{8,6},{9,7},{1... | collective-permute-start | bytes 983048 | tf_op jit(solution)/shard_map/ppermute | solution.py:442
  131.0 19.4 %collective-permute-start.5 = (f32[8,80,128]{2,1,0:T(8,128)S(1)}, f32[8,80,128]{2,1,0:T(8,128)S(1)}, u32[]{:S(2)}, u32[]{:S(2)}) collective-permute-start(f32[8,80,128]{2,1,0:T(8,128)S(1)} %all_to_all.81.refs_0_.own_ref), channel_id=1, source_target_pairs={{0,2},{1,3},{2,4},{3,5},{4,6},{5,7},{6,8},{7,9},{8,10},{9,11},{10,... | collective-permute-start | bytes 983048 | tf_op jit(solution)/shard_map/ppermute | solution.py:441
  142.5 12.8 %all-to-all-start.8 = ((f32[8,16,128]{2,1,0:T(8,128)}), f32[8,16,128]{2,1,0:T(8,128)S(1)}, u32[]{:S(2)}, u32[]{:S(2)}) async-start(f32[8,16,128]{2,1,0:T(8,128)} %sum_copies.11), calls=%async_computation.8 | async-start | bytes 131072 | tf_op jit(solution)/shard_map/all_to_all | solution.py:31
  186.7 7.4 %all-to-all-start.10 = ((f32[4,1,192]{2,1,0:T(1,128)}), f32[4,1,192]{2,1,0:T(1,128)S(1)}, u32[]{:S(2)}, u32[]{:S(2)}) async-start(f32[4,1,192]{2,1,0:T(1,128)} %copy.15), calls=%async_computation.10 | async-start | bytes 8192 | tf_op jit(solution)/shard_map/all_to_all | solution.py:523
  190.0 0.7 copy-start.3

commit v5 on v4

--- a/solution.py
+++ b/solution.py
@@ -7,7 +7,7 @@
 
 REACH = 2
 NSUB = 4
-BLOCK = 4
+BLOCK = 8
 RADIUS = 0.18
 BOTH = ("grp", "node")
 CORE_X = (1, 128, 256)
@@ -232,11 +232,17 @@
     store_parcel(parcel_ref, start, pack(nt(start, start)))
 
 
-def pick_kernel(index_ref, own_ref, up_ref, down_ref, slots_ref):
+def half_kernel(core_ref, own_ref, half_ref):
+    count, rows = half_ref.shape[:2]
+    for i in range(count):
+        half_ref[i] = own_ref[core_ref[0] * count + i, :rows]
+
+
+def pick_kernel(index_ref, own_ref, mine_ref, other_ref, slots_ref):
     count = own_ref.shape[0]
     for slot in range(slots_ref.shape[0]):
         chosen = index_ref[slot]
-        for side, ref in enumerate((down_ref, own_ref, up_ref)):
+        for side, ref in enumerate((mine_ref, own_ref, other_ref)):
 
             @pl.when(chosen // count == side)
             def _(ref=ref, slot=slot, chosen=chosen):
@@ -269,11 +275,13 @@
 
     applied = multiply_tiles(weight_ref, tiles_ref, values)
     applied_ref[...] = applied
-    store_parcel(parcel_ref, applied, pack(0.5 * (nt(block, applied) + nt(applied, block))))
-
-
-def first_kernel(root, weight_ref, sum_ref, block_ref, applied_ref, block_slots_ref, applied_slots_ref, tiles_ref, theta_ref, start_theta_ref, residual_ref, residual_slots_ref, image_ref, parcel_ref):
-    theta = half_sum(load_packed(sum_ref))
+    store_parcel(parcel_ref, applied, pack(nt(block, applied)))
+
+
+def first_kernel(root, weight_ref, sum_ref, block_ref, applied_ref, block_slots_ref, applied_slots_ref, tiles_ref, theta_ref, start_theta_ref, residual_ref, residual_slots_ref, image_ref, parcel_ref, overlap_ref):
+    product = load_packed(sum_ref)
+    theta = half_sum(product)
+    overlap_ref[...] = product - theta
     theta_ref[...] = theta
     start_theta_ref[...] = root * theta
     block = block_ref[...]
@@ -288,28 +296,47 @@
 
     image = multiply_tiles(weight_ref, tiles_ref, values)
     image_ref[...] = image
-    trial = jnp.concatenate([block, residual], axis=0)
-    applied_trial = jnp.concatenate([applied, image], axis=0)
-    cross = 0.5 * (nt(trial, image) + nt(applied_trial, residual))
-    store_parcel(parcel_ref, image, jnp.concatenate([nt(trial, residual), cross], axis=1))
-
-
-def assemble_first(grams, theta):
+    cross = 0.5 * (nt(block, image) + nt(applied, residual))
+    own = nt(residual, image)
+    order = cross.shape[0]
+    row = lax.broadcasted_iota(jnp.int32, (order, order), 0)
+    column = lax.broadcasted_iota(jnp.int32, (order, order), 1)
+    both = jnp.where(row >= column, nt(residual, residual), half_sum(own))
+    diagonal = jnp.sum(jnp.where(row == column, own, F32(0.0)), axis=0, keepdims=True)
+    partial = jnp.concatenate([cross, both], axis=1)
+    tail = jnp.concatenate([diagonal, jnp.zeros_like(diagonal)], axis=1)
+    members = parcel_ref.shape[0]
+    share = order // members
+    for i in range(members):
+        parcel_ref[i, :order] = image
+        parcel_ref[i, order : order + share] = partial[share * i : share * (i + 1)]
+        parcel_ref[i, order + share :] = tail
+
+
+def assemble_first(gathered_ref, theta):
+    members = gathered_ref.shape[0]
     columns = theta.shape[0]
-    cross = grams[:columns, columns:]
-    overlap = grams[:columns, :columns]
-    own = half_sum(grams[columns:, columns:])
-    basis = (overlap, grams[columns:, :columns])
+    share = columns // members
+    grams = jnp.concatenate([gathered_ref[i, :share] for i in range(members)], axis=0)
+    diagonal = gathered_ref[0, share:, :columns]
+    cross = grams[:, :columns]
+    both = grams[:, columns:]
+    turned = both.T
+    row = lax.broadcasted_iota(jnp.int32, (columns, columns), 0)
+    column = lax.broadcasted_iota(jnp.int32, (columns, columns), 1)
+    basis = jnp.where(row >= column, both, turned)
+    own = jnp.where(row < column, both, jnp.where(row > column, turned, diagonal))
     gram = jnp.concatenate(
         [jnp.concatenate([theta, cross], axis=1), jnp.concatenate([cross.T, own], axis=1)], axis=0
     )
     return basis, gram
 
 
-def second_kernel(weight_ref, grams_ref, theta_ref, block_ref, residual_ref, applied_ref, image_ref, block_slots_ref, residual_slots_ref, applied_slots_ref, image_slots_ref, tiles_ref, coeffs_ref, theta_out_ref, trial_ref, grams_out_ref, basis_ref):
+def second_kernel(weight_ref, grams_ref, overlap_ref, theta_ref, block_ref, residual_ref, applied_ref, image_ref, block_slots_ref, residual_slots_ref, applied_slots_ref, image_slots_ref, tiles_ref, coeffs_ref, theta_out_ref, trial_ref, grams_out_ref, basis_ref):
     columns = theta_ref.shape[0]
     width = block_ref.shape[1]
-    (overlap, own), gram = assemble_first(grams_ref[...], theta_ref[...])
+    overlap = overlap_ref[...]
+    own, gram = assemble_first(grams_ref, theta_ref[...])
     factor = inverse_factor(own - tn(overlap, overlap))
     linv = jnp.concatenate(
         [
@@ -343,10 +370,11 @@
     grams_out_ref[...] = jnp.concatenate([nt(residual, trial), cross], axis=0)
 
 
-def carry_kernel(coeffs_ref, grams_ref, theta_ref, trial_ref, order_ref, carried_ref, pieces_ref):
+def carry_kernel(coeffs_ref, grams_ref, overlap_ref, theta_ref, trial_ref, order_ref, carried_ref, pieces_ref):
     columns = theta_ref.shape[0]
     coeffs = coeffs_ref[...]
-    (overlap, own), gram = assemble_first(grams_ref[...], theta_ref[...])
+    overlap = overlap_ref[...]
+    own, gram = assemble_first(grams_ref, theta_ref[...])
     basis = jnp.concatenate(
         [
             jnp.concatenate([eye(columns), overlap], axis=1),
@@ -424,12 +452,18 @@
     node_index = ids % nodes
     chips = nodes // 2
     chip_offset = (node_index // 2 - here // 2 + 1 + chips) % chips
-    index = jnp.clip(chip_offset * 8 + node_index % 2 + 2 * group_index, 0, 23).astype(jnp.int32)
+    core = here % 2
+    member = node_index % 2 + 2 * group_index
+    half = 2 * groups // 2
+    fetched = jnp.where(member // half == core, 0, 4 * groups) + chip_offset // 2 * half + member % half
+    index = jnp.where(chip_offset == 1, 2 * groups + member, fetched)
+    index = jnp.clip(index, 0, 6 * groups - 1).astype(jnp.int32)
     slot_iota = jnp.arange(slots, dtype=jnp.int32)
     weights = jnp.where(slot_iota < live_counts[0], tile_scales[0], F32(0.0))
     tiles = weight_tiles[0]
     to_next = [(source, (source + 2) % nodes) for source in range(nodes)]
     to_last = [(source, (source - 2) % nodes) for source in range(nodes)]
+    to_pair = [(source, source ^ 1) for source in range(nodes)]
     root = float(rows_dev * groups * nodes) ** 0.5
     slab = (columns, rows_dev)
     square = (columns, columns)
@@ -438,32 +472,36 @@
 
     def exchange(parcel):
         received = swap(parcel, CORE_X)
-        down = lax.ppermute(received, "node", to_next)
-        up = lax.ppermute(received, "node", to_last)
-        rows = run(pick_kernel, "pick_slots", [slab_slots], index, received, up, down, scalars=1)[0]
-        shared = swap(sum_copies(received, 2 ** len(Y_Z), columns), Y_Z)
+        partial = sum_copies(received, 2 ** len(Y_Z), columns)
+        shared = swap(partial, Y_Z)
+        later, _ = lax.optimization_barrier((received, partial))
+        part = run(half_kernel, "half", [((half,) + slab, F32)], core[None], later, scalars=1)[0]
+        mine = jnp.concatenate(
+            [lax.ppermute(part, "node", to_next), lax.ppermute(part, "node", to_last)], axis=0
+        )
+        other = lax.ppermute(mine, "node", to_pair)
+        rows = run(pick_kernel, "pick_slots", [slab_slots], index, received, mine, other, scalars=1)[0]
         summed = swap(sum_copies(shared, 2 ** len(CORE_X)), CORE_X)
-        return rows, summed.reshape(-1, rows_dev)
-
-    def parcel_of(rows):
-        members = 2 * groups
-        return ((members, columns + rows // members, rows_dev), F32)
-
-    small = parcel_of(columns // 2)
+        return rows, summed
+
+    def parcel_of(share):
+        return ((2 * groups, columns + share, rows_dev), F32)
+
+    small = parcel_of(columns // (4 * groups))
     start_slots, gram = exchange(run(gram_kernel, "start_gram", [small], start_block)[0])
     block, block_slots, applied, parcel = run(
         start_kernel,
         "start_step",
         [(slab, F32), slab_slots, (slab, F32), small],
         weights,
-        gram,
+        gram.reshape(packed),
         start_block,
         start_slots,
         tiles,
         scalars=1,
     )
     applied_slots, theta_sum = exchange(parcel)
-    theta, start_theta, residual, residual_slots, image, parcel = run(
+    theta, start_theta, residual, residual_slots, image, parcel, overlap = run(
         lambda *refs: first_kernel(root, *refs),
         "first_residual",
         [
@@ -472,10 +510,11 @@
             (slab, F32),
             slab_slots,
             (slab, F32),
-            parcel_of(2 * columns),
+            parcel_of(columns // (2 * groups) + 1),
+            (square, F32),
         ],
         weights,
-        theta_sum,
+        theta_sum.reshape(packed),
         block,
         applied,
         block_slots,
@@ -495,6 +534,7 @@
         ],
         weights,
         grams,
+        overlap,
         theta,
         block,
         residual,
@@ -514,6 +554,7 @@
         [((4 * columns, 2 * columns), F32), ((rows_dev, 3 * columns), F32)],
         coeffs,
         grams,
+        overlap,
         theta,
         trial,
         row_order,

time: 230 us -> 242 us (1.052)
  blocking collectives: 94.9 us -> 64.6 us
  starting transfers between devices: 62.5 us -> 88.4 us
  waiting for transfers between devices: 25.2 us -> 43.7 us
  Pallas kernels: 42.8 us -> 39.5 us
    all_to_all x4 -> x2, blocking collectives: 56.3 us -> 21 us  [swap(): lax.all_to_all(values, BOTH, split_axis=0, concat_axis=0, tiled=True, axi...]
    ppermute x6 -> x9, starting transfers between devices: 22.8 us -> 39.2 us  [the longest x3 22 us: exchange(): lax.ppermute(part, 'node', to_last)]
    all_to_all x5 -> x7, waiting for transfers between devices: 20.7 us -> 33 us  [swap(): lax.all_to_all(values, BOTH, split_axis=0, concat_axis=0, tiled=True, axi...]
    all_to_all x5 -> x7, starting transfers between devices: 36.5 us -> 46 us  [swap(): lax.all_to_all(values, BOTH, split_axis=0, concat_axis=0, tiled=True, axi...]
    ppermute x6 -> x9, waiting for transfers between devices: 1.86 us -> 8.17 us  [the longest x3 8.15 us: exchange(): lax.ppermute(part, 'node', to_last)]
    all_to_all x2, blocking collectives: 38.6 us -> 43.6 us  [over(): return lax.all_to_all(values, axis, split_axis=0, concat_axis=0, tiled=True)]
    pallas_call x17 -> x20, Pallas kernels: 42.8 us -> 39.5 us  [run(): pl.pallas_call(kernel, out_shape=[jax.ShapeDtypeStruct(shape, dtype) for...]
  transfers between devices with their start and end apart: 12 -> 17, of which waited for: 7 -> 8; matrix products, arithmetic and copies ran while one was open for 0% -> 0% of each run, Pallas kernels for 2% -> 2%
where the time goes in v5:
time: 242 us; the launch traced here: 241 us
  starting transfers between devices  88.4 us (37%)
  blocking collectives  64.6 us (27%)
  waiting for transfers between devices  43.7 us (18%)
  Pallas kernels  39.5 us (16%)
  local copies, waits for them, and re-layouts  3.1 us (1%)
    all_to_all x7, starting transfers between devices, swap(): lax.all_to_all(values, BOTH, split_axis=0, concat_axis=0, tiled=True, axi...  46 us
    all_to_all x2, blocking collectives, over(): return lax.all_to_all(values, axis, split_axis=0, concat_axis=0, tiled=True)  43.6 us
    pallas_call x20, Pallas kernels, run(): pl.pallas_call(kernel, out_shape=[jax.ShapeDtypeStruct(shape, dtype) for...  39.5 us
    all_to_all x7, waiting for transfers between devices, swap(): lax.all_to_all(values, BOTH, split_axis=0, concat_axis=0, tiled=True, axi...  33 us
    ppermute x3, starting transfers between devices, exchange(): lax.ppermute(part, 'node', to_last)  22 us
    all_to_all x2, blocking collectives, swap(): lax.all_to_all(values, BOTH, split_axis=0, concat_axis=0, tiled=True, axi...  21 us
    ppermute x3, starting transfers between devices, exchange(): other = lax.ppermute(mine, 'node', to_pair)  10.6 us
    ppermute x3, waiting for transfers between devices, exchange(): lax.ppermute(part, 'node', to_last)  8.15 us
  transfers between devices with their start and end apart: 17, of which 8 were waited for; matrix products, arithmetic and copies ran while one was open for 0% of the time, Pallas kernels for 2%

profile of v5, /device:TPU:1, one launch (start us, length us, event | category | flops | bytes accessed | tf_op | source)
XLA Modules:
  0.0 241.0 jit_solution(16465750020880414035)
XLA Ops:
  2.4 10.2 %all-to-all-start = ((f32[8,68,128]{2,1,0:T(8,128)}), f32[8,68,128]{2,1,0:T(8,128)S(1)}, u32[]{:S(2)}, u32[]{:S(2)}) async-start(f32[8,68,128]{2,1,0:T(8,128)} %start_gram.1), calls=%async_computation | async-start | bytes 589824 | tf_op jit(solution)/shard_map/all_to_all | solution.py:31
  12.6 6.8 %all-to-all-done.refs_0_.own_ref = f32[8,68,128]{2,1,0:T(8,128)S(1)} async-done(((f32[8,68,128]{2,1,0:T(8,128)}), f32[8,68,128]{2,1,0:T(8,128)S(1)}, u32[]{:S(2)}, u32[]{:S(2)}) %all-to-all-start) | async-done | bytes 278560 | tf_op jit(solution)/shard_map/all_to_all | solution.py:31
  22.0 9.2 %collective-permute-start.1 = (f32[4,64,128]{2,1,0:T(8,128)S(1)}, f32[4,64,128]{2,1,0:T(8,128)S(1)}, u32[]{:S(2)}, u32[]{:S(2)}) collective-permute-start(f32[4,64,128]{2,1,0:T(8,128)S(1)} %half.3), channel_id=1, source_target_pairs={{0,126},{1,127},{2,0},{3,1},{4,2},{5,3},{6,4},{7,5},{8,6},{9,7},{1... | collective-permute-start | bytes 393224 | tf_op jit(solution)/shard_map/ppermute | solution.py:480
  31.2 7.3 %all-to-all-start.1 = ((f32[64,4,128]{2,1,0:T(4,128)}), f32[64,4,128]{2,1,0:T(4,128)S(1)}, u32[]{:S(2)}, u32[]{:S(2)}) async-start(f32[64,4,128]{2,1,0:T(4,128)} %sum_copies.6), calls=%async_computation.1 | async-start | bytes 262144 | tf_op jit(solution)/shard_map/all_to_all | solution.py:31
  38.6 3.8 %collective-permute-start.2 = (f32[8,64,128]{2,1,0:T(8,128)S(1)}, f32[8,64,128]{2,1,0:T(8,128)S(1)}, u32[]{:S(2)}, u32[]{:S(2)}) collective-permute-start(f32[8,64,128]{2,1,0:T(8,128)S(1)} %constant_dynamic-update-slice_fusion.mine_ref), channel_id=1, source_target_pairs={{0,1},{1,0},{2,3},{3,2},{4,5},{5,4},{6,7},{7,6},{8,9},{9,8},{10,11... | collective-permute-start | bytes 786440 | tf_op jit(solution)/shard_map/ppermute | solution.py:482
  43.1 6.9 %all-to-all-done.1.refs_0_ = f32[64,4,128]{2,1,0:T(4,128)S(1)} async-done(((f32[64,4,128]{2,1,0:T(4,128)}), f32[64,4,128]{2,1,0:T(4,128)S(1)}, u32[]{:S(2)}, u32[]{:S(2)}) %all-to-all-start.1) | async-done | bytes 131104 | tf_op jit(solution)/shard_map/all_to_all | solution.py:31
  50.7 6.4 %all-to-all-start.2 = ((f32[8,4,128]{2,1,0:T(4,128)}), f32[8,4,128]{2,1,0:T(4,128)S(1)}, u32[]{:S(2)}, u32[]{:S(2)}) async-start(f32[8,4,128]{2,1,0:T(4,128)} %sum_copies.7), calls=%async_computation.2 | async-start | bytes 32768 | tf_op jit(solution)/shard_map/all_to_all | solution.py:31
  58.6 3.1 %all-to-all-done.2 = f32[8,4,128]{2,1,0:T(4,128)S(1)} async-done(((f32[8,4,128]{2,1,0:T(4,128)}), f32[8,4,128]{2,1,0:T(4,128)S(1)}, u32[]{:S(2)}, u32[]{:S(2)}) %all-to-all-start.2) | async-done | bytes 16416 | tf_op jit(solution)/shard_map/all_to_all | solution.py:31
  61.7 4.5 %start_step.1 = (f32[64,128]{1,0:T(8,128)S(1)}, f32[12,64,128]{2,1,0:T(8,128)S(1)}, f32[64,128]{1,0:T(8,128)S(1)}, f32[8,68,128]{2,1,0:T(8,128)S(1)}) custom-call(f32[12]{0:T(128)S(1)} %compare_select_fusion.4.weight_ref.refs_0_, f32[32,128]{1,0:T(8,128)S(1)} %bitcast.44, f32[64,128]{1,0:T(8,128)S(1)} %copy-done.2, f32[12,64,128]{2,1,0:T(8,128)S(1)} %pick_slots.3.slots_ref, ...), custom_call_target="tpu_custom_call" | custom-call | tf_op jit(solution)/shard_map/start_step/pallas_call | solution.py:39
  66.3 10.5 %all_to_all.78.refs_0_.own_ref = f32[8,68,128]{2,1,0:T(8,128)S(1)} all-to-all(f32[8,68,128]{2,1,0:T(8,128)S(1)} %get-tuple-element.26), channel_id=1, replica_groups={{0,1,128,129,256,257,384,385},{2,3,130,131,258,259,386,387},{4,5,132,13..., dimensions={0} | all-to-all | bytes 557056 | tf_op jit(solution)/shard_map/all_to_all | solution.py:31
  77.4 2.3 collective-permute-start.3
  79.7 6.3 %collective-permute-start.4 = (f32[4,64,128]{2,1,0:T(8,128)S(1)}, f32[4,64,128]{2,1,0:T(8,128)S(1)}, u32[]{:S(2)}, u32[]{:S(2)}) collective-permute-start(f32[4,64,128]{2,1,0:T(8,128)S(1)} %half.4), channel_id=1, source_target_pairs={{0,126},{1,127},{2,0},{3,1},{4,2},{5,3},{6,4},{7,5},{8,6},{9,7},{1... | collective-permute-start | bytes 393224 | tf_op jit(solution)/shard_map/ppermute | solution.py:480
  86.0 4.6 %all-to-all-start.4 = ((f32[64,4,128]{2,1,0:T(4,128)}), f32[64,4,128]{2,1,0:T(4,128)S(1)}, u32[]{:S(2)}, u32[]{:S(2)}) async-start(f32[64,4,128]{2,1,0:T(4,128)} %sum_copies.8), calls=%async_computation.4 | async-start | bytes 262144 | tf_op jit(solution)/shard_map/all_to_all | solution.py:31
  90.7 3.0 %collective-permute-start.5 = (f32[8,64,128]{2,1,0:T(8,128)S(1)}, f32[8,64,128]{2,1,0:T(8,128)S(1)}, u32[]{:S(2)}, u32[]{:S(2)}) collective-permute-start(f32[8,64,128]{2,1,0:T(8,128)S(1)} %constant_dynamic-update-slice_fusion.2.mine_ref), channel_id=1, source_target_pairs={{0,1},{1,0},{2,3},{3,2},{4,5},{5,4},{6,7},{7,6},{8,9},{9,8},{10,11... | collective-permute-start | bytes 786440 | tf_op jit(solution)/shard_map/ppermute | solution.py:482
  93.8 8.5 %all-to-all-done.4.refs_0_ = f32[64,4,128]{2,1,0:T(4,128)S(1)} async-done(((f32[64,4,128]{2,1,0:T(4,128)}), f32[64,4,128]{2,1,0:T(4,128)S(1)}, u32[]{:S(2)}, u32[]{:S(2)}) %all-to-all-start.4) | async-done | bytes 131104 | tf_op jit(solution)/shard_map/all_to_all | solution.py:31
  102.9 5.5 %all-to-all-start.5 = ((f32[8,4,128]{2,1,0:T(4,128)}), f32[8,4,128]{2,1,0:T(4,128)S(1)}, u32[]{:S(2)}, u32[]{:S(2)}) async-start(f32[8,4,128]{2,1,0:T(4,128)} %sum_copies.9), calls=%async_computation.5 | async-start | bytes 32768 | tf_op jit(solution)/shard_map/all_to_all | solution.py:31
  109.3 3.8 %all-to-all-done.5 = f32[8,4,128]{2,1,0:T(4,128)S(1)} async-done(((f32[8,4,128]{2,1,0:T(4,128)}), f32[8,4,128]{2,1,0:T(4,128)S(1)}, u32[]{:S(2)}, u32[]{:S(2)}) %all-to-all-start.5) | async-done | bytes 16416 | tf_op jit(solution)/shard_map/all_to_all | solution.py:31
  113.1 3.2 %first_residual.1 = (f32[64,64]{1,0:T(8,128)S(1)}, f32[64,64]{1,0:T(8,128)}, f32[64,128]{1,0:T(8,128)S(1)}, f32[12,64,128]{2,1,0:T(8,128)S(1)}, f32[64,128]{1,0:...) custom-call(f32[12]{0:T(128)S(1)} %compare_select_fusion.4.weight_ref.refs_0_, f32[32,128]{1,0:T(8,128)S(1)} %bitcast.43, ...), custom_call_target="tpu_custom_call" | custom-call | tf_op jit(solution)/shard_map/first_residual/pallas_call | solution.py:39
  116.2 10.6 %all_to_all.79.refs_0_.own_ref = f32[8,73,128]{2,1,0:T(8,128)S(1)} all-to-all(f32[8,73,128]{2,1,0:T(8,128)S(1)} %get-tuple-element.31), channel_id=1, replica_groups={{0,1,128,129,256,257,384,385},{2,3,130,131,258,259,386,387},{4,5,132,13..., dimensions={0} | all-to-all | bytes 598016 | tf_op jit(solution)/shard_map/all_to_all | solution.py:31
  127.6 2.4 collective-permute-start.6
  130.0 6.6 %all-to-all-start.7 = ((f32[64,9,128]{2,1,0:T(8,128)}), f32[64,9,128]{2,1,0:T(8,128)S(1)}, u32[]{:S(2)}, u32[]{:S(2)}) async-start(f32[64,9,128]{2,1,0:T(8,128)} %sum_copies.10), calls=%async_computation.7 | async-start | bytes 1048576 | tf_op jit(solution)/shard_map/all_to_all | solution.py:31
  136.6 6.6 %collective-permute-start.7 = (f32[4,64,128]{2,1,0:T(8,128)S(1)}, f32[4,64,128]{2,1,0:T(8,128)S(1)}, u32[]{:S(2)}, u32[]{:S(2)}) collective-permute-start(f32[4,64,128]{2,1,0:T(8,128)S(1)} %half.5), channel_id=1, source_target_pairs={{0,126},{1,127},{2,0},{3,1},{4,2},{5,3},{6,4},{7,5},{8,6},{9,7},{1... | collective-permute-start | bytes 393224 | tf_op jit(solution)/shard_map/ppermute | solution.py:480
  143.2 8.1 %collective-permute-done.7 = f32[4,64,128]{2,1,0:T(8,128)S(1)} collective-permute-done((f32[4,64,128]{2,1,0:T(8,128)S(1)}, f32[4,64,128]{2,1,0:T(8,128)S(1)}, u32[]{:S(2)}, u32[]{:S(2)}) %collective-permute-start.7) | collective-permute-done | bytes 131104 | tf_op jit(solution)/shard_map/ppermute | solution.py:480
  151.4 3.7 %collective-permute-start.8 = (f32[8,64,128]{2,1,0:T(8,128)S(1)}, f32[8,64,128]{2,1,0:T(8,128)S(1)}, u32[]{:S(2)}, u32[]{:S(2)}) collective-permute-start(f32[8,64,128]{2,1,0:T(8,128)S(1)} %constant_dynamic-update-slice_fusion.4.mine_ref), channel_id=1, source_target_pairs={{0,1},{1,0},{2,3},{3,2},{4,5},{5,4},{6,7},{7,6},{8,9},{9,8},{10,11... | collective-permute-start | bytes 786440 | tf_op jit(solution)/shard_map/ppermute | solution.py:482
  155.8 5.4 %all-to-all-start.8 = ((f32[8,9,128]{2,1,0:T(8,128)}), f32[8,9,128]{2,1,0:T(8,128)S(1)}, u32[]{:S(2)}, u32[]{:S(2)}) async-start(f32[8,9,128]{2,1,0:T(8,128)} %sum_copies.11), calls=%async_computation.8 | async-start | bytes 131072 | tf_op jit(solution)/shard_map/all_to_all | solution.py:31
  162.2 3.8 %all-to-all-done.8.grams_ref = f32[8,9,128]{2,1,0:T(8,128)S(1)} async-done(((f32[8,9,128]{2,1,0:T(8,128)}), f32[8,9,128]{2,1,0:T(8,128)S(1)}, u32[]{:S(2)}, u32[]{:S(2)}) %all-to-all-start.8) | async-done | bytes 36896 | tf_op jit(solution)/shard_map/all_to_all | solution.py:31
  166.0 10.8 %second_step.1 = (f32[128,128]{1,0:T(8,128)S(1)}, f32[64,64]{1,0:T(8,128)S(1)}, f32[192,128]{1,0:T(8,128)S(1)}, f32[128,192]{1,0:T(8,128)S(1)}) custom-call(f32[12]{0:T(128)S(1)} %compare_select_fusion.4.weight_ref.refs_0_, f32[8,9,128]{2,1,0:T(8,128)S(1)} %all-to-all-done.8.grams_ref, f32[64,64]{1,0:T(8,128)S(1)} %get-tuple-element.32.overlap_ref, ...), custom_call_target="tpu_custom_call" | custom-call | tf_op jit(solution)/shard_map/second_step/pallas_call | solution.py:39
  177.0 23.2 %all_to_all.80 = f32[128,1,192]{2,1,0:T(1,128)S(1)} all-to-all(f32[128,1,192]{2,1,0:T(1,128)S(1)} %copy.12), channel_id=1, replica_groups=mesh['grp'=4,'node'=128] {'node'}, dimensions={0} | all-to-all | bytes 196608 | tf_op jit(solution)/shard_map/all_to_all | solution.py:564
  200.8 3.2 %all-to-all-start.10 = ((f32[4,1,192]{2,1,0:T(1,128)}), f32[4,1,192]{2,1,0:T(1,128)S(1)}, u32[]{:S(2)}, u32[]{:S(2)}) async-start(f32[4,1,192]{2,1,0:T(1,128)} %copy.15), calls=%async_computation.10 | async-start | bytes 8192 | tf_op jit(solution)/shard_map/all_to_all | solution.py:564
  205.7 2.5 %all-to-all-done.10 = f32[4,1,192]{2,1,0:T(1,128)S(1)} async-done(((f32[4,1,192]{2,1,0:T(1,128)}), f32[4,1,192]{2,1,0:T(1,128)S(1)}, u32[]{:S(2)}, u32[]{:S(2)}) %all-to-all-start.10) | async-done | bytes 3104 | tf_op jit(solution)/shard_map/all_to_all | solution.py:564
  208.5 20.4 %all_to_all.81 = f32[128,1,384]{2,1,0:T(1,128)S(1)} all-to-all(f32[128,1,384]{2,1,0:T(1,128)S(1)} %copy.16), channel_id=1, replica_groups=mesh['grp'=4,'node'=128] {'node'}, dimensions={0} | all-to-all | bytes 393216 | tf_op jit(solution)/shard_map/all_to_all | solution.py:564
  228.9 12.1 %last_step.1 = (f32[64,64]{1,0:T(8,128)}, f32[64,128]{1,0:T(8,128)}) custom-call(f32[128,384]{1,0:T(8,128)S(1)} %bitcast.39, f32[256,128]{1,0:T(8,128)S(1)} %get-tuple-element.42.refs_1_, f32[64,64]{1,0:T(8,128)S(1)} %get-tuple-element.43.refs_2_), custom_call_target="tpu_custom_call" | custom-call | tf_op jit(solution)/shard_map/last_step/pallas_call | solution.py:39
  (52 shorter events, 14.0 us)
Async XLA Ops:
  0.6 0.8 copy-start.1
  2.4 17.0 %all-to-all-start = ((f32[8,68,128]{2,1,0:T(8,128)}), f32[8,68,128]{2,1,0:T(8,128)S(1)}, u32[]{:S(2)}, u32[]{:S(2)}) async-start(f32[8,68,128]{2,1,0:T(8,128)} %start_gram.1), calls=%async_computation | async-start | bytes 589824 | tf_op jit(solution)/shard_map/all_to_all | solution.py:31
  20.1 18.4 %collective-permute-start = (f32[4,64,128]{2,1,0:T(8,128)S(1)}, f32[4,64,128]{2,1,0:T(8,128)S(1)}, u32[]{:S(2)}, u32[]{:S(2)}) collective-permute-start(f32[4,64,128]{2,1,0:T(8,128)S(1)} %half.3), channel_id=1, source_target_pairs={{0,2},{1,3},{2,4},{3,5},{4,6},{5,7},{6,8},{7,9},{8,10},{9,11},{10,... | collective-permute-start | bytes 393224 | tf_op jit(solution)/shard_map/ppermute | solution.py:480
  22.0 16.5 %collective-permute-start.1 = (f32[4,64,128]{2,1,0:T(8,128)S(1)}, f32[4,64,128]{2,1,0:T(8,128)S(1)}, u32[]{:S(2)}, u32[]{:S(2)}) collective-permute-start(f32[4,64,128]{2,1,0:T(8,128)S(1)} %half.3), channel_id=1, source_target_pairs={{0,126},{1,127},{2,0},{3,1},{4,2},{5,3},{6,4},{7,5},{8,6},{9,7},{1... | collective-permute-start | bytes 393224 | tf_op jit(solution)/shard_map/ppermute | solution.py:480
  31.2 18.9 %all-to-all-start.1 = ((f32[64,4,128]{2,1,0:T(4,128)}), f32[64,4,128]{2,1,0:T(4,128)S(1)}, u32[]{:S(2)}, u32[]{:S(2)}) async-start(f32[64,4,128]{2,1,0:T(4,128)} %sum_copies.6), calls=%async_computation.1 | async-start | bytes 262144 | tf_op jit(solution)/shard_map/all_to_all | solution.py:31
  38.5 3.9 %copy-start.4 = (s32[1,12]{1,0:T(1,128)S(1)}, s32[1,12]{1,0:T(1,128)}, u32[]{:S(2)}) copy-start(s32[1,12]{1,0:T(1,128)} %param.9) | copy-start | bytes 148
  38.6 19.2 %collective-permute-start.2 = (f32[8,64,128]{2,1,0:T(8,128)S(1)}, f32[8,64,128]{2,1,0:T(8,128)S(1)}, u32[]{:S(2)}, u32[]{:S(2)}) collective-permute-start(f32[8,64,128]{2,1,0:T(8,128)S(1)} %constant_dynamic-update-slice_fusion.mine_ref), channel_id=1, source_target_pairs={{0,1},{1,0},{2,3},{3,2},{4,5},{5,4},{6,7},{7,6},{8,9},{9,8},{10,11... | collective-permute-start | bytes 786440 | tf_op jit(solution)/shard_map/ppermute | solution.py:482
  50.7 11.0 %all-to-all-start.2 = ((f32[8,4,128]{2,1,0:T(4,128)}), f32[8,4,128]{2,1,0:T(4,128)S(1)}, u32[]{:S(2)}, u32[]{:S(2)}) async-start(f32[8,4,128]{2,1,0:T(4,128)} %sum_copies.7), calls=%async_computation.2 | async-start | bytes 32768 | tf_op jit(solution)/shard_map/all_to_all | solution.py:31
  57.1 0.7 copy-start.5
  57.7 4.0 %copy-start = (bf16[1,12,128,128]{3,2,1,0:T(8,128)(2,1)S(1)}, bf16[1,12,128,128]{3,2,1,0:T(8,128)(2,1)}, u32[]{:S(2)}) copy-start(bf16[1,12,128,128]{3,2,1,0:T(8,128)(2,1)} %param.7) | copy-start | bytes 1179652
  57.7 4.0 %copy-start.2 = (f32[64,128]{1,0:T(8,128)S(1)}, f32[64,128]{1,0:T(8,128)}, u32[]{:S(2)}) copy-start(f32[64,128]{1,0:T(8,128)} %start_ref.3) | copy-start | bytes 98308
  77.4 13.3 %collective-permute-start.3 = (f32[4,64,128]{2,1,0:T(8,128)S(1)}, f32[4,64,128]{2,1,0:T(8,128)S(1)}, u32[]{:S(2)}, u32[]{:S(2)}) collective-permute-start(f32[4,64,128]{2,1,0:T(8,128)S(1)} %half.4), channel_id=1, source_target_pairs={{0,2},{1,3},{2,4},{3,5},{4,6},{5,7},{6,8},{7,9},{8,10},{9,11},{10,... | collective-permute-start | bytes 393224 | tf_op jit(solution)/shard_map/ppermute | solution.py:480
  79.7 11.0 %collective-permute-start.4 = (f32[4,64,128]{2,1,0:T(8,128)S(1)}, f32[4,64,128]{2,1,0:T(8,128)S(1)}, u32[]{:S(2)}, u32[]{:S(2)}) collective-permute-start(f32[4,64,128]{2,1,0:T(8,128)S(1)} %half.4), channel_id=1, source_target_pairs={{0,126},{1,127},{2,0},{3,1},{4,2},{5,3},{6,4},{7,5},{8,6},{9,7},{1... | collective-permute-start | bytes 393224 | tf_op jit(solution)/shard_map/ppermute | solution.py:480
  86.0 16.3 %all-to-all-start.4 = ((f32[64,4,128]{2,1,0:T(4,128)}), f32[64,4,128]{2,1,0:T(4,128)S(1)}, u32[]{:S(2)}, u32[]{:S(2)}) async-start(f32[64,4,128]{2,1,0:T(4,128)} %sum_copies.8), calls=%async_computation.4 | async-start | bytes 262144 | tf_op jit(solution)/shard_map/all_to_all | solution.py:31
  90.7 17.6 %collective-permute-start.5 = (f32[8,64,128]{2,1,0:T(8,128)S(1)}, f32[8,64,128]{2,1,0:T(8,128)S(1)}, u32[]{:S(2)}, u32[]{:S(2)}) collective-permute-start(f32[8,64,128]{2,1,0:T(8,128)S(1)} %constant_dynamic-update-slice_fusion.2.mine_ref), channel_id=1, source_target_pairs={{0,1},{1,0},{2,3},{3,2},{4,5},{5,4},{6,7},{7,6},{8,9},{9,8},{10,11... | collective-permute-start | bytes 786440 | tf_op jit(solution)/shard_map/ppermute | solution.py:482
  102.9 10.1 %all-to-all-start.5 = ((f32[8,4,128]{2,1,0:T(4,128)}), f32[8,4,128]{2,1,0:T(4,128)S(1)}, u32[]{:S(2)}, u32[]{:S(2)}) async-start(f32[8,4,128]{2,1,0:T(4,128)} %sum_copies.9), calls=%async_computation.5 | async-start | bytes 32768 | tf_op jit(solution)/shard_map/all_to_all | solution.py:31
  127.6 15.6 %collective-permute-start.6 = (f32[4,64,128]{2,1,0:T(8,128)S(1)}, f32[4,64,128]{2,1,0:T(8,128)S(1)}, u32[]{:S(2)}, u32[]{:S(2)}) collective-permute-start(f32[4,64,128]{2,1,0:T(8,128)S(1)} %half.5), channel_id=1, source_target_pairs={{0,2},{1,3},{2,4},{3,5},{4,6},{5,7},{6,8},{7,9},{8,10},{9,11},{10,... | collective-permute-start | bytes 393224 | tf_op jit(solution)/shard_map/ppermute | solution.py:480
  130.0 25.1 %all-to-all-start.7 = ((f32[64,9,128]{2,1,0:T(8,128)}), f32[64,9,128]{2,1,0:T(8,128)S(1)}, u32[]{:S(2)}, u32[]{:S(2)}) async-start(f32[64,9,128]{2,1,0:T(8,128)} %sum_copies.10), calls=%async_computation.7 | async-start | bytes 1048576 | tf_op jit(solution)/shard_map/all_to_all | solution.py:31
  136.6 14.7 %collective-permute-start.7 = (f32[4,64,128]{2,1,0:T(8,128)S(1)}, f32[4,64,128]{2,1,0:T(8,128)S(1)}, u32[]{:S(2)}, u32[]{:S(2)}) collective-permute-start(f32[4,64,128]{2,1,0:T(8,128)S(1)} %half.5), channel_id=1, source_target_pairs={{0,126},{1,127},{2,0},{3,1},{4,2},{5,3},{6,4},{7,5},{8,6},{9,7},{1... | collective-permute-start | bytes 393224 | tf_op jit(solution)/shard_map/ppermute | solution.py:480
  151.4 9.8 %collective-permute-start.8 = (f32[8,64,128]{2,1,0:T(8,128)S(1)}, f32[8,64,128]{2,1,0:T(8,128)S(1)}, u32[]{:S(2)}, u32[]{:S(2)}) collective-permute-start(f32[8,64,128]{2,1,0:T(8,128)S(1)} %constant_dynamic-update-slice_fusion.4.mine_ref), channel_id=1, source_target_pairs={{0,1},{1,0},{2,3},{3,2},{4,5},{5,4},{6,7},{7,6},{8,9},{9,8},{10,11... | collective-permute-start | bytes 786440 | tf_op jit(solution)/shard_map/ppermute | solution.py:482
  155.8 10.3 %all-to-all-start.8 = ((f32[8,9,128]{2,1,0:T(8,128)}), f32[8,9,128]{2,1,0:T(8,128)S(1)}, u32[]{:S(2)}, u32[]{:S(2)}) async-start(f32[8,9,128]{2,1,0:T(8,128)} %sum_copies.11), calls=%async_computation.8 | async-start | bytes 131072 | tf_op jit(solution)/shard_map/all_to_all | solution.py:31
  200.8 7.4 %all-to-all-start.10 = ((f32[4,1,192]{2,1,0:T(1,128)}), f32[4,1,192]{2,1,0:T(1,128)S(1)}, u32[]{:S(2)}, u32[]{:S(2)}) async-start(f32[4,1,192]{2,1,0:T(1,128)} %copy.15), calls=%async_computation.10 | async-start | bytes 8192 | tf_op jit(solution)/shard_map/all_to_all | solution.py:564
  204.1 0.7 copy-start.3

commit v6 on v5

--- a/solution.py
+++ b/solution.py
@@ -232,21 +232,16 @@
     store_parcel(parcel_ref, start, pack(nt(start, start)))
 
 
-def half_kernel(core_ref, own_ref, half_ref):
-    count, rows = half_ref.shape[:2]
-    for i in range(count):
-        half_ref[i] = own_ref[core_ref[0] * count + i, :rows]
-
-
-def pick_kernel(index_ref, own_ref, mine_ref, other_ref, slots_ref):
+def neighbour_rows(index_ref, own_ref, up_ref, down_ref, rows):
     count = own_ref.shape[0]
-    for slot in range(slots_ref.shape[0]):
-        chosen = index_ref[slot]
-        for side, ref in enumerate((mine_ref, own_ref, other_ref)):
-
-            @pl.when(chosen // count == side)
-            def _(ref=ref, slot=slot, chosen=chosen):
-                slots_ref[slot] = ref[chosen % count, : slots_ref.shape[1]]
+
+    def at(slot):
+        side = lax.div(index_ref[slot], count)
+        member = lax.rem(index_ref[slot], count)
+        outer = jnp.where(side == 0, down_ref[member, :rows], up_ref[member, :rows])
+        return jnp.where(side == 1, own_ref[member, :rows], outer)
+
+    return at
 
 
 def multiply_tiles(weight_ref, tiles_ref, slot_values):
@@ -263,13 +258,15 @@
     return acc
 
 
-def start_kernel(weight_ref, gram_ref, start_ref, slots_ref, tiles_ref, block_ref, block_slots_ref, applied_ref, parcel_ref):
+def start_kernel(weight_ref, index_ref, own_ref, up_ref, down_ref, gram_ref, start_ref, tiles_ref, block_ref, block_slots_ref, applied_ref, parcel_ref):
     inverse = inverse_factor(load_packed(gram_ref))
     block = nn(inverse, start_ref[...])
     block_ref[...] = block
 
+    rows_at = neighbour_rows(index_ref, own_ref, up_ref, down_ref, block.shape[0])
+
     def values(slot):
-        there = nn(inverse, slots_ref[slot])
+        there = nn(inverse, rows_at(slot))
         block_slots_ref[slot] = there
         return there
 
@@ -278,7 +275,7 @@
     store_parcel(parcel_ref, applied, pack(nt(block, applied)))
 
 
-def first_kernel(root, weight_ref, sum_ref, block_ref, applied_ref, block_slots_ref, applied_slots_ref, tiles_ref, theta_ref, start_theta_ref, residual_ref, residual_slots_ref, image_ref, parcel_ref, overlap_ref):
+def first_kernel(root, weight_ref, index_ref, own_ref, up_ref, down_ref, sum_ref, block_ref, applied_ref, block_slots_ref, tiles_ref, theta_ref, start_theta_ref, residual_ref, residual_slots_ref, image_ref, parcel_ref, overlap_ref, applied_slots_ref):
     product = load_packed(sum_ref)
     theta = half_sum(product)
     overlap_ref[...] = product - theta
@@ -289,8 +286,12 @@
     residual = applied - nn(theta, block)
     residual_ref[...] = residual
 
+    rows_at = neighbour_rows(index_ref, own_ref, up_ref, down_ref, block.shape[0])
+
     def values(slot):
-        there = applied_slots_ref[slot] - nn(theta, block_slots_ref[slot])
+        applied_there = rows_at(slot)
+        applied_slots_ref[slot] = applied_there
+        there = applied_there - nn(theta, block_slots_ref[slot])
         residual_slots_ref[slot] = there
         return there
 
@@ -332,7 +333,7 @@
     return basis, gram
 
 
-def second_kernel(weight_ref, grams_ref, overlap_ref, theta_ref, block_ref, residual_ref, applied_ref, image_ref, block_slots_ref, residual_slots_ref, applied_slots_ref, image_slots_ref, tiles_ref, coeffs_ref, theta_out_ref, trial_ref, grams_out_ref, basis_ref):
+def second_kernel(weight_ref, index_ref, own_ref, up_ref, down_ref, grams_ref, overlap_ref, theta_ref, block_ref, residual_ref, applied_ref, image_ref, block_slots_ref, residual_slots_ref, applied_slots_ref, tiles_ref, coeffs_ref, theta_out_ref, trial_ref, grams_out_ref, basis_ref):
     columns = theta_ref.shape[0]
     width = block_ref.shape[1]
     overlap = overlap_ref[...]
@@ -352,9 +353,16 @@
     coeffs_ref[...] = both
     mix = jnp.concatenate([coeffs, -nn(coeffs, theta)], axis=0).T
 
+    image_at = neighbour_rows(index_ref, own_ref, up_ref, down_ref, columns)
+
     def values(slot):
-        parts = (applied_slots_ref, image_slots_ref, block_slots_ref, residual_slots_ref)
-        return nn(mix, jnp.concatenate([ref[slot] for ref in parts], axis=0))
+        parts = [
+            applied_slots_ref[slot],
+            image_at(slot),
+            block_slots_ref[slot],
+            residual_slots_ref[slot],
+        ]
+        return nn(mix, jnp.concatenate(parts, axis=0))
 
     image = multiply_tiles(weight_ref, tiles_ref, values)
     block, applied = block_ref[...], applied_ref[...]
@@ -452,18 +460,12 @@
     node_index = ids % nodes
     chips = nodes // 2
     chip_offset = (node_index // 2 - here // 2 + 1 + chips) % chips
-    core = here % 2
-    member = node_index % 2 + 2 * group_index
-    half = 2 * groups // 2
-    fetched = jnp.where(member // half == core, 0, 4 * groups) + chip_offset // 2 * half + member % half
-    index = jnp.where(chip_offset == 1, 2 * groups + member, fetched)
-    index = jnp.clip(index, 0, 6 * groups - 1).astype(jnp.int32)
+    index = jnp.clip(chip_offset * 8 + node_index % 2 + 2 * group_index, 0, 23).astype(jnp.int32)
     slot_iota = jnp.arange(slots, dtype=jnp.int32)
     weights = jnp.where(slot_iota < live_counts[0], tile_scales[0], F32(0.0))
     tiles = weight_tiles[0]
     to_next = [(source, (source + 2) % nodes) for source in range(nodes)]
     to_last = [(source, (source - 2) % nodes) for source in range(nodes)]
-    to_pair = [(source, source ^ 1) for source in range(nodes)]
     root = float(rows_dev * groups * nodes) ** 0.5
     slab = (columns, rows_dev)
     square = (columns, columns)
@@ -475,33 +477,30 @@
         partial = sum_copies(received, 2 ** len(Y_Z), columns)
         shared = swap(partial, Y_Z)
         later, _ = lax.optimization_barrier((received, partial))
-        part = run(half_kernel, "half", [((half,) + slab, F32)], core[None], later, scalars=1)[0]
-        mine = jnp.concatenate(
-            [lax.ppermute(part, "node", to_next), lax.ppermute(part, "node", to_last)], axis=0
-        )
-        other = lax.ppermute(mine, "node", to_pair)
-        rows = run(pick_kernel, "pick_slots", [slab_slots], index, received, mine, other, scalars=1)[0]
+        down = lax.ppermute(later, "node", to_next)
+        up = lax.ppermute(later, "node", to_last)
         summed = swap(sum_copies(shared, 2 ** len(CORE_X)), CORE_X)
-        return rows, summed
+        return (received, up, down), summed
 
     def parcel_of(share):
         return ((2 * groups, columns + share, rows_dev), F32)
 
     small = parcel_of(columns // (4 * groups))
-    start_slots, gram = exchange(run(gram_kernel, "start_gram", [small], start_block)[0])
+    start_rows, gram = exchange(run(gram_kernel, "start_gram", [small], start_block)[0])
     block, block_slots, applied, parcel = run(
         start_kernel,
         "start_step",
         [(slab, F32), slab_slots, (slab, F32), small],
         weights,
+        index,
+        *start_rows,
         gram.reshape(packed),
         start_block,
-        start_slots,
         tiles,
-        scalars=1,
-    )
-    applied_slots, theta_sum = exchange(parcel)
-    theta, start_theta, residual, residual_slots, image, parcel, overlap = run(
+        scalars=2,
+    )
+    applied_rows, theta_sum = exchange(parcel)
+    theta, start_theta, residual, residual_slots, image, parcel, overlap, applied_slots = run(
         lambda *refs: first_kernel(root, *refs),
         "first_residual",
         [
@@ -512,17 +511,19 @@
             (slab, F32),
             parcel_of(columns // (2 * groups) + 1),
             (square, F32),
+            slab_slots,
         ],
         weights,
+        index,
+        *applied_rows,
         theta_sum.reshape(packed),
         block,
         applied,
         block_slots,
-        applied_slots,
         tiles,
-        scalars=1,
-    )
-    image_slots, grams = exchange(parcel)
+        scalars=2,
+    )
+    image_rows, grams = exchange(parcel)
     coeffs, next_theta, trial, last_grams = run(
         second_kernel,
         "second_step",
@@ -533,6 +534,8 @@
             ((2 * columns, 3 * columns), F32),
         ],
         weights,
+        index,
+        *image_rows,
         grams,
         overlap,
         theta,
@@ -543,9 +546,8 @@
         block_slots,
         residual_slots,
         applied_slots,
-        image_slots,
         tiles,
-        scalars=1,
+        scalars=2,
         scratch=[pltpu.VMEM((2 * columns, columns), F32)],
     )
     carried, pieces = run(

time: 242 us -> 225 us (0.930)
  blocking collectives: 64.6 us -> 102 us
  starting transfers between devices: 88.4 us -> 59.5 us
  waiting for transfers between devices: 43.7 us -> 22.8 us
  Pallas kernels: 39.5 us -> 34.8 us
    all_to_all x2 -> x5, blocking collectives: 21 us -> 63.5 us  [swap(): lax.all_to_all(values, BOTH, split_axis=0, concat_axis=0, tiled=True, axi...]
    all_to_all x7 -> x4, starting transfers between devices: 46 us -> 30.5 us  [swap(): lax.all_to_all(values, BOTH, split_axis=0, concat_axis=0, tiled=True, axi...]
    ppermute x9 -> x6, starting transfers between devices: 39.2 us -> 25.8 us  [the longest x3 18 us: exchange(): up = lax.ppermute(later, 'node', to_last)]
    all_to_all x7 -> x4, waiting for transfers between devices: 33 us -> 20.3 us  [swap(): lax.all_to_all(values, BOTH, split_axis=0, concat_axis=0, tiled=True, axi...]
    ppermute x9 -> x6, waiting for transfers between devices: 8.17 us -> 0.02 us  [the longest x3 0.01 us: exchange(): down = lax.ppermute(later, 'node', to_next)]
    all_to_all x2, blocking collectives: 43.6 us -> 38.7 us  [over(): return lax.all_to_all(values, axis, split_axis=0, concat_axis=0, tiled=True)]
    pallas_call x20 -> x14, Pallas kernels: 39.5 us -> 34.8 us  [run(): pl.pallas_call(kernel, out_shape=[jax.ShapeDtypeStruct(shape, dtype) for...]
  transfers between devices with their start and end apart: 17 -> 11, of which waited for: 8 -> 5; matrix products, arithmetic and copies ran while one was open for 0% -> 0% of each run, Pallas kernels for 2% -> 1%
where the time goes in v6:
time: 225 us; the launch traced here: 224 us
  blocking collectives  102 us (45%)
  starting transfers between devices  59.5 us (26%)
  Pallas kernels  34.8 us (15%)
  waiting for transfers between devices  22.8 us (10%)
  local copies, waits for them, and re-layouts  3.04 us (1%)
    all_to_all x5, blocking collectives, swap(): lax.all_to_all(values, BOTH, split_axis=0, concat_axis=0, tiled=True, axi...  63.5 us
    all_to_all x2, blocking collectives, over(): return lax.all_to_all(values, axis, split_axis=0, concat_axis=0, tiled=True)  38.7 us
    pallas_call x14, Pallas kernels, run(): pl.pallas_call(kernel, out_shape=[jax.ShapeDtypeStruct(shape, dtype) for...  34.8 us
    all_to_all x4, starting transfers between devices, swap(): lax.all_to_all(values, BOTH, split_axis=0, concat_axis=0, tiled=True, axi...  30.5 us
    all_to_all x4, waiting for transfers between devices, swap(): lax.all_to_all(values, BOTH, split_axis=0, concat_axis=0, tiled=True, axi...  20.3 us
    ppermute x3, starting transfers between devices, exchange(): up = lax.ppermute(later, 'node', to_last)  18 us
    ppermute x3, starting transfers between devices, exchange(): down = lax.ppermute(later, 'node', to_next)  7.8 us
  transfers between devices with their start and end apart: 11, of which 5 were waited for; matrix products, arithmetic and copies ran while one was open for 0% of the time, Pallas kernels for 1%

profile of v6, /device:TPU:1, one launch (start us, length us, event | category | flops | bytes accessed | tf_op | source)
XLA Modules:
  0.0 223.9 jit_solution(13476070950850146088)
XLA Ops:
  0.6 0.7 copy-done.1
  1.6 16.6 %all_to_all.78.refs_0_.own_ref = f32[8,68,128]{2,1,0:T(8,128)S(1)} all-to-all(f32[8,68,128]{2,1,0:T(8,128)S(1)} %start_gram.1), channel_id=1, replica_groups={{0,1,128,129,256,257,384,385},{2,3,130,131,258,259,386,387},{4,5,132,13..., dimensions={0} | all-to-all | bytes 557056 | tf_op jit(solution)/shard_map/all_to_all | solution.py:31
  18.2 0.7 sum_copies.6
  18.9 12.7 %all-to-all-start.1 = ((f32[64,4,128]{2,1,0:T(4,128)}), f32[64,4,128]{2,1,0:T(4,128)S(1)}, u32[]{:S(2)}, u32[]{:S(2)}) async-start(f32[64,4,128]{2,1,0:T(4,128)} %sum_copies.6), calls=%async_computation.1 | async-start | bytes 262144 | tf_op jit(solution)/shard_map/all_to_all | solution.py:31
  31.6 2.9 %collective-permute-start.1 = (f32[8,68,128]{2,1,0:T(8,128)S(1)}, f32[8,68,128]{2,1,0:T(8,128)S(1)}, u32[]{:S(2)}, u32[]{:S(2)}) collective-permute-start(f32[8,68,128]{2,1,0:T(8,128)S(1)} %all_to_all.78.refs_0_.own_ref), channel_id=1, source_target_pairs={{0,2},{1,3},{2,4},{3,5},{4,6},{5,7},{6,8},{7,9},{8,10},{9,11},{10,... | collective-permute-start | bytes 835592 | tf_op jit(solution)/shard_map/ppermute | solution.py:480
  34.5 5.7 %collective-permute-start = (f32[8,68,128]{2,1,0:T(8,128)S(1)}, f32[8,68,128]{2,1,0:T(8,128)S(1)}, u32[]{:S(2)}, u32[]{:S(2)}) collective-permute-start(f32[8,68,128]{2,1,0:T(8,128)S(1)} %all_to_all.78.refs_0_.own_ref), channel_id=1, source_target_pairs={{0,126},{1,127},{2,0},{3,1},{4,2},{5,3},{6,4},{7,5},{8,6},{9,7},{1... | collective-permute-start | bytes 835592 | tf_op jit(solution)/shard_map/ppermute | solution.py:481
  40.9 2.7 %all-to-all-done.1.refs_0_ = f32[64,4,128]{2,1,0:T(4,128)S(1)} async-done(((f32[64,4,128]{2,1,0:T(4,128)}), f32[64,4,128]{2,1,0:T(4,128)S(1)}, u32[]{:S(2)}, u32[]{:S(2)}) %all-to-all-start.1) | async-done | bytes 131104 | tf_op jit(solution)/shard_map/all_to_all | solution.py:31
  44.3 5.3 %all-to-all-start.2 = ((f32[8,4,128]{2,1,0:T(4,128)}), f32[8,4,128]{2,1,0:T(4,128)S(1)}, u32[]{:S(2)}, u32[]{:S(2)}) async-start(f32[8,4,128]{2,1,0:T(4,128)} %sum_copies.7), calls=%async_computation.2 | async-start | bytes 32768 | tf_op jit(solution)/shard_map/all_to_all | solution.py:31
  50.3 4.0 %all-to-all-done.2 = f32[8,4,128]{2,1,0:T(4,128)S(1)} async-done(((f32[8,4,128]{2,1,0:T(4,128)}), f32[8,4,128]{2,1,0:T(4,128)S(1)}, u32[]{:S(2)}, u32[]{:S(2)}) %all-to-all-start.2) | async-done | bytes 16416 | tf_op jit(solution)/shard_map/all_to_all | solution.py:31
  54.3 4.6 %start_step.1 = (f32[64,128]{1,0:T(8,128)S(1)}, f32[12,64,128]{2,1,0:T(8,128)S(1)}, f32[64,128]{1,0:T(8,128)S(1)}, f32[8,68,128]{2,1,0:T(8,128)S(1)}) custom-call(f32[12]{0:T(128)S(1)} %compare_select_fusion.2.weight_ref.refs_0_, s32[12]{0:T(128)S(1)} %fusion.4.index_ref.refs_1_, f32[8,68,128]{2,1,0:T(8,128)S(1)} %all_to_all.78.refs_0_.own_ref, ...), custom_call_target="tpu_custom_call" | custom-call | tf_op jit(solution)/shard_map/start_step/pallas_call | solution.py:39
  58.9 10.5 %all_to_all.79.refs_0_.refs_2_ = f32[8,68,128]{2,1,0:T(8,128)S(1)} all-to-all(f32[8,68,128]{2,1,0:T(8,128)S(1)} %get-tuple-element.27), channel_id=1, replica_groups={{0,1,128,129,256,257,384,385},{2,3,130,131,258,259,386,387},{4,5,132,13..., dimensions={0} | all-to-all | bytes 557056 | tf_op jit(solution)/shard_map/all_to_all | solution.py:31
  69.3 2.1 collective-permute-start.3
  71.4 6.5 %collective-permute-start.2 = (f32[8,68,128]{2,1,0:T(8,128)S(1)}, f32[8,68,128]{2,1,0:T(8,128)S(1)}, u32[]{:S(2)}, u32[]{:S(2)}) collective-permute-start(f32[8,68,128]{2,1,0:T(8,128)S(1)} %all_to_all.79.refs_0_.refs_2_), channel_id=1, source_target_pairs={{0,126},{1,127},{2,0},{3,1},{4,2},{5,3},{6,4},{7,5},{8,6},{9,7},{1... | collective-permute-start | bytes 835592 | tf_op jit(solution)/shard_map/ppermute | solution.py:481
  78.0 16.3 %all_to_all.80.refs_0_ = f32[64,4,128]{2,1,0:T(4,128)S(1)} all-to-all(f32[64,4,128]{2,1,0:T(4,128)S(1)} %sum_copies.8), channel_id=1, replica_groups={{0,2,4,6,8,10,12,14,16,18,20,22,24,26,28,30,32,34,36,38,40,42,44,46,48,..., dimensions={0} | all-to-all | bytes 262144 | tf_op jit(solution)/shard_map/all_to_all | solution.py:31
  94.2 9.6 %all_to_all.81 = f32[8,4,128]{2,1,0:T(4,128)S(1)} all-to-all(f32[8,4,128]{2,1,0:T(4,128)S(1)} %sum_copies.9), channel_id=1, replica_groups={{0,1,128,129,256,257,384,385},{2,3,130,131,258,259,386,387},{4,5,132,13..., dimensions={0} | all-to-all | bytes 32768 | tf_op jit(solution)/shard_map/all_to_all | solution.py:31
  103.9 3.2 %first_residual.1 = (f32[64,64]{1,0:T(8,128)S(1)}, f32[64,64]{1,0:T(8,128)}, f32[64,128]{1,0:T(8,128)S(1)}, f32[12,64,128]{2,1,0:T(8,128)S(1)}, f32[64,128]{1,0:...) custom-call(f32[12]{0:T(128)S(1)} %compare_select_fusion.2.weight_ref.refs_0_, ...), custom_call_target="tpu_custom_call" | custom-call | tf_op jit(solution)/shard_map/first_residual/pallas_call | solution.py:39
  107.0 10.6 %all_to_all.82.refs_0_.own_ref = f32[8,73,128]{2,1,0:T(8,128)S(1)} all-to-all(f32[8,73,128]{2,1,0:T(8,128)S(1)} %get-tuple-element.32), channel_id=1, replica_groups={{0,1,128,129,256,257,384,385},{2,3,130,131,258,259,386,387},{4,5,132,13..., dimensions={0} | all-to-all | bytes 598016 | tf_op jit(solution)/shard_map/all_to_all | solution.py:31
  117.6 0.8 sum_copies.10
  118.4 4.6 %all-to-all-start.7 = ((f32[64,9,128]{2,1,0:T(8,128)}), f32[64,9,128]{2,1,0:T(8,128)S(1)}, u32[]{:S(2)}, u32[]{:S(2)}) async-start(f32[64,9,128]{2,1,0:T(8,128)} %sum_copies.10), calls=%async_computation.7 | async-start | bytes 1048576 | tf_op jit(solution)/shard_map/all_to_all | solution.py:31
  123.1 2.8 %collective-permute-start.5 = (f32[8,73,128]{2,1,0:T(8,128)S(1)}, f32[8,73,128]{2,1,0:T(8,128)S(1)}, u32[]{:S(2)}, u32[]{:S(2)}) collective-permute-start(f32[8,73,128]{2,1,0:T(8,128)S(1)} %all_to_all.82.refs_0_.own_ref), channel_id=1, source_target_pairs={{0,2},{1,3},{2,4},{3,5},{4,6},{5,7},{6,8},{7,9},{8,10},{9,11},{10,... | collective-permute-start | bytes 897032 | tf_op jit(solution)/shard_map/ppermute | solution.py:480
  125.9 5.8 %collective-permute-start.4 = (f32[8,73,128]{2,1,0:T(8,128)S(1)}, f32[8,73,128]{2,1,0:T(8,128)S(1)}, u32[]{:S(2)}, u32[]{:S(2)}) collective-permute-start(f32[8,73,128]{2,1,0:T(8,128)S(1)} %all_to_all.82.refs_0_.own_ref), channel_id=1, source_target_pairs={{0,126},{1,127},{2,0},{3,1},{4,2},{5,3},{6,4},{7,5},{8,6},{9,7},{1... | collective-permute-start | bytes 897032 | tf_op jit(solution)/shard_map/ppermute | solution.py:481
  131.7 8.7 %all-to-all-done.7.refs_0_ = f32[64,9,128]{2,1,0:T(8,128)S(1)} async-done(((f32[64,9,128]{2,1,0:T(8,128)}), f32[64,9,128]{2,1,0:T(8,128)S(1)}, u32[]{:S(2)}, u32[]{:S(2)}) %all-to-all-start.7) | async-done | bytes 294944 | tf_op jit(solution)/shard_map/all_to_all | solution.py:31
  140.4 0.7 sum_copies.11
  141.1 7.9 %all-to-all-start.8 = ((f32[8,9,128]{2,1,0:T(8,128)}), f32[8,9,128]{2,1,0:T(8,128)S(1)}, u32[]{:S(2)}, u32[]{:S(2)}) async-start(f32[8,9,128]{2,1,0:T(8,128)} %sum_copies.11), calls=%async_computation.8 | async-start | bytes 131072 | tf_op jit(solution)/shard_map/all_to_all | solution.py:31
  148.9 4.9 %all-to-all-done.8.grams_ref = f32[8,9,128]{2,1,0:T(8,128)S(1)} async-done(((f32[8,9,128]{2,1,0:T(8,128)}), f32[8,9,128]{2,1,0:T(8,128)S(1)}, u32[]{:S(2)}, u32[]{:S(2)}) %all-to-all-start.8) | async-done | bytes 36896 | tf_op jit(solution)/shard_map/all_to_all | solution.py:31
  153.8 10.8 %second_step.1 = (f32[128,128]{1,0:T(8,128)S(1)}, f32[64,64]{1,0:T(8,128)S(1)}, f32[192,128]{1,0:T(8,128)S(1)}, f32[128,192]{1,0:T(8,128)S(1)}) custom-call(f32[12]{0:T(128)S(1)} %compare_select_fusion.2.weight_ref.refs_0_, s32[12]{0:T(128)S(1)} %fusion.4.index_ref.refs_1_, f32[8,73,128]{2,1,0:T(8,128)S(1)} %all_to_all.82.refs_0_.own_ref, ...), custom_call_target="tpu_custom_call" | custom-call | tf_op jit(solution)/shard_map/second_step/pallas_call | solution.py:39
  164.7 18.4 %all_to_all.83 = f32[128,1,192]{2,1,0:T(1,128)S(1)} all-to-all(f32[128,1,192]{2,1,0:T(1,128)S(1)} %copy.12), channel_id=1, replica_groups=mesh['grp'=4,'node'=128] {'node'}, dimensions={0} | all-to-all | bytes 196608 | tf_op jit(solution)/shard_map/all_to_all | solution.py:566
  183.7 3.2 %all-to-all-start.10 = ((f32[4,1,192]{2,1,0:T(1,128)}), f32[4,1,192]{2,1,0:T(1,128)S(1)}, u32[]{:S(2)}, u32[]{:S(2)}) async-start(f32[4,1,192]{2,1,0:T(1,128)} %copy.15), calls=%async_computation.10 | async-start | bytes 8192 | tf_op jit(solution)/shard_map/all_to_all | solution.py:566
  187.6 0.9 carry.1
  188.6 2.5 %all-to-all-done.10 = f32[4,1,192]{2,1,0:T(1,128)S(1)} async-done(((f32[4,1,192]{2,1,0:T(1,128)}), f32[4,1,192]{2,1,0:T(1,128)S(1)}, u32[]{:S(2)}, u32[]{:S(2)}) %all-to-all-start.10) | async-done | bytes 3104 | tf_op jit(solution)/shard_map/all_to_all | solution.py:566
  191.4 20.4 %all_to_all.84 = f32[128,1,384]{2,1,0:T(1,128)S(1)} all-to-all(f32[128,1,384]{2,1,0:T(1,128)S(1)} %copy.16), channel_id=1, replica_groups=mesh['grp'=4,'node'=128] {'node'}, dimensions={0} | all-to-all | bytes 393216 | tf_op jit(solution)/shard_map/all_to_all | solution.py:566
  211.8 12.1 %last_step.1 = (f32[64,64]{1,0:T(8,128)}, f32[64,128]{1,0:T(8,128)}) custom-call(f32[128,384]{1,0:T(8,128)S(1)} %bitcast.38, f32[256,128]{1,0:T(8,128)S(1)} %get-tuple-element.44.refs_1_, f32[64,64]{1,0:T(8,128)S(1)} %get-tuple-element.45.refs_2_), custom_call_target="tpu_custom_call" | custom-call | tf_op jit(solution)/shard_map/last_step/pallas_call | solution.py:39
  (31 shorter events, 3.4 us)
Async XLA Ops:
  0.6 0.8 copy-start.1
  18.2 36.1 %copy-start = (bf16[1,12,128,128]{3,2,1,0:T(8,128)(2,1)S(1)}, bf16[1,12,128,128]{3,2,1,0:T(8,128)(2,1)}, u32[]{:S(2)}) copy-start(bf16[1,12,128,128]{3,2,1,0:T(8,128)(2,1)} %param.7) | copy-start | bytes 1179652
  18.9 24.8 %all-to-all-start.1 = ((f32[64,4,128]{2,1,0:T(4,128)}), f32[64,4,128]{2,1,0:T(4,128)S(1)}, u32[]{:S(2)}, u32[]{:S(2)}) async-start(f32[64,4,128]{2,1,0:T(4,128)} %sum_copies.6), calls=%async_computation.1 | async-start | bytes 262144 | tf_op jit(solution)/shard_map/all_to_all | solution.py:31
  31.6 8.6 %copy-start.4 = (s32[1,12]{1,0:T(1,128)S(1)}, s32[1,12]{1,0:T(1,128)}, u32[]{:S(2)}) copy-start(s32[1,12]{1,0:T(1,128)} %param.9) | copy-start | bytes 148
  31.6 22.7 %collective-permute-start.1 = (f32[8,68,128]{2,1,0:T(8,128)S(1)}, f32[8,68,128]{2,1,0:T(8,128)S(1)}, u32[]{:S(2)}, u32[]{:S(2)}) collective-permute-start(f32[8,68,128]{2,1,0:T(8,128)S(1)} %all_to_all.78.refs_0_.own_ref), channel_id=1, source_target_pairs={{0,2},{1,3},{2,4},{3,5},{4,6},{5,7},{6,8},{7,9},{8,10},{9,11},{10,... | collective-permute-start | bytes 835592 | tf_op jit(solution)/shard_map/ppermute | solution.py:480
  34.5 19.8 %collective-permute-start = (f32[8,68,128]{2,1,0:T(8,128)S(1)}, f32[8,68,128]{2,1,0:T(8,128)S(1)}, u32[]{:S(2)}, u32[]{:S(2)}) collective-permute-start(f32[8,68,128]{2,1,0:T(8,128)S(1)} %all_to_all.78.refs_0_.own_ref), channel_id=1, source_target_pairs={{0,126},{1,127},{2,0},{3,1},{4,2},{5,3},{6,4},{7,5},{8,6},{9,7},{1... | collective-permute-start | bytes 835592 | tf_op jit(solution)/shard_map/ppermute | solution.py:481
  44.3 10.0 %copy-start.2 = (f32[64,128]{1,0:T(8,128)S(1)}, f32[64,128]{1,0:T(8,128)}, u32[]{:S(2)}) copy-start(f32[64,128]{1,0:T(8,128)} %start_ref.3) | copy-start | bytes 98308
  44.3 10.0 %all-to-all-start.2 = ((f32[8,4,128]{2,1,0:T(4,128)}), f32[8,4,128]{2,1,0:T(4,128)S(1)}, u32[]{:S(2)}, u32[]{:S(2)}) async-start(f32[8,4,128]{2,1,0:T(4,128)} %sum_copies.7), calls=%async_computation.2 | async-start | bytes 32768 | tf_op jit(solution)/shard_map/all_to_all | solution.py:31
  49.6 0.7 copy-start.5
  69.3 34.5 %collective-permute-start.3 = (f32[8,68,128]{2,1,0:T(8,128)S(1)}, f32[8,68,128]{2,1,0:T(8,128)S(1)}, u32[]{:S(2)}, u32[]{:S(2)}) collective-permute-start(f32[8,68,128]{2,1,0:T(8,128)S(1)} %all_to_all.79.refs_0_.refs_2_), channel_id=1, source_target_pairs={{0,2},{1,3},{2,4},{3,5},{4,6},{5,7},{6,8},{7,9},{8,10},{9,11},{10,... | collective-permute-start | bytes 835592 | tf_op jit(solution)/shard_map/ppermute | solution.py:480
  71.4 32.4 %collective-permute-start.2 = (f32[8,68,128]{2,1,0:T(8,128)S(1)}, f32[8,68,128]{2,1,0:T(8,128)S(1)}, u32[]{:S(2)}, u32[]{:S(2)}) collective-permute-start(f32[8,68,128]{2,1,0:T(8,128)S(1)} %all_to_all.79.refs_0_.refs_2_), channel_id=1, source_target_pairs={{0,126},{1,127},{2,0},{3,1},{4,2},{5,3},{6,4},{7,5},{8,6},{9,7},{1... | collective-permute-start | bytes 835592 | tf_op jit(solution)/shard_map/ppermute | solution.py:481
  118.4 22.0 %all-to-all-start.7 = ((f32[64,9,128]{2,1,0:T(8,128)}), f32[64,9,128]{2,1,0:T(8,128)S(1)}, u32[]{:S(2)}, u32[]{:S(2)}) async-start(f32[64,9,128]{2,1,0:T(8,128)} %sum_copies.10), calls=%async_computation.7 | async-start | bytes 1048576 | tf_op jit(solution)/shard_map/all_to_all | solution.py:31
  123.1 25.9 %collective-permute-start.5 = (f32[8,73,128]{2,1,0:T(8,128)S(1)}, f32[8,73,128]{2,1,0:T(8,128)S(1)}, u32[]{:S(2)}, u32[]{:S(2)}) collective-permute-start(f32[8,73,128]{2,1,0:T(8,128)S(1)} %all_to_all.82.refs_0_.own_ref), channel_id=1, source_target_pairs={{0,2},{1,3},{2,4},{3,5},{4,6},{5,7},{6,8},{7,9},{8,10},{9,11},{10,... | collective-permute-start | bytes 897032 | tf_op jit(solution)/shard_map/ppermute | solution.py:480
  125.9 23.0 %collective-permute-start.4 = (f32[8,73,128]{2,1,0:T(8,128)S(1)}, f32[8,73,128]{2,1,0:T(8,128)S(1)}, u32[]{:S(2)}, u32[]{:S(2)}) collective-permute-start(f32[8,73,128]{2,1,0:T(8,128)S(1)} %all_to_all.82.refs_0_.own_ref), channel_id=1, source_target_pairs={{0,126},{1,127},{2,0},{3,1},{4,2},{5,3},{6,4},{7,5},{8,6},{9,7},{1... | collective-permute-start | bytes 897032 | tf_op jit(solution)/shard_map/ppermute | solution.py:481
  141.1 12.7 %all-to-all-start.8 = ((f32[8,9,128]{2,1,0:T(8,128)}), f32[8,9,128]{2,1,0:T(8,128)S(1)}, u32[]{:S(2)}, u32[]{:S(2)}) async-start(f32[8,9,128]{2,1,0:T(8,128)} %sum_copies.11), calls=%async_computation.8 | async-start | bytes 131072 | tf_op jit(solution)/shard_map/all_to_all | solution.py:31
  183.7 7.4 %all-to-all-start.10 = ((f32[4,1,192]{2,1,0:T(1,128)}), f32[4,1,192]{2,1,0:T(1,128)S(1)}, u32[]{:S(2)}, u32[]{:S(2)}) async-start(f32[4,1,192]{2,1,0:T(1,128)} %copy.15), calls=%async_computation.10 | async-start | bytes 8192 | tf_op jit(solution)/shard_map/all_to_all | solution.py:566
  187.0 0.7 copy-start.3

commit v7 on v6

--- a/solution.py
+++ b/solution.py
@@ -209,9 +209,12 @@
     return coeffs, theta
 
 
-def load_packed(ref):
-    width = ref.shape[1] // 2
-    return jnp.concatenate([ref[:, :width], ref[:, width:]], axis=0)
+def load_square(gathered_ref):
+    width = gathered_ref.shape[2]
+    members = gathered_ref.shape[0]
+    share = width // 4 // members
+    packed = jnp.concatenate([gathered_ref[i, :share] for i in range(members)], axis=0)
+    return jnp.concatenate([packed[:, : width // 2], packed[:, width // 2 :]], axis=0)
 
 
 def store_parcel(ref, value, partial):
@@ -219,7 +222,9 @@
     share = partial.shape[0] // members
     for i in range(members):
         ref[i, :rows] = value
-        ref[i, rows:] = partial[share * i : share * (i + 1)]
+        ref[i, rows : rows + share] = partial[share * i : share * (i + 1)]
+        if ref.shape[1] > rows + share:
+            ref[i, rows + share :] = jnp.zeros((ref.shape[1] - rows - share, ref.shape[2]), F32)
 
 
 def pack(matrix):
@@ -232,13 +237,13 @@
     store_parcel(parcel_ref, start, pack(nt(start, start)))
 
 
-def neighbour_rows(index_ref, own_ref, up_ref, down_ref, rows):
+def neighbour_rows(index_ref, own_ref, other_ref, mine_ref, rows):
     count = own_ref.shape[0]
 
     def at(slot):
         side = lax.div(index_ref[slot], count)
         member = lax.rem(index_ref[slot], count)
-        outer = jnp.where(side == 0, down_ref[member, :rows], up_ref[member, :rows])
+        outer = jnp.where(side == 0, mine_ref[member, :rows], other_ref[member, :rows])
         return jnp.where(side == 1, own_ref[member, :rows], outer)
 
     return at
@@ -258,12 +263,12 @@
     return acc
 
 
-def start_kernel(weight_ref, index_ref, own_ref, up_ref, down_ref, gram_ref, start_ref, tiles_ref, block_ref, block_slots_ref, applied_ref, parcel_ref):
-    inverse = inverse_factor(load_packed(gram_ref))
+def start_kernel(weight_ref, index_ref, own_ref, other_ref, mine_ref, gram_ref, start_ref, tiles_ref, block_ref, block_slots_ref, applied_ref, parcel_ref):
+    inverse = inverse_factor(load_square(gram_ref))
     block = nn(inverse, start_ref[...])
     block_ref[...] = block
 
-    rows_at = neighbour_rows(index_ref, own_ref, up_ref, down_ref, block.shape[0])
+    rows_at = neighbour_rows(index_ref, own_ref, other_ref, mine_ref, block.shape[0])
 
     def values(slot):
         there = nn(inverse, rows_at(slot))
@@ -275,8 +280,8 @@
     store_parcel(parcel_ref, applied, pack(nt(block, applied)))
 
 
-def first_kernel(root, weight_ref, index_ref, own_ref, up_ref, down_ref, sum_ref, block_ref, applied_ref, block_slots_ref, tiles_ref, theta_ref, start_theta_ref, residual_ref, residual_slots_ref, image_ref, parcel_ref, overlap_ref, applied_slots_ref):
-    product = load_packed(sum_ref)
+def first_kernel(root, weight_ref, index_ref, own_ref, other_ref, mine_ref, sum_ref, block_ref, applied_ref, block_slots_ref, tiles_ref, theta_ref, start_theta_ref, residual_ref, residual_slots_ref, image_ref, parcel_ref, overlap_ref, applied_slots_ref):
+    product = load_square(sum_ref)
     theta = half_sum(product)
     overlap_ref[...] = product - theta
     theta_ref[...] = theta
@@ -286,7 +291,7 @@
     residual = applied - nn(theta, block)
     residual_ref[...] = residual
 
-    rows_at = neighbour_rows(index_ref, own_ref, up_ref, down_ref, block.shape[0])
+    rows_at = neighbour_rows(index_ref, own_ref, other_ref, mine_ref, block.shape[0])
 
     def values(slot):
         applied_there = rows_at(slot)
@@ -333,7 +338,7 @@
     return basis, gram
 
 
-def second_kernel(weight_ref, index_ref, own_ref, up_ref, down_ref, grams_ref, overlap_ref, theta_ref, block_ref, residual_ref, applied_ref, image_ref, block_slots_ref, residual_slots_ref, applied_slots_ref, tiles_ref, coeffs_ref, theta_out_ref, trial_ref, grams_out_ref, basis_ref):
+def second_kernel(weight_ref, index_ref, own_ref, other_ref, mine_ref, grams_ref, overlap_ref, theta_ref, block_ref, residual_ref, applied_ref, image_ref, block_slots_ref, residual_slots_ref, applied_slots_ref, tiles_ref, coeffs_ref, theta_out_ref, trial_ref, grams_out_ref, basis_ref):
     columns = theta_ref.shape[0]
     width = block_ref.shape[1]
     overlap = overlap_ref[...]
@@ -353,7 +358,7 @@
     coeffs_ref[...] = both
     mix = jnp.concatenate([coeffs, -nn(coeffs, theta)], axis=0).T
 
-    image_at = neighbour_rows(index_ref, own_ref, up_ref, down_ref, columns)
+    image_at = neighbour_rows(index_ref, own_ref, other_ref, mine_ref, columns)
 
     def values(slot):
         parts = [
@@ -460,16 +465,18 @@
     node_index = ids % nodes
     chips = nodes // 2
     chip_offset = (node_index // 2 - here // 2 + 1 + chips) % chips
-    index = jnp.clip(chip_offset * 8 + node_index % 2 + 2 * group_index, 0, 23).astype(jnp.int32)
+    fetched = jnp.where(chip_offset // 2 == here % 2, 0, 2)
+    side = jnp.where(chip_offset == 1, 1, fetched)
+    index = side * (2 * groups) + node_index % 2 + 2 * group_index
+    index = jnp.clip(index, 0, 6 * groups - 1).astype(jnp.int32)
     slot_iota = jnp.arange(slots, dtype=jnp.int32)
     weights = jnp.where(slot_iota < live_counts[0], tile_scales[0], F32(0.0))
     tiles = weight_tiles[0]
-    to_next = [(source, (source + 2) % nodes) for source in range(nodes)]
-    to_last = [(source, (source - 2) % nodes) for source in range(nodes)]
+    outward = [(source, (source + 2 - 4 * (source % 2)) % nodes) for source in range(nodes)]
+    to_pair = [(source, source ^ 1) for source in range(nodes)]
     root = float(rows_dev * groups * nodes) ** 0.5
     slab = (columns, rows_dev)
     square = (columns, columns)
-    packed = (columns // 2, 2 * columns)
     slab_slots = ((slots,) + slab, F32)
 
     def exchange(parcel):
@@ -477,24 +484,25 @@
         partial = sum_copies(received, 2 ** len(Y_Z), columns)
         shared = swap(partial, Y_Z)
         later, _ = lax.optimization_barrier((received, partial))
-        down = lax.ppermute(later, "node", to_next)
-        up = lax.ppermute(later, "node", to_last)
+        mine = lax.ppermute(later, "node", outward)
+        other = lax.ppermute(mine, "node", to_pair)
         summed = swap(sum_copies(shared, 2 ** len(CORE_X)), CORE_X)
-        return (received, up, down), summed
+        return (received, other, mine), summed
 
     def parcel_of(share):
         return ((2 * groups, columns + share, rows_dev), F32)
 
     small = parcel_of(columns // (4 * groups))
+    large = parcel_of(columns // (2 * groups) + 1)
     start_rows, gram = exchange(run(gram_kernel, "start_gram", [small], start_block)[0])
     block, block_slots, applied, parcel = run(
         start_kernel,
         "start_step",
-        [(slab, F32), slab_slots, (slab, F32), small],
+        [(slab, F32), slab_slots, (slab, F32), large],
         weights,
         index,
         *start_rows,
-        gram.reshape(packed),
+        gram,
         start_block,
         tiles,
         scalars=2,
@@ -509,14 +517,14 @@
             (slab, F32),
             slab_slots,
             (slab, F32),
-            parcel_of(columns // (2 * groups) + 1),
+            large,
             (square, F32),
             slab_slots,
         ],
         weights,
         index,
         *applied_rows,
-        theta_sum.reshape(packed),
+        theta_sum,
         block,
         applied,
         block_slots,

time: 225 us -> 237 us (1.053)
  blocking collectives: 102 us -> 79 us
  waiting for transfers between devices: 22.8 us -> 44.7 us
  starting transfers between devices: 59.5 us -> 72.4 us
    all_to_all x5 -> x3, blocking collectives: 63.5 us -> 37.8 us  [swap(): lax.all_to_all(values, BOTH, split_axis=0, concat_axis=0, tiled=True, axi...]
    ppermute x6, waiting for transfers between devices: 0.02 us -> 20.5 us  [the longest x3 20.5 us: exchange(): mine = lax.ppermute(later, 'node', outward)]
    ppermute x6, starting transfers between devices: 25.8 us -> 40.1 us  [the longest x3 23 us: exchange(): mine = lax.ppermute(later, 'node', outward)]
    all_to_all x2, blocking collectives: 38.7 us -> 41.1 us  [over(): return lax.all_to_all(values, axis, split_axis=0, concat_axis=0, tiled=True)]
    all_to_all x4 -> x6, waiting for transfers between devices: 20.3 us -> 21.8 us  [swap(): lax.all_to_all(values, BOTH, split_axis=0, concat_axis=0, tiled=True, axi...]
    all_to_all x4 -> x6, starting transfers between devices: 30.5 us -> 29.1 us  [swap(): lax.all_to_all(values, BOTH, split_axis=0, concat_axis=0, tiled=True, axi...]
  transfers between devices with their start and end apart: 11 -> 13, of which waited for: 5 -> 7; matrix products, arithmetic and copies ran while one was open for 0% -> 0% of each run, Pallas kernels for 1% -> 1%
where the time goes in v7:
time: 237 us; the launch traced here: 236 us
  blocking collectives  79 us (33%)
  starting transfers between devices  72.4 us (31%)
  waiting for transfers between devices  44.7 us (19%)
  Pallas kernels  36.3 us (15%)
  local copies, waits for them, and re-layouts  2.39 us (1%)
    all_to_all x2, blocking collectives, over(): return lax.all_to_all(values, axis, split_axis=0, concat_axis=0, tiled=True)  41.1 us
    all_to_all x3, blocking collectives, swap(): lax.all_to_all(values, BOTH, split_axis=0, concat_axis=0, tiled=True, axi...  37.8 us
    pallas_call x14, Pallas kernels, run(): pl.pallas_call(kernel, out_shape=[jax.ShapeDtypeStruct(shape, dtype) for...  36.3 us
    all_to_all x6, starting transfers between devices, swap(): lax.all_to_all(values, BOTH, split_axis=0, concat_axis=0, tiled=True, axi...  29.1 us
    ppermute x3, starting transfers between devices, exchange(): mine = lax.ppermute(later, 'node', outward)  23 us
    all_to_all x6, waiting for transfers between devices, swap(): lax.all_to_all(values, BOTH, split_axis=0, concat_axis=0, tiled=True, axi...  21.8 us
    ppermute x3, waiting for transfers between devices, exchange(): mine = lax.ppermute(later, 'node', outward)  20.5 us
    ppermute x3, starting transfers between devices, exchange(): other = lax.ppermute(mine, 'node', to_pair)  17.1 us
  transfers between devices with their start and end apart: 13, of which 7 were waited for; matrix products, arithmetic and copies ran while one was open for 0% of the time, Pallas kernels for 1%

profile of v7, /device:TPU:1, one launch (start us, length us, event | category | flops | bytes accessed | tf_op | source)
XLA Modules:
  0.0 236.3 jit_solution(778804335810411960)
XLA Ops:
  1.6 16.6 %all_to_all.78.refs_0_.own_ref = f32[8,68,128]{2,1,0:T(8,128)S(1)} all-to-all(f32[8,68,128]{2,1,0:T(8,128)S(1)} %start_gram.1), channel_id=1, replica_groups={{0,1,128,129,256,257,384,385},{2,3,130,131,258,259,386,387},{4,5,132,13..., dimensions={0} | all-to-all | bytes 557056 | tf_op jit(solution)/shard_map/all_to_all | solution.py:31
  18.9 9.9 %collective-permute-start = (f32[8,68,128]{2,1,0:T(8,128)S(1)}, f32[8,68,128]{2,1,0:T(8,128)S(1)}, u32[]{:S(2)}, u32[]{:S(2)}) collective-permute-start(f32[8,68,128]{2,1,0:T(8,128)S(1)} %all_to_all.78.refs_0_.own_ref), channel_id=1, source_target_pairs={{0,2},{1,127},{2,4},{3,1},{4,6},{5,3},{6,8},{7,5},{8,10},{9,7},{10... | collective-permute-start | bytes 835592 | tf_op jit(solution)/shard_map/ppermute | solution.py:487
  28.8 4.9 %all-to-all-start.1 = ((f32[64,4,128]{2,1,0:T(4,128)}), f32[64,4,128]{2,1,0:T(4,128)S(1)}, u32[]{:S(2)}, u32[]{:S(2)}) async-start(f32[64,4,128]{2,1,0:T(4,128)} %sum_copies.6), calls=%async_computation.1 | async-start | bytes 262144 | tf_op jit(solution)/shard_map/all_to_all | solution.py:31
  34.4 3.2 %collective-permute-start.1 = (f32[8,68,128]{2,1,0:T(8,128)S(1)}, f32[8,68,128]{2,1,0:T(8,128)S(1)}, u32[]{:S(2)}, u32[]{:S(2)}) collective-permute-start(f32[8,68,128]{2,1,0:T(8,128)S(1)} %collective-permute-done.mine_ref), channel_id=1, source_target_pairs={{0,1},{1,0},{2,3},{3,2},{4,5},{5,4},{6,7},{7,6},{8,9},{9,8},{10,11... | collective-permute-start | bytes 835592 | tf_op jit(solution)/shard_map/ppermute | solution.py:488
  37.6 7.7 %all-to-all-done.1.refs_0_ = f32[64,4,128]{2,1,0:T(4,128)S(1)} async-done(((f32[64,4,128]{2,1,0:T(4,128)}), f32[64,4,128]{2,1,0:T(4,128)S(1)}, u32[]{:S(2)}, u32[]{:S(2)}) %all-to-all-start.1) | async-done | bytes 131104 | tf_op jit(solution)/shard_map/all_to_all | solution.py:31
  45.9 5.8 %all-to-all-start.2 = ((f32[8,4,128]{2,1,0:T(4,128)}), f32[8,4,128]{2,1,0:T(4,128)S(1)}, u32[]{:S(2)}, u32[]{:S(2)}) async-start(f32[8,4,128]{2,1,0:T(4,128)} %sum_copies.7), calls=%async_computation.2 | async-start | bytes 32768 | tf_op jit(solution)/shard_map/all_to_all | solution.py:31
  51.8 4.6 %all-to-all-done.2.gram_ref = f32[8,4,128]{2,1,0:T(4,128)S(1)} async-done(((f32[8,4,128]{2,1,0:T(4,128)}), f32[8,4,128]{2,1,0:T(4,128)S(1)}, u32[]{:S(2)}, u32[]{:S(2)}) %all-to-all-start.2) | async-done | bytes 16416 | tf_op jit(solution)/shard_map/all_to_all | solution.py:31
  56.4 4.6 %start_step.1 = (f32[64,128]{1,0:T(8,128)S(1)}, f32[12,64,128]{2,1,0:T(8,128)S(1)}, f32[64,128]{1,0:T(8,128)S(1)}, f32[8,73,128]{2,1,0:T(8,128)S(1)}) custom-call(f32[12]{0:T(128)S(1)} %compare_select_fusion.4.weight_ref.refs_0_, s32[12]{0:T(128)S(1)} %fusion.4.index_ref.refs_1_, f32[8,68,128]{2,1,0:T(8,128)S(1)} %all_to_all.78.refs_0_.own_ref, ...), custom_call_target="tpu_custom_call" | custom-call | tf_op jit(solution)/shard_map/start_step/pallas_call | solution.py:39
  61.0 10.6 %all_to_all.79.refs_0_.refs_2_ = f32[8,73,128]{2,1,0:T(8,128)S(1)} all-to-all(f32[8,73,128]{2,1,0:T(8,128)S(1)} %get-tuple-element.27), channel_id=1, replica_groups={{0,1,128,129,256,257,384,385},{2,3,130,131,258,259,386,387},{4,5,132,13..., dimensions={0} | all-to-all | bytes 598016 | tf_op jit(solution)/shard_map/all_to_all | solution.py:31
  71.6 0.9 sum_copies.8
  72.5 4.6 %all-to-all-start.4 = ((f32[64,9,128]{2,1,0:T(8,128)}), f32[64,9,128]{2,1,0:T(8,128)S(1)}, u32[]{:S(2)}, u32[]{:S(2)}) async-start(f32[64,9,128]{2,1,0:T(8,128)} %sum_copies.8), calls=%async_computation.4 | async-start | bytes 1048576 | tf_op jit(solution)/shard_map/all_to_all | solution.py:31
  77.1 6.6 %collective-permute-start.2 = (f32[8,73,128]{2,1,0:T(8,128)S(1)}, f32[8,73,128]{2,1,0:T(8,128)S(1)}, u32[]{:S(2)}, u32[]{:S(2)}) collective-permute-start(f32[8,73,128]{2,1,0:T(8,128)S(1)} %all_to_all.79.refs_0_.refs_2_), channel_id=1, source_target_pairs={{0,2},{1,127},{2,4},{3,1},{4,6},{5,3},{6,8},{7,5},{8,10},{9,7},{10... | collective-permute-start | bytes 897032 | tf_op jit(solution)/shard_map/ppermute | solution.py:487
  83.7 10.2 %collective-permute-done.2.refs_4_ = f32[8,73,128]{2,1,0:T(8,128)S(1)} collective-permute-done((f32[8,73,128]{2,1,0:T(8,128)S(1)}, f32[8,73,128]{2,1,0:T(8,128)S(1)}, u32[]{:S(2)}, u32[]{:S(2)}) %collective-permute-start.2) | collective-permute-done | bytes 299040 | tf_op jit(solution)/shard_map/ppermute | solution.py:487
  93.9 7.0 %collective-permute-start.3 = (f32[8,73,128]{2,1,0:T(8,128)S(1)}, f32[8,73,128]{2,1,0:T(8,128)S(1)}, u32[]{:S(2)}, u32[]{:S(2)}) collective-permute-start(f32[8,73,128]{2,1,0:T(8,128)S(1)} %collective-permute-done.2.refs_4_), channel_id=1, source_target_pairs={{0,1},{1,0},{2,3},{3,2},{4,5},{5,4},{6,7},{7,6},{8,9},{9,8},{10,11... | collective-permute-start | bytes 897032 | tf_op jit(solution)/shard_map/ppermute | solution.py:488
  101.5 3.3 %all-to-all-start.5 = ((f32[8,9,128]{2,1,0:T(8,128)}), f32[8,9,128]{2,1,0:T(8,128)S(1)}, u32[]{:S(2)}, u32[]{:S(2)}) async-start(f32[8,9,128]{2,1,0:T(8,128)} %sum_copies.9), calls=%async_computation.5 | async-start | bytes 131072 | tf_op jit(solution)/shard_map/all_to_all | solution.py:31
  104.8 4.8 %all-to-all-done.5.refs_5_ = f32[8,9,128]{2,1,0:T(8,128)S(1)} async-done(((f32[8,9,128]{2,1,0:T(8,128)}), f32[8,9,128]{2,1,0:T(8,128)S(1)}, u32[]{:S(2)}, u32[]{:S(2)}) %all-to-all-start.5) | async-done | bytes 36896 | tf_op jit(solution)/shard_map/all_to_all | solution.py:31
  109.7 3.2 %first_residual.1 = (f32[64,64]{1,0:T(8,128)S(1)}, f32[64,64]{1,0:T(8,128)}, f32[64,128]{1,0:T(8,128)S(1)}, f32[12,64,128]{2,1,0:T(8,128)S(1)}, f32[64,128]{1,0:...) custom-call(f32[12]{0:T(128)S(1)} %compare_select_fusion.4.weight_ref.refs_0_, ...), custom_call_target="tpu_custom_call" | custom-call | tf_op jit(solution)/shard_map/first_residual/pallas_call | solution.py:39
  112.8 10.6 %all_to_all.80.refs_0_.own_ref = f32[8,73,128]{2,1,0:T(8,128)S(1)} all-to-all(f32[8,73,128]{2,1,0:T(8,128)S(1)} %get-tuple-element.32), channel_id=1, replica_groups={{0,1,128,129,256,257,384,385},{2,3,130,131,258,259,386,387},{4,5,132,13..., dimensions={0} | all-to-all | bytes 598016 | tf_op jit(solution)/shard_map/all_to_all | solution.py:31
  123.5 0.9 sum_copies.10
  124.3 6.9 %all-to-all-start.7 = ((f32[64,9,128]{2,1,0:T(8,128)}), f32[64,9,128]{2,1,0:T(8,128)S(1)}, u32[]{:S(2)}, u32[]{:S(2)}) async-start(f32[64,9,128]{2,1,0:T(8,128)} %sum_copies.10), calls=%async_computation.7 | async-start | bytes 1048576 | tf_op jit(solution)/shard_map/all_to_all | solution.py:31
  131.2 6.6 %collective-permute-start.4 = (f32[8,73,128]{2,1,0:T(8,128)S(1)}, f32[8,73,128]{2,1,0:T(8,128)S(1)}, u32[]{:S(2)}, u32[]{:S(2)}) collective-permute-start(f32[8,73,128]{2,1,0:T(8,128)S(1)} %all_to_all.80.refs_0_.own_ref), channel_id=1, source_target_pairs={{0,2},{1,127},{2,4},{3,1},{4,6},{5,3},{6,8},{7,5},{8,10},{9,7},{10... | collective-permute-start | bytes 897032 | tf_op jit(solution)/shard_map/ppermute | solution.py:487
  137.8 10.3 %collective-permute-done.4.mine_ref = f32[8,73,128]{2,1,0:T(8,128)S(1)} collective-permute-done((f32[8,73,128]{2,1,0:T(8,128)S(1)}, f32[8,73,128]{2,1,0:T(8,128)S(1)}, u32[]{:S(2)}, u32[]{:S(2)}) %collective-permute-start.4) | collective-permute-done | bytes 299040 | tf_op jit(solution)/shard_map/ppermute | solution.py:487
  148.1 6.9 %collective-permute-start.5 = (f32[8,73,128]{2,1,0:T(8,128)S(1)}, f32[8,73,128]{2,1,0:T(8,128)S(1)}, u32[]{:S(2)}, u32[]{:S(2)}) collective-permute-start(f32[8,73,128]{2,1,0:T(8,128)S(1)} %collective-permute-done.4.mine_ref), channel_id=1, source_target_pairs={{0,1},{1,0},{2,3},{3,2},{4,5},{5,4},{6,7},{7,6},{8,9},{9,8},{10,11... | collective-permute-start | bytes 897032 | tf_op jit(solution)/shard_map/ppermute | solution.py:488
  155.7 3.5 %all-to-all-start.8 = ((f32[8,9,128]{2,1,0:T(8,128)}), f32[8,9,128]{2,1,0:T(8,128)S(1)}, u32[]{:S(2)}, u32[]{:S(2)}) async-start(f32[8,9,128]{2,1,0:T(8,128)} %sum_copies.11), calls=%async_computation.8 | async-start | bytes 131072 | tf_op jit(solution)/shard_map/all_to_all | solution.py:31
  159.2 4.6 %all-to-all-done.8.grams_ref = f32[8,9,128]{2,1,0:T(8,128)S(1)} async-done(((f32[8,9,128]{2,1,0:T(8,128)}), f32[8,9,128]{2,1,0:T(8,128)S(1)}, u32[]{:S(2)}, u32[]{:S(2)}) %all-to-all-start.8) | async-done | bytes 36896 | tf_op jit(solution)/shard_map/all_to_all | solution.py:31
  163.8 10.8 %second_step.1 = (f32[128,128]{1,0:T(8,128)S(1)}, f32[64,64]{1,0:T(8,128)S(1)}, f32[192,128]{1,0:T(8,128)S(1)}, f32[128,192]{1,0:T(8,128)S(1)}) custom-call(f32[12]{0:T(128)S(1)} %compare_select_fusion.4.weight_ref.refs_0_, s32[12]{0:T(128)S(1)} %fusion.4.index_ref.refs_1_, f32[8,73,128]{2,1,0:T(8,128)S(1)} %all_to_all.80.refs_0_.own_ref, ...), custom_call_target="tpu_custom_call" | custom-call | tf_op jit(solution)/shard_map/second_step/pallas_call | solution.py:39
  174.8 20.8 %all_to_all.81 = f32[128,1,192]{2,1,0:T(1,128)S(1)} all-to-all(f32[128,1,192]{2,1,0:T(1,128)S(1)} %copy.12), channel_id=1, replica_groups=mesh['grp'=4,'node'=128] {'node'}, dimensions={0} | all-to-all | bytes 196608 | tf_op jit(solution)/shard_map/all_to_all | solution.py:574
  196.2 3.2 %all-to-all-start.10 = ((f32[4,1,192]{2,1,0:T(1,128)}), f32[4,1,192]{2,1,0:T(1,128)S(1)}, u32[]{:S(2)}, u32[]{:S(2)}) async-start(f32[4,1,192]{2,1,0:T(1,128)} %copy.15), calls=%async_computation.10 | async-start | bytes 8192 | tf_op jit(solution)/shard_map/all_to_all | solution.py:574
  200.1 0.9 carry.1
  201.0 2.5 %all-to-all-done.10 = f32[4,1,192]{2,1,0:T(1,128)S(1)} async-done(((f32[4,1,192]{2,1,0:T(1,128)}), f32[4,1,192]{2,1,0:T(1,128)S(1)}, u32[]{:S(2)}, u32[]{:S(2)}) %all-to-all-start.10) | async-done | bytes 3104 | tf_op jit(solution)/shard_map/all_to_all | solution.py:574
  203.8 20.4 %all_to_all.82 = f32[128,1,384]{2,1,0:T(1,128)S(1)} all-to-all(f32[128,1,384]{2,1,0:T(1,128)S(1)} %copy.16), channel_id=1, replica_groups=mesh['grp'=4,'node'=128] {'node'}, dimensions={0} | all-to-all | bytes 393216 | tf_op jit(solution)/shard_map/all_to_all | solution.py:574
  224.2 12.1 %last_step.1 = (f32[64,64]{1,0:T(8,128)}, f32[64,128]{1,0:T(8,128)}) custom-call(f32[128,384]{1,0:T(8,128)S(1)} %bitcast.36, f32[256,128]{1,0:T(8,128)S(1)} %get-tuple-element.44.refs_1_, f32[64,64]{1,0:T(8,128)S(1)} %get-tuple-element.45.refs_2_), custom_call_target="tpu_custom_call" | custom-call | tf_op jit(solution)/shard_map/last_step/pallas_call | solution.py:39
  (33 shorter events, 5.4 us)
Async XLA Ops:
  0.6 0.8 copy-start.1
  18.2 38.2 %copy-start = (bf16[1,12,128,128]{3,2,1,0:T(8,128)(2,1)S(1)}, bf16[1,12,128,128]{3,2,1,0:T(8,128)(2,1)}, u32[]{:S(2)}) copy-start(bf16[1,12,128,128]{3,2,1,0:T(8,128)(2,1)} %param.7) | copy-start | bytes 1179652
  18.9 15.5 %collective-permute-start = (f32[8,68,128]{2,1,0:T(8,128)S(1)}, f32[8,68,128]{2,1,0:T(8,128)S(1)}, u32[]{:S(2)}, u32[]{:S(2)}) collective-permute-start(f32[8,68,128]{2,1,0:T(8,128)S(1)} %all_to_all.78.refs_0_.own_ref), channel_id=1, source_target_pairs={{0,2},{1,127},{2,4},{3,1},{4,6},{5,3},{6,8},{7,5},{8,10},{9,7},{10... | collective-permute-start | bytes 835592 | tf_op jit(solution)/shard_map/ppermute | solution.py:487
  28.8 16.5 %all-to-all-start.1 = ((f32[64,4,128]{2,1,0:T(4,128)}), f32[64,4,128]{2,1,0:T(4,128)S(1)}, u32[]{:S(2)}, u32[]{:S(2)}) async-start(f32[64,4,128]{2,1,0:T(4,128)} %sum_copies.6), calls=%async_computation.1 | async-start | bytes 262144 | tf_op jit(solution)/shard_map/all_to_all | solution.py:31
  34.4 3.2 %copy-start.5 = (f32[1,12]{1,0:T(1,128)S(1)}, f32[1,12]{1,0:T(1,128)}, u32[]{:S(2)}) copy-start(f32[1,12]{1,0:T(1,128)} %param.8) | copy-start | bytes 148
  34.4 22.0 %collective-permute-start.1 = (f32[8,68,128]{2,1,0:T(8,128)S(1)}, f32[8,68,128]{2,1,0:T(8,128)S(1)}, u32[]{:S(2)}, u32[]{:S(2)}) collective-permute-start(f32[8,68,128]{2,1,0:T(8,128)S(1)} %collective-permute-done.mine_ref), channel_id=1, source_target_pairs={{0,1},{1,0},{2,3},{3,2},{4,5},{5,4},{6,7},{7,6},{8,9},{9,8},{10,11... | collective-permute-start | bytes 835592 | tf_op jit(solution)/shard_map/ppermute | solution.py:488
  45.3 6.5 %copy-start.4 = (s32[1,12]{1,0:T(1,128)S(1)}, s32[1,12]{1,0:T(1,128)}, u32[]{:S(2)}) copy-start(s32[1,12]{1,0:T(1,128)} %param.9) | copy-start | bytes 148
  45.9 10.5 %copy-start.2 = (f32[64,128]{1,0:T(8,128)S(1)}, f32[64,128]{1,0:T(8,128)}, u32[]{:S(2)}) copy-start(f32[64,128]{1,0:T(8,128)} %start_ref.3) | copy-start | bytes 98308
  45.9 10.5 %all-to-all-start.2 = ((f32[8,4,128]{2,1,0:T(4,128)}), f32[8,4,128]{2,1,0:T(4,128)S(1)}, u32[]{:S(2)}, u32[]{:S(2)}) async-start(f32[8,4,128]{2,1,0:T(4,128)} %sum_copies.7), calls=%async_computation.2 | async-start | bytes 32768 | tf_op jit(solution)/shard_map/all_to_all | solution.py:31
  72.5 28.4 %all-to-all-start.4 = ((f32[64,9,128]{2,1,0:T(8,128)}), f32[64,9,128]{2,1,0:T(8,128)S(1)}, u32[]{:S(2)}, u32[]{:S(2)}) async-start(f32[64,9,128]{2,1,0:T(8,128)} %sum_copies.8), calls=%async_computation.4 | async-start | bytes 1048576 | tf_op jit(solution)/shard_map/all_to_all | solution.py:31
  77.1 16.7 %collective-permute-start.2 = (f32[8,73,128]{2,1,0:T(8,128)S(1)}, f32[8,73,128]{2,1,0:T(8,128)S(1)}, u32[]{:S(2)}, u32[]{:S(2)}) collective-permute-start(f32[8,73,128]{2,1,0:T(8,128)S(1)} %all_to_all.79.refs_0_.refs_2_), channel_id=1, source_target_pairs={{0,2},{1,127},{2,4},{3,1},{4,6},{5,3},{6,8},{7,5},{8,10},{9,7},{10... | collective-permute-start | bytes 897032 | tf_op jit(solution)/shard_map/ppermute | solution.py:487
  93.9 11.0 %collective-permute-start.3 = (f32[8,73,128]{2,1,0:T(8,128)S(1)}, f32[8,73,128]{2,1,0:T(8,128)S(1)}, u32[]{:S(2)}, u32[]{:S(2)}) collective-permute-start(f32[8,73,128]{2,1,0:T(8,128)S(1)} %collective-permute-done.2.refs_4_), channel_id=1, source_target_pairs={{0,1},{1,0},{2,3},{3,2},{4,5},{5,4},{6,7},{7,6},{8,9},{9,8},{10,11... | collective-permute-start | bytes 897032 | tf_op jit(solution)/shard_map/ppermute | solution.py:488
  101.5 8.1 %all-to-all-start.5 = ((f32[8,9,128]{2,1,0:T(8,128)}), f32[8,9,128]{2,1,0:T(8,128)S(1)}, u32[]{:S(2)}, u32[]{:S(2)}) async-start(f32[8,9,128]{2,1,0:T(8,128)} %sum_copies.9), calls=%async_computation.5 | async-start | bytes 131072 | tf_op jit(solution)/shard_map/all_to_all | solution.py:31
  124.3 30.7 %all-to-all-start.7 = ((f32[64,9,128]{2,1,0:T(8,128)}), f32[64,9,128]{2,1,0:T(8,128)S(1)}, u32[]{:S(2)}, u32[]{:S(2)}) async-start(f32[64,9,128]{2,1,0:T(8,128)} %sum_copies.10), calls=%async_computation.7 | async-start | bytes 1048576 | tf_op jit(solution)/shard_map/all_to_all | solution.py:31
  131.2 16.8 %collective-permute-start.4 = (f32[8,73,128]{2,1,0:T(8,128)S(1)}, f32[8,73,128]{2,1,0:T(8,128)S(1)}, u32[]{:S(2)}, u32[]{:S(2)}) collective-permute-start(f32[8,73,128]{2,1,0:T(8,128)S(1)} %all_to_all.80.refs_0_.own_ref), channel_id=1, source_target_pairs={{0,2},{1,127},{2,4},{3,1},{4,6},{5,3},{6,8},{7,5},{8,10},{9,7},{10... | collective-permute-start | bytes 897032 | tf_op jit(solution)/shard_map/ppermute | solution.py:487
  148.1 11.1 %collective-permute-start.5 = (f32[8,73,128]{2,1,0:T(8,128)S(1)}, f32[8,73,128]{2,1,0:T(8,128)S(1)}, u32[]{:S(2)}, u32[]{:S(2)}) collective-permute-start(f32[8,73,128]{2,1,0:T(8,128)S(1)} %collective-permute-done.4.mine_ref), channel_id=1, source_target_pairs={{0,1},{1,0},{2,3},{3,2},{4,5},{5,4},{6,7},{7,6},{8,9},{9,8},{10,11... | collective-permute-start | bytes 897032 | tf_op jit(solution)/shard_map/ppermute | solution.py:488
  155.7 8.1 %all-to-all-start.8 = ((f32[8,9,128]{2,1,0:T(8,128)}), f32[8,9,128]{2,1,0:T(8,128)S(1)}, u32[]{:S(2)}, u32[]{:S(2)}) async-start(f32[8,9,128]{2,1,0:T(8,128)} %sum_copies.11), calls=%async_computation.8 | async-start | bytes 131072 | tf_op jit(solution)/shard_map/all_to_all | solution.py:31
  196.2 7.4 %all-to-all-start.10 = ((f32[4,1,192]{2,1,0:T(1,128)}), f32[4,1,192]{2,1,0:T(1,128)S(1)}, u32[]{:S(2)}, u32[]{:S(2)}) async-start(f32[4,1,192]{2,1,0:T(1,128)} %copy.15), calls=%async_computation.10 | async-start | bytes 8192 | tf_op jit(solution)/shard_map/all_to_all | solution.py:574
  199.4 0.7 copy-start.3

commit v8 on v6

--- a/solution.py
+++ b/solution.py
@@ -11,6 +11,8 @@
 RADIUS = 0.18
 BOTH = ("grp", "node")
 CORE_X = (1, 128, 256)
+CORE = (1,)
+CORE_X1 = (1, 128)
 Y_Z = (2, 4, 8, 16, 32, 64)
 
 
@@ -209,17 +211,20 @@
     return coeffs, theta
 
 
-def load_packed(ref):
-    width = ref.shape[1] // 2
-    return jnp.concatenate([ref[:, :width], ref[:, width:]], axis=0)
+def load_square(gathered_ref):
+    members, _, width = gathered_ref.shape
+    packed = jnp.concatenate([gathered_ref[i] for i in range(members)], axis=0)
+    return jnp.concatenate([packed[:, : width // 2], packed[:, width // 2 :]], axis=0)
 
 
 def store_parcel(ref, value, partial):
-    members, rows = ref.shape[0], value.shape[0]
-    share = partial.shape[0] // members
-    for i in range(members):
+    rows = value.shape[0]
+    share = ref.shape[1] - rows
+    shares = partial.shape[0] // share
+    for i in range(ref.shape[0]):
+        first = share * (i % shares)
         ref[i, :rows] = value
-        ref[i, rows:] = partial[share * i : share * (i + 1)]
+        ref[i, rows:] = partial[first : first + share]
 
 
 def pack(matrix):
@@ -259,7 +264,7 @@
 
 
 def start_kernel(weight_ref, index_ref, own_ref, up_ref, down_ref, gram_ref, start_ref, tiles_ref, block_ref, block_slots_ref, applied_ref, parcel_ref):
-    inverse = inverse_factor(load_packed(gram_ref))
+    inverse = inverse_factor(load_square(gram_ref))
     block = nn(inverse, start_ref[...])
     block_ref[...] = block
 
@@ -276,7 +281,7 @@
 
 
 def first_kernel(root, weight_ref, index_ref, own_ref, up_ref, down_ref, sum_ref, block_ref, applied_ref, block_slots_ref, tiles_ref, theta_ref, start_theta_ref, residual_ref, residual_slots_ref, image_ref, parcel_ref, overlap_ref, applied_slots_ref):
-    product = load_packed(sum_ref)
+    product = load_square(sum_ref)
     theta = half_sum(product)
     overlap_ref[...] = product - theta
     theta_ref[...] = theta
@@ -306,11 +311,12 @@
     diagonal = jnp.sum(jnp.where(row == column, own, F32(0.0)), axis=0, keepdims=True)
     partial = jnp.concatenate([cross, both], axis=1)
     tail = jnp.concatenate([diagonal, jnp.zeros_like(diagonal)], axis=1)
-    members = parcel_ref.shape[0]
-    share = order // members
-    for i in range(members):
+    share = parcel_ref.shape[1] - order - 1
+    shares = order // share
+    for i in range(parcel_ref.shape[0]):
+        first = share * (i % shares)
         parcel_ref[i, :order] = image
-        parcel_ref[i, order : order + share] = partial[share * i : share * (i + 1)]
+        parcel_ref[i, order : order + share] = partial[first : first + share]
         parcel_ref[i, order + share :] = tail
 
 
@@ -469,24 +475,23 @@
     root = float(rows_dev * groups * nodes) ** 0.5
     slab = (columns, rows_dev)
     square = (columns, columns)
-    packed = (columns // 2, 2 * columns)
     slab_slots = ((slots,) + slab, F32)
 
-    def exchange(parcel):
+    def exchange(parcel, last):
         received = swap(parcel, CORE_X)
         partial = sum_copies(received, 2 ** len(Y_Z), columns)
         shared = swap(partial, Y_Z)
         later, _ = lax.optimization_barrier((received, partial))
         down = lax.ppermute(later, "node", to_next)
         up = lax.ppermute(later, "node", to_last)
-        summed = swap(sum_copies(shared, 2 ** len(CORE_X)), CORE_X)
+        summed = swap(sum_copies(shared, 2 ** len(last)), last)
         return (received, up, down), summed
 
     def parcel_of(share):
         return ((2 * groups, columns + share, rows_dev), F32)
 
-    small = parcel_of(columns // (4 * groups))
-    start_rows, gram = exchange(run(gram_kernel, "start_gram", [small], start_block)[0])
+    small = parcel_of(columns // 4)
+    start_rows, gram = exchange(run(gram_kernel, "start_gram", [small], start_block)[0], CORE)
     block, block_slots, applied, parcel = run(
         start_kernel,
         "start_step",
@@ -494,12 +499,12 @@
         weights,
         index,
         *start_rows,
-        gram.reshape(packed),
+        gram,
         start_block,
         tiles,
         scalars=2,
     )
-    applied_rows, theta_sum = exchange(parcel)
+    applied_rows, theta_sum = exchange(parcel, CORE)
     theta, start_theta, residual, residual_slots, image, parcel, overlap, applied_slots = run(
         lambda *refs: first_kernel(root, *refs),
         "first_residual",
@@ -509,21 +514,21 @@
             (slab, F32),
             slab_slots,
             (slab, F32),
-            parcel_of(columns // (2 * groups) + 1),
+            parcel_of(columns // 4 + 1),
             (square, F32),
             slab_slots,
         ],
         weights,
         index,
         *applied_rows,
-        theta_sum.reshape(packed),
+        theta_sum,
         block,
         applied,
         block_slots,
         tiles,
         scalars=2,
     )
-    image_rows, grams = exchange(parcel)
+    image_rows, grams = exchange(parcel, CORE_X1)
     coeffs, next_theta, trial, last_grams = run(
         second_kernel,
         "second_step",

time: 225 us -> 233 us (1.036)
  blocking collectives: 102 us -> 76.9 us
  starting transfers between devices: 59.5 us -> 77.1 us
  waiting for transfers between devices: 22.8 us -> 37.4 us
    all_to_all x5 -> x3, blocking collectives: 63.5 us -> 37.5 us  [swap(): lax.all_to_all(values, BOTH, split_axis=0, concat_axis=0, tiled=True, axi...]
    all_to_all x4 -> x6, starting transfers between devices: 30.5 us -> 47.9 us  [swap(): lax.all_to_all(values, BOTH, split_axis=0, concat_axis=0, tiled=True, axi...]
    all_to_all x4 -> x6, waiting for transfers between devices: 20.3 us -> 34.9 us  [swap(): lax.all_to_all(values, BOTH, split_axis=0, concat_axis=0, tiled=True, axi...]
  transfers between devices with their start and end apart: 11 -> 13, of which waited for: 5 -> 7; matrix products, arithmetic and copies ran while one was open for 0% -> 0% of each run, Pallas kernels for 1% -> 1%
where the time goes in v8:
time: 233 us; the launch traced here: 232 us
  starting transfers between devices  77.1 us (33%)
  blocking collectives  76.9 us (33%)
  waiting for transfers between devices  37.4 us (16%)
  Pallas kernels  36.5 us (16%)
  local copies, waits for them, and re-layouts  2.41 us (1%)
    all_to_all x6, starting transfers between devices, swap(): lax.all_to_all(values, BOTH, split_axis=0, concat_axis=0, tiled=True, axi...  47.9 us
    all_to_all x2, blocking collectives, over(): return lax.all_to_all(values, axis, split_axis=0, concat_axis=0, tiled=True)  39.4 us
    all_to_all x3, blocking collectives, swap(): lax.all_to_all(values, BOTH, split_axis=0, concat_axis=0, tiled=True, axi...  37.5 us
    pallas_call x14, Pallas kernels, run(): pl.pallas_call(kernel, out_shape=[jax.ShapeDtypeStruct(shape, dtype) for...  36.5 us
    all_to_all x6, waiting for transfers between devices, swap(): lax.all_to_all(values, BOTH, split_axis=0, concat_axis=0, tiled=True, axi...  34.9 us
    ppermute x3, starting transfers between devices, exchange(): up = lax.ppermute(later, 'node', to_last)  17.1 us
    ppermute x3, starting transfers between devices, exchange(): down = lax.ppermute(later, 'node', to_next)  8.89 us
  transfers between devices with their start and end apart: 13, of which 7 were waited for; matrix products, arithmetic and copies ran while one was open for 0% of the time, Pallas kernels for 1%

profile of v8, /device:TPU:1, one launch (start us, length us, event | category | flops | bytes accessed | tf_op | source)
XLA Modules:
  0.0 231.8 jit_solution(822279631497960419)
XLA Ops:
  1.6 16.8 %all_to_all.78.refs_0_.own_ref = f32[8,80,128]{2,1,0:T(8,128)S(1)} all-to-all(f32[8,80,128]{2,1,0:T(8,128)S(1)} %start_gram.1), channel_id=1, replica_groups={{0,1,128,129,256,257,384,385},{2,3,130,131,258,259,386,387},{4,5,132,13..., dimensions={0} | all-to-all | bytes 655360 | tf_op jit(solution)/shard_map/all_to_all | solution.py:33
  18.4 0.8 sum_copies.6
  19.2 12.8 %all-to-all-start.1 = ((f32[64,16,128]{2,1,0:T(8,128)}), f32[64,16,128]{2,1,0:T(8,128)S(1)}, u32[]{:S(2)}, u32[]{:S(2)}) async-start(f32[64,16,128]{2,1,0:T(8,128)} %sum_copies.6), calls=%async_computation.1 | async-start | bytes 1048576 | tf_op jit(solution)/shard_map/all_to_all | solution.py:33
  32.0 3.1 %collective-permute-start.1 = (f32[8,80,128]{2,1,0:T(8,128)S(1)}, f32[8,80,128]{2,1,0:T(8,128)S(1)}, u32[]{:S(2)}, u32[]{:S(2)}) collective-permute-start(f32[8,80,128]{2,1,0:T(8,128)S(1)} %all_to_all.78.refs_0_.own_ref), channel_id=1, source_target_pairs={{0,2},{1,3},{2,4},{3,5},{4,6},{5,7},{6,8},{7,9},{8,10},{9,11},{10,... | collective-permute-start | bytes 983048 | tf_op jit(solution)/shard_map/ppermute | solution.py:485
  35.1 5.7 %collective-permute-start = (f32[8,80,128]{2,1,0:T(8,128)S(1)}, f32[8,80,128]{2,1,0:T(8,128)S(1)}, u32[]{:S(2)}, u32[]{:S(2)}) collective-permute-start(f32[8,80,128]{2,1,0:T(8,128)S(1)} %all_to_all.78.refs_0_.own_ref), channel_id=1, source_target_pairs={{0,126},{1,127},{2,0},{3,1},{4,2},{5,3},{6,4},{7,5},{8,6},{9,7},{1... | collective-permute-start | bytes 983048 | tf_op jit(solution)/shard_map/ppermute | solution.py:486
  41.5 7.8 %all-to-all-done.1.refs_0_ = f32[64,16,128]{2,1,0:T(8,128)S(1)} async-done(((f32[64,16,128]{2,1,0:T(8,128)}), f32[64,16,128]{2,1,0:T(8,128)S(1)}, u32[]{:S(2)}, u32[]{:S(2)}) %all-to-all-start.1) | async-done | bytes 524320 | tf_op jit(solution)/shard_map/all_to_all | solution.py:33
  49.9 8.1 %all-to-all-start.2 = ((f32[2,16,128]{2,1,0:T(8,128)}), f32[2,16,128]{2,1,0:T(8,128)S(1)}, u32[]{:S(2)}, u32[]{:S(2)}) async-start(f32[2,16,128]{2,1,0:T(8,128)} %sum_copies.7), calls=%async_computation.2 | async-start | bytes 32768 | tf_op jit(solution)/shard_map/all_to_all | solution.py:33
  58.0 1.0 all-to-all-done.2.gram_ref
  59.1 4.6 %start_step.1 = (f32[64,128]{1,0:T(8,128)S(1)}, f32[12,64,128]{2,1,0:T(8,128)S(1)}, f32[64,128]{1,0:T(8,128)S(1)}, f32[8,80,128]{2,1,0:T(8,128)S(1)}) custom-call(f32[12]{0:T(128)S(1)} %compare_select_fusion.2.weight_ref.refs_0_, s32[12]{0:T(128)S(1)} %fusion.4.index_ref.refs_1_, f32[8,80,128]{2,1,0:T(8,128)S(1)} %all_to_all.78.refs_0_.own_ref, ...), custom_call_target="tpu_custom_call" | custom-call | tf_op jit(solution)/shard_map/start_step/pallas_call | solution.py:41
  63.6 10.3 %all_to_all.79.refs_0_.refs_2_ = f32[8,80,128]{2,1,0:T(8,128)S(1)} all-to-all(f32[8,80,128]{2,1,0:T(8,128)S(1)} %get-tuple-element.27), channel_id=1, replica_groups={{0,1,128,129,256,257,384,385},{2,3,130,131,258,259,386,387},{4,5,132,13..., dimensions={0} | all-to-all | bytes 655360 | tf_op jit(solution)/shard_map/all_to_all | solution.py:33
  74.7 4.8 %all-to-all-start.4 = ((f32[64,16,128]{2,1,0:T(8,128)}), f32[64,16,128]{2,1,0:T(8,128)S(1)}, u32[]{:S(2)}, u32[]{:S(2)}) async-start(f32[64,16,128]{2,1,0:T(8,128)} %sum_copies.8), calls=%async_computation.4 | async-start | bytes 1048576 | tf_op jit(solution)/shard_map/all_to_all | solution.py:33
  79.5 2.9 %collective-permute-start.3 = (f32[8,80,128]{2,1,0:T(8,128)S(1)}, f32[8,80,128]{2,1,0:T(8,128)S(1)}, u32[]{:S(2)}, u32[]{:S(2)}) collective-permute-start(f32[8,80,128]{2,1,0:T(8,128)S(1)} %all_to_all.79.refs_0_.refs_2_), channel_id=1, source_target_pairs={{0,2},{1,3},{2,4},{3,5},{4,6},{5,7},{6,8},{7,9},{8,10},{9,11},{10,... | collective-permute-start | bytes 983048 | tf_op jit(solution)/shard_map/ppermute | solution.py:485
  82.5 5.7 %collective-permute-start.2 = (f32[8,80,128]{2,1,0:T(8,128)S(1)}, f32[8,80,128]{2,1,0:T(8,128)S(1)}, u32[]{:S(2)}, u32[]{:S(2)}) collective-permute-start(f32[8,80,128]{2,1,0:T(8,128)S(1)} %all_to_all.79.refs_0_.refs_2_), channel_id=1, source_target_pairs={{0,126},{1,127},{2,0},{3,1},{4,2},{5,3},{6,4},{7,5},{8,6},{9,7},{1... | collective-permute-start | bytes 983048 | tf_op jit(solution)/shard_map/ppermute | solution.py:486
  88.1 8.7 %all-to-all-done.4.refs_0_ = f32[64,16,128]{2,1,0:T(8,128)S(1)} async-done(((f32[64,16,128]{2,1,0:T(8,128)}), f32[64,16,128]{2,1,0:T(8,128)S(1)}, u32[]{:S(2)}, u32[]{:S(2)}) %all-to-all-start.4) | async-done | bytes 524320 | tf_op jit(solution)/shard_map/all_to_all | solution.py:33
  97.4 8.0 %all-to-all-start.5 = ((f32[2,16,128]{2,1,0:T(8,128)}), f32[2,16,128]{2,1,0:T(8,128)S(1)}, u32[]{:S(2)}, u32[]{:S(2)}) async-start(f32[2,16,128]{2,1,0:T(8,128)} %sum_copies.9), calls=%async_computation.5 | async-start | bytes 32768 | tf_op jit(solution)/shard_map/all_to_all | solution.py:33
  105.4 1.0 all-to-all-done.5.refs_5_
  106.5 3.2 %first_residual.1 = (f32[64,64]{1,0:T(8,128)S(1)}, f32[64,64]{1,0:T(8,128)}, f32[64,128]{1,0:T(8,128)S(1)}, f32[12,64,128]{2,1,0:T(8,128)S(1)}, f32[64,128]{1,0:...) custom-call(f32[12]{0:T(128)S(1)} %compare_select_fusion.2.weight_ref.refs_0_, ...), custom_call_target="tpu_custom_call" | custom-call | tf_op jit(solution)/shard_map/first_residual/pallas_call | solution.py:41
  109.7 10.5 %all_to_all.80.refs_0_.own_ref = f32[8,81,128]{2,1,0:T(8,128)S(1)} all-to-all(f32[8,81,128]{2,1,0:T(8,128)S(1)} %get-tuple-element.32), channel_id=1, replica_groups={{0,1,128,129,256,257,384,385},{2,3,130,131,258,259,386,387},{4,5,132,13..., dimensions={0} | all-to-all | bytes 663552 | tf_op jit(solution)/shard_map/all_to_all | solution.py:33
  120.2 0.9 sum_copies.10
  121.1 4.9 %all-to-all-start.7 = ((f32[64,17,128]{2,1,0:T(8,128)}), f32[64,17,128]{2,1,0:T(8,128)S(1)}, u32[]{:S(2)}, u32[]{:S(2)}) async-start(f32[64,17,128]{2,1,0:T(8,128)} %sum_copies.10), calls=%async_computation.7 | async-start | bytes 1572864 | tf_op jit(solution)/shard_map/all_to_all | solution.py:33
  126.0 2.9 %collective-permute-start.5 = (f32[8,81,128]{2,1,0:T(8,128)S(1)}, f32[8,81,128]{2,1,0:T(8,128)S(1)}, u32[]{:S(2)}, u32[]{:S(2)}) collective-permute-start(f32[8,81,128]{2,1,0:T(8,128)S(1)} %all_to_all.80.refs_0_.own_ref), channel_id=1, source_target_pairs={{0,2},{1,3},{2,4},{3,5},{4,6},{5,7},{6,8},{7,9},{8,10},{9,11},{10,... | collective-permute-start | bytes 995336 | tf_op jit(solution)/shard_map/ppermute | solution.py:485
  128.9 5.7 %collective-permute-start.4 = (f32[8,81,128]{2,1,0:T(8,128)S(1)}, f32[8,81,128]{2,1,0:T(8,128)S(1)}, u32[]{:S(2)}, u32[]{:S(2)}) collective-permute-start(f32[8,81,128]{2,1,0:T(8,128)S(1)} %all_to_all.80.refs_0_.own_ref), channel_id=1, source_target_pairs={{0,126},{1,127},{2,0},{3,1},{4,2},{5,3},{6,4},{7,5},{8,6},{9,7},{1... | collective-permute-start | bytes 995336 | tf_op jit(solution)/shard_map/ppermute | solution.py:486
  134.6 13.2 %all-to-all-done.7.refs_0_ = f32[64,17,128]{2,1,0:T(8,128)S(1)} async-done(((f32[64,17,128]{2,1,0:T(8,128)}), f32[64,17,128]{2,1,0:T(8,128)S(1)}, u32[]{:S(2)}, u32[]{:S(2)}) %all-to-all-start.7) | async-done | bytes 557088 | tf_op jit(solution)/shard_map/all_to_all | solution.py:33
  148.4 9.3 %all-to-all-start.8 = ((f32[4,17,128]{2,1,0:T(8,128)}), f32[4,17,128]{2,1,0:T(8,128)S(1)}, u32[]{:S(2)}, u32[]{:S(2)}) async-start(f32[4,17,128]{2,1,0:T(8,128)} %sum_copies.11), calls=%async_computation.8 | async-start | bytes 98304 | tf_op jit(solution)/shard_map/all_to_all | solution.py:33
  157.8 3.2 %all-to-all-done.8.grams_ref = f32[4,17,128]{2,1,0:T(8,128)S(1)} async-done(((f32[4,17,128]{2,1,0:T(8,128)}), f32[4,17,128]{2,1,0:T(8,128)S(1)}, u32[]{:S(2)}, u32[]{:S(2)}) %all-to-all-start.8) | async-done | bytes 34848 | tf_op jit(solution)/shard_map/all_to_all | solution.py:33
  161.0 10.8 %second_step.1 = (f32[128,128]{1,0:T(8,128)S(1)}, f32[64,64]{1,0:T(8,128)S(1)}, f32[192,128]{1,0:T(8,128)S(1)}, f32[128,192]{1,0:T(8,128)S(1)}) custom-call(f32[12]{0:T(128)S(1)} %compare_select_fusion.2.weight_ref.refs_0_, s32[12]{0:T(128)S(1)} %fusion.4.index_ref.refs_1_, f32[8,81,128]{2,1,0:T(8,128)S(1)} %all_to_all.80.refs_0_.own_ref, ...), custom_call_target="tpu_custom_call" | custom-call | tf_op jit(solution)/shard_map/second_step/pallas_call | solution.py:41
  172.0 19.0 %all_to_all.81 = f32[128,1,192]{2,1,0:T(1,128)S(1)} all-to-all(f32[128,1,192]{2,1,0:T(1,128)S(1)} %copy.12), channel_id=1, replica_groups=mesh['grp'=4,'node'=128] {'node'}, dimensions={0} | all-to-all | bytes 196608 | tf_op jit(solution)/shard_map/all_to_all | solution.py:571
  191.6 3.2 %all-to-all-start.10 = ((f32[4,1,192]{2,1,0:T(1,128)}), f32[4,1,192]{2,1,0:T(1,128)S(1)}, u32[]{:S(2)}, u32[]{:S(2)}) async-start(f32[4,1,192]{2,1,0:T(1,128)} %copy.15), calls=%async_computation.10 | async-start | bytes 8192 | tf_op jit(solution)/shard_map/all_to_all | solution.py:571
  195.5 0.9 carry.1
  196.5 2.5 %all-to-all-done.10 = f32[4,1,192]{2,1,0:T(1,128)S(1)} async-done(((f32[4,1,192]{2,1,0:T(1,128)}), f32[4,1,192]{2,1,0:T(1,128)S(1)}, u32[]{:S(2)}, u32[]{:S(2)}) %all-to-all-start.10) | async-done | bytes 3104 | tf_op jit(solution)/shard_map/all_to_all | solution.py:571
  199.3 20.4 %all_to_all.82 = f32[128,1,384]{2,1,0:T(1,128)S(1)} all-to-all(f32[128,1,384]{2,1,0:T(1,128)S(1)} %copy.16), channel_id=1, replica_groups=mesh['grp'=4,'node'=128] {'node'}, dimensions={0} | all-to-all | bytes 393216 | tf_op jit(solution)/shard_map/all_to_all | solution.py:571
  219.7 12.1 %last_step.1 = (f32[64,64]{1,0:T(8,128)}, f32[64,128]{1,0:T(8,128)}) custom-call(f32[128,384]{1,0:T(8,128)S(1)} %bitcast.36, f32[256,128]{1,0:T(8,128)S(1)} %get-tuple-element.44.refs_1_, f32[64,64]{1,0:T(8,128)S(1)} %get-tuple-element.45.refs_2_), custom_call_target="tpu_custom_call" | custom-call | tf_op jit(solution)/shard_map/last_step/pallas_call | solution.py:41
  (45 shorter events, 5.6 us)
Async XLA Ops:
  0.6 0.8 copy-start.3
  19.2 21.6 %copy-start.10 = (s32[1,12]{1,0:T(1,128)S(1)}, s32[1,12]{1,0:T(1,128)}, u32[]{:S(2)}) copy-start(s32[1,12]{1,0:T(1,128)} %param.9) | copy-start | bytes 148
  19.2 22.3 %copy-start.11 = (f32[1,12]{1,0:T(1,128)S(1)}, f32[1,12]{1,0:T(1,128)}, u32[]{:S(2)}) copy-start(f32[1,12]{1,0:T(1,128)} %param.8) | copy-start | bytes 148
  19.2 30.1 %all-to-all-start.1 = ((f32[64,16,128]{2,1,0:T(8,128)}), f32[64,16,128]{2,1,0:T(8,128)S(1)}, u32[]{:S(2)}, u32[]{:S(2)}) async-start(f32[64,16,128]{2,1,0:T(8,128)} %sum_copies.6), calls=%async_computation.1 | async-start | bytes 1048576 | tf_op jit(solution)/shard_map/all_to_all | solution.py:33
  32.0 27.1 %copy-start = (bf16[1,12,128,128]{3,2,1,0:T(8,128)(2,1)S(1)}, bf16[1,12,128,128]{3,2,1,0:T(8,128)(2,1)}, u32[]{:S(2)}) copy-start(bf16[1,12,128,128]{3,2,1,0:T(8,128)(2,1)} %param.7) | copy-start | bytes 1179652
  32.0 26.0 %collective-permute-start.1 = (f32[8,80,128]{2,1,0:T(8,128)S(1)}, f32[8,80,128]{2,1,0:T(8,128)S(1)}, u32[]{:S(2)}, u32[]{:S(2)}) collective-permute-start(f32[8,80,128]{2,1,0:T(8,128)S(1)} %all_to_all.78.refs_0_.own_ref), channel_id=1, source_target_pairs={{0,2},{1,3},{2,4},{3,5},{4,6},{5,7},{6,8},{7,9},{8,10},{9,11},{10,... | collective-permute-start | bytes 983048 | tf_op jit(solution)/shard_map/ppermute | solution.py:485
  35.1 23.0 %collective-permute-start = (f32[8,80,128]{2,1,0:T(8,128)S(1)}, f32[8,80,128]{2,1,0:T(8,128)S(1)}, u32[]{:S(2)}, u32[]{:S(2)}) collective-permute-start(f32[8,80,128]{2,1,0:T(8,128)S(1)} %all_to_all.78.refs_0_.own_ref), channel_id=1, source_target_pairs={{0,126},{1,127},{2,0},{3,1},{4,2},{5,3},{6,4},{7,5},{8,6},{9,7},{1... | collective-permute-start | bytes 983048 | tf_op jit(solution)/shard_map/ppermute | solution.py:486
  49.9 9.2 %copy-start.4 = (f32[64,128]{1,0:T(8,128)S(1)}, f32[64,128]{1,0:T(8,128)}, u32[]{:S(2)}) copy-start(f32[64,128]{1,0:T(8,128)} %start_ref.3) | copy-start | bytes 98308
  49.9 9.2 %all-to-all-start.2 = ((f32[2,16,128]{2,1,0:T(8,128)}), f32[2,16,128]{2,1,0:T(8,128)S(1)}, u32[]{:S(2)}, u32[]{:S(2)}) async-start(f32[2,16,128]{2,1,0:T(8,128)} %sum_copies.7), calls=%async_computation.2 | async-start | bytes 32768 | tf_op jit(solution)/shard_map/all_to_all | solution.py:33
  74.7 22.0 %all-to-all-start.4 = ((f32[64,16,128]{2,1,0:T(8,128)}), f32[64,16,128]{2,1,0:T(8,128)S(1)}, u32[]{:S(2)}, u32[]{:S(2)}) async-start(f32[64,16,128]{2,1,0:T(8,128)} %sum_copies.8), calls=%async_computation.4 | async-start | bytes 1048576 | tf_op jit(solution)/shard_map/all_to_all | solution.py:33
  79.5 25.9 %collective-permute-start.3 = (f32[8,80,128]{2,1,0:T(8,128)S(1)}, f32[8,80,128]{2,1,0:T(8,128)S(1)}, u32[]{:S(2)}, u32[]{:S(2)}) collective-permute-start(f32[8,80,128]{2,1,0:T(8,128)S(1)} %all_to_all.79.refs_0_.refs_2_), channel_id=1, source_target_pairs={{0,2},{1,3},{2,4},{3,5},{4,6},{5,7},{6,8},{7,9},{8,10},{9,11},{10,... | collective-permute-start | bytes 983048 | tf_op jit(solution)/shard_map/ppermute | solution.py:485
  82.5 23.0 %collective-permute-start.2 = (f32[8,80,128]{2,1,0:T(8,128)S(1)}, f32[8,80,128]{2,1,0:T(8,128)S(1)}, u32[]{:S(2)}, u32[]{:S(2)}) collective-permute-start(f32[8,80,128]{2,1,0:T(8,128)S(1)} %all_to_all.79.refs_0_.refs_2_), channel_id=1, source_target_pairs={{0,126},{1,127},{2,0},{3,1},{4,2},{5,3},{6,4},{7,5},{8,6},{9,7},{1... | collective-permute-start | bytes 983048 | tf_op jit(solution)/shard_map/ppermute | solution.py:486
  97.4 9.0 %all-to-all-start.5 = ((f32[2,16,128]{2,1,0:T(8,128)}), f32[2,16,128]{2,1,0:T(8,128)S(1)}, u32[]{:S(2)}, u32[]{:S(2)}) async-start(f32[2,16,128]{2,1,0:T(8,128)} %sum_copies.9), calls=%async_computation.5 | async-start | bytes 32768 | tf_op jit(solution)/shard_map/all_to_all | solution.py:33
  109.6 10.5 %copy-start.1 = (f32[64,64]{1,0:T(8,128)}, f32[64,64]{1,0:T(8,128)S(1)}, u32[]{:S(2)}) copy-start(f32[64,64]{1,0:T(8,128)S(1)} %get-tuple-element.34.overlap_ref) | copy-start | bytes 49156
  109.7 10.5 %copy-start.5 = (f32[64,128]{1,0:T(8,128)}, f32[64,128]{1,0:T(8,128)S(1)}, u32[]{:S(2)}) copy-start(f32[64,128]{1,0:T(8,128)S(1)} %get-tuple-element.36.residual_ref) | copy-start | bytes 98308
  109.7 10.5 %copy-start.7 = (f32[64,128]{1,0:T(8,128)}, f32[64,128]{1,0:T(8,128)S(1)}, u32[]{:S(2)}) copy-start(f32[64,128]{1,0:T(8,128)S(1)} %get-tuple-element.37.image_ref) | copy-start | bytes 98308
  121.1 26.7 %all-to-all-start.7 = ((f32[64,17,128]{2,1,0:T(8,128)}), f32[64,17,128]{2,1,0:T(8,128)S(1)}, u32[]{:S(2)}, u32[]{:S(2)}) async-start(f32[64,17,128]{2,1,0:T(8,128)} %sum_copies.10), calls=%async_computation.7 | async-start | bytes 1572864 | tf_op jit(solution)/shard_map/all_to_all | solution.py:33
  126.0 31.8 %collective-permute-start.5 = (f32[8,81,128]{2,1,0:T(8,128)S(1)}, f32[8,81,128]{2,1,0:T(8,128)S(1)}, u32[]{:S(2)}, u32[]{:S(2)}) collective-permute-start(f32[8,81,128]{2,1,0:T(8,128)S(1)} %all_to_all.80.refs_0_.own_ref), channel_id=1, source_target_pairs={{0,2},{1,3},{2,4},{3,5},{4,6},{5,7},{6,8},{7,9},{8,10},{9,11},{10,... | collective-permute-start | bytes 995336 | tf_op jit(solution)/shard_map/ppermute | solution.py:485
  128.9 28.9 %collective-permute-start.4 = (f32[8,81,128]{2,1,0:T(8,128)S(1)}, f32[8,81,128]{2,1,0:T(8,128)S(1)}, u32[]{:S(2)}, u32[]{:S(2)}) collective-permute-start(f32[8,81,128]{2,1,0:T(8,128)S(1)} %all_to_all.80.refs_0_.own_ref), channel_id=1, source_target_pairs={{0,126},{1,127},{2,0},{3,1},{4,2},{5,3},{6,4},{7,5},{8,6},{9,7},{1... | collective-permute-start | bytes 995336 | tf_op jit(solution)/shard_map/ppermute | solution.py:486
  148.4 12.6 %copy-start.2 = (f32[64,64]{1,0:T(8,128)S(1)}, f32[64,64]{1,0:T(8,128)}, u32[]{:S(2)}) copy-start(f32[64,64]{1,0:T(8,128)} %copy-done.1) | copy-start | bytes 49156
  148.4 12.6 %copy-start.6 = (f32[64,128]{1,0:T(8,128)S(1)}, f32[64,128]{1,0:T(8,128)}, u32[]{:S(2)}) copy-start(f32[64,128]{1,0:T(8,128)} %copy-done.5) | copy-start | bytes 98308
  148.4 12.6 %copy-start.8 = (f32[64,128]{1,0:T(8,128)S(1)}, f32[64,128]{1,0:T(8,128)}, u32[]{:S(2)}) copy-start(f32[64,128]{1,0:T(8,128)} %copy-done.7) | copy-start | bytes 98308
  148.4 12.6 %all-to-all-start.8 = ((f32[4,17,128]{2,1,0:T(8,128)}), f32[4,17,128]{2,1,0:T(8,128)S(1)}, u32[]{:S(2)}, u32[]{:S(2)}) async-start(f32[4,17,128]{2,1,0:T(8,128)} %sum_copies.11), calls=%async_computation.8 | async-start | bytes 98304 | tf_op jit(solution)/shard_map/all_to_all | solution.py:33
  191.6 7.4 %all-to-all-start.10 = ((f32[4,1,192]{2,1,0:T(1,128)}), f32[4,1,192]{2,1,0:T(1,128)S(1)}, u32[]{:S(2)}, u32[]{:S(2)}) async-start(f32[4,1,192]{2,1,0:T(1,128)} %copy.15), calls=%async_computation.10 | async-start | bytes 8192 | tf_op jit(solution)/shard_map/all_to_all | solution.py:571
  194.9 0.7 copy-start.9

commit v9 on v6

--- a/solution.py
+++ b/solution.py
@@ -371,9 +371,9 @@
     old_trial = jnp.concatenate([block, previous], axis=0)
     old_applied = jnp.concatenate([applied, previous_image], axis=0)
     fresh = tn(both, jnp.concatenate([old_trial, old_applied], axis=1))
-    trial = jnp.concatenate([fresh[:columns, :width], residual, fresh[columns:, :width]], axis=0)
+    trial = jnp.concatenate([fresh[:, :width], residual], axis=0)
     trial_ref[...] = trial
-    applied_trial = jnp.concatenate([fresh[:columns, width:], image, fresh[columns:, width:]], axis=0)
+    applied_trial = jnp.concatenate([fresh[:, width:], image], axis=0)
     cross = 0.5 * (nt(image, trial) + nt(residual, applied_trial))
     grams_out_ref[...] = jnp.concatenate([nt(residual, trial), cross], axis=0)
 
@@ -390,9 +390,18 @@
         ],
         axis=0,
     )
-    carried_ref[...] = jnp.concatenate(
-        [tn(coeffs, nn(basis, coeffs)), tn(coeffs, nn(gram, coeffs))], axis=0
-    )
+    products = tn(coeffs, nn(basis, coeffs))
+    block_momentum = products[:columns, columns:]
+    factor = inverse_factor(products[columns:, columns:] - tn(block_momentum, block_momentum))
+    zero = jnp.zeros((columns, columns), F32)
+    inverse = jnp.concatenate(
+        [
+            jnp.concatenate([eye(columns), zero], axis=1),
+            jnp.concatenate([-nt(factor, block_momentum), factor], axis=1),
+        ],
+        axis=0,
+    )
+    carried_ref[...] = jnp.concatenate([inverse, tn(coeffs, nn(gram, coeffs))], axis=0)
     width = trial_ref.shape[1]
     place = lax.broadcasted_iota(jnp.int32, (width, width), 0)
     pick = jnp.where(place == order_ref[...], F32(1.0), F32(0.0))
@@ -406,40 +415,31 @@
     arrived = gathered_ref[:, width:]
     carried = carried_ref[...]
     wide = 2 * columns
-    overlap = jnp.concatenate([grams[:columns, :columns], carried[:columns, columns:wide]], axis=1)
-    mixed = grams[wide:, :columns]
-    spread = tn(overlap, overlap)
-    first = grams[columns:wide, :columns] - spread[:columns, :columns]
-    corner = mixed.T - spread[:columns, columns:]
-    second = carried[columns:wide, columns:wide] - spread[columns:, columns:]
-    factor = inverse_factor(first)
-    middle = nn(factor, corner)
-    other = inverse_factor(second - tn(middle, middle))
-    zero = jnp.zeros((columns, columns), F32)
-    lower = jnp.concatenate(
-        [
-            jnp.concatenate([factor, zero], axis=1),
-            jnp.concatenate([-nn(other, tn(middle, factor)), other], axis=1),
+    known = carried[:wide]
+    overlap = nn(known, grams[:wide, :columns])
+    factor = inverse_factor(grams[wide:, :columns] - tn(overlap, overlap))
+    linv = jnp.concatenate(
+        [
+            jnp.concatenate([known, jnp.zeros((wide, columns), F32)], axis=1),
+            jnp.concatenate([-nn(factor, tn(overlap, known)), factor], axis=1),
         ],
         axis=0,
     )
-    linv = jnp.concatenate(
-        [
-            jnp.concatenate([eye(columns), zero, zero], axis=1),
-            jnp.concatenate([-nt(lower, overlap), lower], axis=1),
+    cross = grams[:wide, columns:]
+    own = half_sum(grams[wide:, columns:])
+    block_momentum = carried[wide : wide + columns, columns:]
+    momentum = half_sum(carried[wide + columns :, columns:])
+    upper = jnp.concatenate(
+        [
+            jnp.concatenate([theta_ref[...], block_momentum], axis=1),
+            jnp.concatenate([block_momentum.T, momentum], axis=1),
         ],
         axis=0,
     )
-    cross = grams[:columns, columns:]
-    own = half_sum(grams[columns:wide, columns:])
-    momentum_cross = grams[wide:, columns:]
-    block_momentum = carried[wide : wide + columns, columns:wide]
-    momentum = half_sum(carried[wide + columns :, columns:wide])
     gram = jnp.concatenate(
         [
-            jnp.concatenate([theta_ref[...], cross, block_momentum], axis=1),
-            jnp.concatenate([cross.T, own, momentum_cross.T], axis=1),
-            jnp.concatenate([block_momentum.T, momentum_cross, momentum], axis=1),
+            jnp.concatenate([upper, cross], axis=1),
+            jnp.concatenate([cross.T, own], axis=1),
         ],
         axis=0,
     )

time: 225 us -> 222 us (0.987)
  waiting for transfers between devices: 22.8 us -> 20.4 us
    all_to_all x1, waiting for transfers between devices: 2.49 us -> 0.01 us  [over(): return lax.all_to_all(values, axis, split_axis=0, concat_axis=0, tiled=True)]
  transfers between devices with their start and end apart: 11 -> 11, of which waited for: 5 -> 4; matrix products, arithmetic and copies ran while one was open for 0% -> 0% of each run, Pallas kernels for 1% -> 2%
where the time goes in v9:
time: 222 us; the launch traced here: 221 us
  blocking collectives  101 us (45%)
  starting transfers between devices  59.8 us (27%)
  Pallas kernels  35 us (16%)
  waiting for transfers between devices  20.4 us (9%)
  local copies, waits for them, and re-layouts  3.04 us (1%)
    all_to_all x5, blocking collectives, swap(): lax.all_to_all(values, BOTH, split_axis=0, concat_axis=0, tiled=True, axi...  63.5 us
    all_to_all x2, blocking collectives, over(): return lax.all_to_all(values, axis, split_axis=0, concat_axis=0, tiled=True)  37.9 us
    pallas_call x14, Pallas kernels, run(): pl.pallas_call(kernel, out_shape=[jax.ShapeDtypeStruct(shape, dtype) for...  35 us
    all_to_all x4, starting transfers between devices, swap(): lax.all_to_all(values, BOTH, split_axis=0, concat_axis=0, tiled=True, axi...  30.5 us
    all_to_all x4, waiting for transfers between devices, swap(): lax.all_to_all(values, BOTH, split_axis=0, concat_axis=0, tiled=True, axi...  20.3 us
    ppermute x3, starting transfers between devices, exchange(): up = lax.ppermute(later, 'node', to_last)  18 us
    ppermute x3, starting transfers between devices, exchange(): down = lax.ppermute(later, 'node', to_next)  7.8 us
  transfers between devices with their start and end apart: 11, of which 4 were waited for; matrix products, arithmetic and copies ran while one was open for 0% of the time, Pallas kernels for 2%

profile of v9, /device:TPU:1, one launch (start us, length us, event | category | flops | bytes accessed | tf_op | source)
XLA Modules:
  0.0 221.1 jit_solution(16345227016847177172)
XLA Ops:
  0.6 0.7 copy-done.1
  1.6 16.6 %all_to_all.78.refs_0_.own_ref = f32[8,68,128]{2,1,0:T(8,128)S(1)} all-to-all(f32[8,68,128]{2,1,0:T(8,128)S(1)} %start_gram.1), channel_id=1, replica_groups={{0,1,128,129,256,257,384,385},{2,3,130,131,258,259,386,387},{4,5,132,13..., dimensions={0} | all-to-all | bytes 557056 | tf_op jit(solution)/shard_map/all_to_all | solution.py:31
  18.2 0.7 sum_copies.6
  18.9 12.7 %all-to-all-start.1 = ((f32[64,4,128]{2,1,0:T(4,128)}), f32[64,4,128]{2,1,0:T(4,128)S(1)}, u32[]{:S(2)}, u32[]{:S(2)}) async-start(f32[64,4,128]{2,1,0:T(4,128)} %sum_copies.6), calls=%async_computation.1 | async-start | bytes 262144 | tf_op jit(solution)/shard_map/all_to_all | solution.py:31
  31.6 2.9 %collective-permute-start.1 = (f32[8,68,128]{2,1,0:T(8,128)S(1)}, f32[8,68,128]{2,1,0:T(8,128)S(1)}, u32[]{:S(2)}, u32[]{:S(2)}) collective-permute-start(f32[8,68,128]{2,1,0:T(8,128)S(1)} %all_to_all.78.refs_0_.own_ref), channel_id=1, source_target_pairs={{0,2},{1,3},{2,4},{3,5},{4,6},{5,7},{6,8},{7,9},{8,10},{9,11},{10,... | collective-permute-start | bytes 835592 | tf_op jit(solution)/shard_map/ppermute | solution.py:480
  34.5 5.7 %collective-permute-start = (f32[8,68,128]{2,1,0:T(8,128)S(1)}, f32[8,68,128]{2,1,0:T(8,128)S(1)}, u32[]{:S(2)}, u32[]{:S(2)}) collective-permute-start(f32[8,68,128]{2,1,0:T(8,128)S(1)} %all_to_all.78.refs_0_.own_ref), channel_id=1, source_target_pairs={{0,126},{1,127},{2,0},{3,1},{4,2},{5,3},{6,4},{7,5},{8,6},{9,7},{1... | collective-permute-start | bytes 835592 | tf_op jit(solution)/shard_map/ppermute | solution.py:481
  40.9 2.7 %all-to-all-done.1.refs_0_ = f32[64,4,128]{2,1,0:T(4,128)S(1)} async-done(((f32[64,4,128]{2,1,0:T(4,128)}), f32[64,4,128]{2,1,0:T(4,128)S(1)}, u32[]{:S(2)}, u32[]{:S(2)}) %all-to-all-start.1) | async-done | bytes 131104 | tf_op jit(solution)/shard_map/all_to_all | solution.py:31
  44.3 5.3 %all-to-all-start.2 = ((f32[8,4,128]{2,1,0:T(4,128)}), f32[8,4,128]{2,1,0:T(4,128)S(1)}, u32[]{:S(2)}, u32[]{:S(2)}) async-start(f32[8,4,128]{2,1,0:T(4,128)} %sum_copies.7), calls=%async_computation.2 | async-start | bytes 32768 | tf_op jit(solution)/shard_map/all_to_all | solution.py:31
  49.6 0.7 copy-done.5
  50.3 4.0 %all-to-all-done.2 = f32[8,4,128]{2,1,0:T(4,128)S(1)} async-done(((f32[8,4,128]{2,1,0:T(4,128)}), f32[8,4,128]{2,1,0:T(4,128)S(1)}, u32[]{:S(2)}, u32[]{:S(2)}) %all-to-all-start.2) | async-done | bytes 16416 | tf_op jit(solution)/shard_map/all_to_all | solution.py:31
  54.3 4.6 %start_step.1 = (f32[64,128]{1,0:T(8,128)S(1)}, f32[12,64,128]{2,1,0:T(8,128)S(1)}, f32[64,128]{1,0:T(8,128)S(1)}, f32[8,68,128]{2,1,0:T(8,128)S(1)}) custom-call(f32[12]{0:T(128)S(1)} %compare_select_fusion.2.weight_ref.refs_0_, s32[12]{0:T(128)S(1)} %fusion.4.index_ref.refs_1_, f32[8,68,128]{2,1,0:T(8,128)S(1)} %all_to_all.78.refs_0_.own_ref, ...), custom_call_target="tpu_custom_call" | custom-call | tf_op jit(solution)/shard_map/start_step/pallas_call | solution.py:39
  58.9 10.5 %all_to_all.79.refs_0_.refs_2_ = f32[8,68,128]{2,1,0:T(8,128)S(1)} all-to-all(f32[8,68,128]{2,1,0:T(8,128)S(1)} %get-tuple-element.27), channel_id=1, replica_groups={{0,1,128,129,256,257,384,385},{2,3,130,131,258,259,386,387},{4,5,132,13..., dimensions={0} | all-to-all | bytes 557056 | tf_op jit(solution)/shard_map/all_to_all | solution.py:31
  69.3 2.1 collective-permute-start.3
  71.4 6.5 %collective-permute-start.2 = (f32[8,68,128]{2,1,0:T(8,128)S(1)}, f32[8,68,128]{2,1,0:T(8,128)S(1)}, u32[]{:S(2)}, u32[]{:S(2)}) collective-permute-start(f32[8,68,128]{2,1,0:T(8,128)S(1)} %all_to_all.79.refs_0_.refs_2_), channel_id=1, source_target_pairs={{0,126},{1,127},{2,0},{3,1},{4,2},{5,3},{6,4},{7,5},{8,6},{9,7},{1... | collective-permute-start | bytes 835592 | tf_op jit(solution)/shard_map/ppermute | solution.py:481
  78.0 16.3 %all_to_all.80.refs_0_ = f32[64,4,128]{2,1,0:T(4,128)S(1)} all-to-all(f32[64,4,128]{2,1,0:T(4,128)S(1)} %sum_copies.8), channel_id=1, replica_groups={{0,2,4,6,8,10,12,14,16,18,20,22,24,26,28,30,32,34,36,38,40,42,44,46,48,..., dimensions={0} | all-to-all | bytes 262144 | tf_op jit(solution)/shard_map/all_to_all | solution.py:31
  94.2 9.6 %all_to_all.81 = f32[8,4,128]{2,1,0:T(4,128)S(1)} all-to-all(f32[8,4,128]{2,1,0:T(4,128)S(1)} %sum_copies.9), channel_id=1, replica_groups={{0,1,128,129,256,257,384,385},{2,3,130,131,258,259,386,387},{4,5,132,13..., dimensions={0} | all-to-all | bytes 32768 | tf_op jit(solution)/shard_map/all_to_all | solution.py:31
  103.9 3.2 %first_residual.1 = (f32[64,64]{1,0:T(8,128)S(1)}, f32[64,64]{1,0:T(8,128)}, f32[64,128]{1,0:T(8,128)S(1)}, f32[12,64,128]{2,1,0:T(8,128)S(1)}, f32[64,128]{1,0:...) custom-call(f32[12]{0:T(128)S(1)} %compare_select_fusion.2.weight_ref.refs_0_, ...), custom_call_target="tpu_custom_call" | custom-call | tf_op jit(solution)/shard_map/first_residual/pallas_call | solution.py:39
  107.0 10.6 %all_to_all.82.refs_0_.own_ref = f32[8,73,128]{2,1,0:T(8,128)S(1)} all-to-all(f32[8,73,128]{2,1,0:T(8,128)S(1)} %get-tuple-element.32), channel_id=1, replica_groups={{0,1,128,129,256,257,384,385},{2,3,130,131,258,259,386,387},{4,5,132,13..., dimensions={0} | all-to-all | bytes 598016 | tf_op jit(solution)/shard_map/all_to_all | solution.py:31
  117.6 0.8 sum_copies.10
  118.4 4.6 %all-to-all-start.7 = ((f32[64,9,128]{2,1,0:T(8,128)}), f32[64,9,128]{2,1,0:T(8,128)S(1)}, u32[]{:S(2)}, u32[]{:S(2)}) async-start(f32[64,9,128]{2,1,0:T(8,128)} %sum_copies.10), calls=%async_computation.7 | async-start | bytes 1048576 | tf_op jit(solution)/shard_map/all_to_all | solution.py:31
  123.1 2.8 %collective-permute-start.5 = (f32[8,73,128]{2,1,0:T(8,128)S(1)}, f32[8,73,128]{2,1,0:T(8,128)S(1)}, u32[]{:S(2)}, u32[]{:S(2)}) collective-permute-start(f32[8,73,128]{2,1,0:T(8,128)S(1)} %all_to_all.82.refs_0_.own_ref), channel_id=1, source_target_pairs={{0,2},{1,3},{2,4},{3,5},{4,6},{5,7},{6,8},{7,9},{8,10},{9,11},{10,... | collective-permute-start | bytes 897032 | tf_op jit(solution)/shard_map/ppermute | solution.py:480
  125.9 5.8 %collective-permute-start.4 = (f32[8,73,128]{2,1,0:T(8,128)S(1)}, f32[8,73,128]{2,1,0:T(8,128)S(1)}, u32[]{:S(2)}, u32[]{:S(2)}) collective-permute-start(f32[8,73,128]{2,1,0:T(8,128)S(1)} %all_to_all.82.refs_0_.own_ref), channel_id=1, source_target_pairs={{0,126},{1,127},{2,0},{3,1},{4,2},{5,3},{6,4},{7,5},{8,6},{9,7},{1... | collective-permute-start | bytes 897032 | tf_op jit(solution)/shard_map/ppermute | solution.py:481
  131.7 8.7 %all-to-all-done.7.refs_0_ = f32[64,9,128]{2,1,0:T(8,128)S(1)} async-done(((f32[64,9,128]{2,1,0:T(8,128)}), f32[64,9,128]{2,1,0:T(8,128)S(1)}, u32[]{:S(2)}, u32[]{:S(2)}) %all-to-all-start.7) | async-done | bytes 294944 | tf_op jit(solution)/shard_map/all_to_all | solution.py:31
  140.4 0.7 sum_copies.11
  141.1 7.9 %all-to-all-start.8 = ((f32[8,9,128]{2,1,0:T(8,128)}), f32[8,9,128]{2,1,0:T(8,128)S(1)}, u32[]{:S(2)}, u32[]{:S(2)}) async-start(f32[8,9,128]{2,1,0:T(8,128)} %sum_copies.11), calls=%async_computation.8 | async-start | bytes 131072 | tf_op jit(solution)/shard_map/all_to_all | solution.py:31
  148.9 4.9 %all-to-all-done.8.grams_ref = f32[8,9,128]{2,1,0:T(8,128)S(1)} async-done(((f32[8,9,128]{2,1,0:T(8,128)}), f32[8,9,128]{2,1,0:T(8,128)S(1)}, u32[]{:S(2)}, u32[]{:S(2)}) %all-to-all-start.8) | async-done | bytes 36896 | tf_op jit(solution)/shard_map/all_to_all | solution.py:31
  153.8 10.8 %second_step.1 = (f32[128,128]{1,0:T(8,128)S(1)}, f32[64,64]{1,0:T(8,128)S(1)}, f32[192,128]{1,0:T(8,128)S(1)}, f32[128,192]{1,0:T(8,128)S(1)}) custom-call(f32[12]{0:T(128)S(1)} %compare_select_fusion.2.weight_ref.refs_0_, s32[12]{0:T(128)S(1)} %fusion.4.index_ref.refs_1_, f32[8,73,128]{2,1,0:T(8,128)S(1)} %all_to_all.82.refs_0_.own_ref, ...), custom_call_target="tpu_custom_call" | custom-call | tf_op jit(solution)/shard_map/second_step/pallas_call | solution.py:39
  164.7 18.4 %all_to_all.83 = f32[128,1,192]{2,1,0:T(1,128)S(1)} all-to-all(f32[128,1,192]{2,1,0:T(1,128)S(1)} %copy.12), channel_id=1, replica_groups=mesh['grp'=4,'node'=128] {'node'}, dimensions={0} | all-to-all | bytes 196608 | tf_op jit(solution)/shard_map/all_to_all | solution.py:566
  183.7 3.5 %all-to-all-start.10 = ((f32[4,1,192]{2,1,0:T(1,128)}), f32[4,1,192]{2,1,0:T(1,128)S(1)}, u32[]{:S(2)}, u32[]{:S(2)}) async-start(f32[4,1,192]{2,1,0:T(1,128)} %copy.15), calls=%async_computation.10 | async-start | bytes 8192 | tf_op jit(solution)/shard_map/all_to_all | solution.py:566
  187.9 3.8 %carry.1 = (f32[256,128]{1,0:T(8,128)S(1)}, f32[128,192]{1,0:T(8,128)S(1)}) custom-call(f32[128,128]{1,0:T(8,128)S(1)} %get-tuple-element.41.coeffs_ref, f32[8,9,128]{2,1,0:T(8,128)S(1)} %all-to-all-done.8.grams_ref, f32[64,64]{1,0:T(8,128)S(1)} %get-tuple-element.34.overlap_ref, f32[64,64]{1,0:T(8,128)S(1)} %get-tuple-element.35.theta_ref, ...), custom_call_target="tpu_custom_call" | custom-call | tf_op jit(solution)/shard_map/carry/pallas_call | solution.py:39
  192.0 19.6 %all_to_all.84 = f32[128,1,384]{2,1,0:T(1,128)S(1)} all-to-all(f32[128,1,384]{2,1,0:T(1,128)S(1)} %copy.16), channel_id=1, replica_groups=mesh['grp'=4,'node'=128] {'node'}, dimensions={0} | all-to-all | bytes 393216 | tf_op jit(solution)/shard_map/all_to_all | solution.py:566
  211.6 9.5 %last_step.1 = (f32[64,64]{1,0:T(8,128)}, f32[64,128]{1,0:T(8,128)}) custom-call(f32[128,384]{1,0:T(8,128)S(1)} %bitcast.38, f32[256,128]{1,0:T(8,128)S(1)} %get-tuple-element.44.refs_1_, f32[64,64]{1,0:T(8,128)S(1)} %get-tuple-element.45.refs_2_), custom_call_target="tpu_custom_call" | custom-call | tf_op jit(solution)/shard_map/last_step/pallas_call | solution.py:39
  (31 shorter events, 2.7 us)
Async XLA Ops:
  0.6 0.8 copy-start.1
  18.2 36.1 %copy-start = (bf16[1,12,128,128]{3,2,1,0:T(8,128)(2,1)S(1)}, bf16[1,12,128,128]{3,2,1,0:T(8,128)(2,1)}, u32[]{:S(2)}) copy-start(bf16[1,12,128,128]{3,2,1,0:T(8,128)(2,1)} %param.7) | copy-start | bytes 1179652
  18.9 24.8 %all-to-all-start.1 = ((f32[64,4,128]{2,1,0:T(4,128)}), f32[64,4,128]{2,1,0:T(4,128)S(1)}, u32[]{:S(2)}, u32[]{:S(2)}) async-start(f32[64,4,128]{2,1,0:T(4,128)} %sum_copies.6), calls=%async_computation.1 | async-start | bytes 262144 | tf_op jit(solution)/shard_map/all_to_all | solution.py:31
  31.6 8.6 %copy-start.4 = (s32[1,12]{1,0:T(1,128)S(1)}, s32[1,12]{1,0:T(1,128)}, u32[]{:S(2)}) copy-start(s32[1,12]{1,0:T(1,128)} %param.9) | copy-start | bytes 148
  31.6 22.7 %collective-permute-start.1 = (f32[8,68,128]{2,1,0:T(8,128)S(1)}, f32[8,68,128]{2,1,0:T(8,128)S(1)}, u32[]{:S(2)}, u32[]{:S(2)}) collective-permute-start(f32[8,68,128]{2,1,0:T(8,128)S(1)} %all_to_all.78.refs_0_.own_ref), channel_id=1, source_target_pairs={{0,2},{1,3},{2,4},{3,5},{4,6},{5,7},{6,8},{7,9},{8,10},{9,11},{10,... | collective-permute-start | bytes 835592 | tf_op jit(solution)/shard_map/ppermute | solution.py:480
  34.5 19.8 %collective-permute-start = (f32[8,68,128]{2,1,0:T(8,128)S(1)}, f32[8,68,128]{2,1,0:T(8,128)S(1)}, u32[]{:S(2)}, u32[]{:S(2)}) collective-permute-start(f32[8,68,128]{2,1,0:T(8,128)S(1)} %all_to_all.78.refs_0_.own_ref), channel_id=1, source_target_pairs={{0,126},{1,127},{2,0},{3,1},{4,2},{5,3},{6,4},{7,5},{8,6},{9,7},{1... | collective-permute-start | bytes 835592 | tf_op jit(solution)/shard_map/ppermute | solution.py:481
  44.3 10.0 %copy-start.2 = (f32[64,128]{1,0:T(8,128)S(1)}, f32[64,128]{1,0:T(8,128)}, u32[]{:S(2)}) copy-start(f32[64,128]{1,0:T(8,128)} %start_ref.3) | copy-start | bytes 98308
  44.3 10.0 %all-to-all-start.2 = ((f32[8,4,128]{2,1,0:T(4,128)}), f32[8,4,128]{2,1,0:T(4,128)S(1)}, u32[]{:S(2)}, u32[]{:S(2)}) async-start(f32[8,4,128]{2,1,0:T(4,128)} %sum_copies.7), calls=%async_computation.2 | async-start | bytes 32768 | tf_op jit(solution)/shard_map/all_to_all | solution.py:31
  49.6 0.7 copy-start.5
  69.3 34.5 %collective-permute-start.3 = (f32[8,68,128]{2,1,0:T(8,128)S(1)}, f32[8,68,128]{2,1,0:T(8,128)S(1)}, u32[]{:S(2)}, u32[]{:S(2)}) collective-permute-start(f32[8,68,128]{2,1,0:T(8,128)S(1)} %all_to_all.79.refs_0_.refs_2_), channel_id=1, source_target_pairs={{0,2},{1,3},{2,4},{3,5},{4,6},{5,7},{6,8},{7,9},{8,10},{9,11},{10,... | collective-permute-start | bytes 835592 | tf_op jit(solution)/shard_map/ppermute | solution.py:480
  71.4 32.4 %collective-permute-start.2 = (f32[8,68,128]{2,1,0:T(8,128)S(1)}, f32[8,68,128]{2,1,0:T(8,128)S(1)}, u32[]{:S(2)}, u32[]{:S(2)}) collective-permute-start(f32[8,68,128]{2,1,0:T(8,128)S(1)} %all_to_all.79.refs_0_.refs_2_), channel_id=1, source_target_pairs={{0,126},{1,127},{2,0},{3,1},{4,2},{5,3},{6,4},{7,5},{8,6},{9,7},{1... | collective-permute-start | bytes 835592 | tf_op jit(solution)/shard_map/ppermute | solution.py:481
  118.4 22.0 %all-to-all-start.7 = ((f32[64,9,128]{2,1,0:T(8,128)}), f32[64,9,128]{2,1,0:T(8,128)S(1)}, u32[]{:S(2)}, u32[]{:S(2)}) async-start(f32[64,9,128]{2,1,0:T(8,128)} %sum_copies.10), calls=%async_computation.7 | async-start | bytes 1048576 | tf_op jit(solution)/shard_map/all_to_all | solution.py:31
  123.1 25.9 %collective-permute-start.5 = (f32[8,73,128]{2,1,0:T(8,128)S(1)}, f32[8,73,128]{2,1,0:T(8,128)S(1)}, u32[]{:S(2)}, u32[]{:S(2)}) collective-permute-start(f32[8,73,128]{2,1,0:T(8,128)S(1)} %all_to_all.82.refs_0_.own_ref), channel_id=1, source_target_pairs={{0,2},{1,3},{2,4},{3,5},{4,6},{5,7},{6,8},{7,9},{8,10},{9,11},{10,... | collective-permute-start | bytes 897032 | tf_op jit(solution)/shard_map/ppermute | solution.py:480
  125.9 23.0 %collective-permute-start.4 = (f32[8,73,128]{2,1,0:T(8,128)S(1)}, f32[8,73,128]{2,1,0:T(8,128)S(1)}, u32[]{:S(2)}, u32[]{:S(2)}) collective-permute-start(f32[8,73,128]{2,1,0:T(8,128)S(1)} %all_to_all.82.refs_0_.own_ref), channel_id=1, source_target_pairs={{0,126},{1,127},{2,0},{3,1},{4,2},{5,3},{6,4},{7,5},{8,6},{9,7},{1... | collective-permute-start | bytes 897032 | tf_op jit(solution)/shard_map/ppermute | solution.py:481
  141.1 12.7 %all-to-all-start.8 = ((f32[8,9,128]{2,1,0:T(8,128)}), f32[8,9,128]{2,1,0:T(8,128)S(1)}, u32[]{:S(2)}, u32[]{:S(2)}) async-start(f32[8,9,128]{2,1,0:T(8,128)} %sum_copies.11), calls=%async_computation.8 | async-start | bytes 131072 | tf_op jit(solution)/shard_map/all_to_all | solution.py:31
  183.7 7.9 %all-to-all-start.10 = ((f32[4,1,192]{2,1,0:T(1,128)}), f32[4,1,192]{2,1,0:T(1,128)S(1)}, u32[]{:S(2)}, u32[]{:S(2)}) async-start(f32[4,1,192]{2,1,0:T(1,128)} %copy.15), calls=%async_computation.10 | async-start | bytes 8192 | tf_op jit(solution)/shard_map/all_to_all | solution.py:566
  187.2 0.7 copy-start.3

commit v10 on v9

--- a/solution.py
+++ b/solution.py
@@ -73,12 +73,13 @@
 
 
 def row_sum_kernel(parts_ref, out_ref):
-    summed = jnp.sum(parts_ref[...], axis=0, keepdims=True)
-    out_ref[...] = jnp.broadcast_to(summed, out_ref.shape)
+    summed = jnp.sum(parts_ref[...], axis=0)
+    for i in range(out_ref.shape[0]):
+        out_ref[i] = summed
 
 
 def gather_kernel(parts_ref, pieces_ref, out_ref):
-    summed = tree_sum([parts_ref[i : i + 1] for i in range(parts_ref.shape[0])])
+    summed = tree_sum([parts_ref[i] for i in range(parts_ref.shape[0])])
     rows, width = pieces_ref.shape
     out_ref[:, :width] = jnp.broadcast_to(summed, (rows, width))
     out_ref[:, width:] = pieces_ref[...]
@@ -566,7 +567,7 @@
         return lax.all_to_all(values, axis, split_axis=0, concat_axis=0, tiled=True)
 
     row_parts = run(
-        row_sum_kernel, "row_sum", [((groups, 3 * columns), F32)], over(last_grams, "node")
+        row_sum_kernel, "row_sum", [((groups, 1, 3 * columns), F32)], over(last_grams[:, None], "node")
     )[0]
     gathered = over(
         run(

time: 222 us -> 222 us (level)
  no operation moved by 1% of the time
where the time goes in v10:
time: 222 us; the launch traced here: 221 us
  blocking collectives  101 us (45%)
  starting transfers between devices  59.8 us (27%)
  Pallas kernels  35.7 us (16%)
  waiting for transfers between devices  20.4 us (9%)
  local copies, waits for them, and re-layouts  2.43 us (1%)
    all_to_all x5, blocking collectives, swap(): lax.all_to_all(values, BOTH, split_axis=0, concat_axis=0, tiled=True, axi...  63.5 us
    all_to_all x2, blocking collectives, over(): return lax.all_to_all(values, axis, split_axis=0, concat_axis=0, tiled=True)  37.9 us
    pallas_call x14, Pallas kernels, run(): pl.pallas_call(kernel, out_shape=[jax.ShapeDtypeStruct(shape, dtype) for...  35.7 us
    all_to_all x4, starting transfers between devices, swap(): lax.all_to_all(values, BOTH, split_axis=0, concat_axis=0, tiled=True, axi...  30.5 us
    all_to_all x4, waiting for transfers between devices, swap(): lax.all_to_all(values, BOTH, split_axis=0, concat_axis=0, tiled=True, axi...  20.3 us
    ppermute x3, starting transfers between devices, exchange(): up = lax.ppermute(later, 'node', to_last)  18 us
    ppermute x3, starting transfers between devices, exchange(): down = lax.ppermute(later, 'node', to_next)  7.8 us
  transfers between devices with their start and end apart: 11, of which 4 were waited for; matrix products, arithmetic and copies ran while one was open for 0% of the time, Pallas kernels for 2%

profile of v10, /device:TPU:1, one launch (start us, length us, event | category | flops | bytes accessed | tf_op | source)
XLA Modules:
  0.0 221.2 jit_solution(12383118413020213811)
XLA Ops:
  0.6 0.7 copy-done.1
  1.6 16.6 %all_to_all.66.refs_0_.own_ref = f32[8,68,128]{2,1,0:T(8,128)S(1)} all-to-all(f32[8,68,128]{2,1,0:T(8,128)S(1)} %start_gram.1), channel_id=1, replica_groups={{0,1,128,129,256,257,384,385},{2,3,130,131,258,259,386,387},{4,5,132,13..., dimensions={0} | all-to-all | bytes 557056 | tf_op jit(solution)/shard_map/all_to_all | solution.py:31
  18.2 0.7 sum_copies.6
  18.9 12.7 %all-to-all-start.1 = ((f32[64,4,128]{2,1,0:T(4,128)}), f32[64,4,128]{2,1,0:T(4,128)S(1)}, u32[]{:S(2)}, u32[]{:S(2)}) async-start(f32[64,4,128]{2,1,0:T(4,128)} %sum_copies.6), calls=%async_computation.1 | async-start | bytes 262144 | tf_op jit(solution)/shard_map/all_to_all | solution.py:31
  31.6 2.9 %collective-permute-start.1 = (f32[8,68,128]{2,1,0:T(8,128)S(1)}, f32[8,68,128]{2,1,0:T(8,128)S(1)}, u32[]{:S(2)}, u32[]{:S(2)}) collective-permute-start(f32[8,68,128]{2,1,0:T(8,128)S(1)} %all_to_all.66.refs_0_.own_ref), channel_id=1, source_target_pairs={{0,2},{1,3},{2,4},{3,5},{4,6},{5,7},{6,8},{7,9},{8,10},{9,11},{10,... | collective-permute-start | bytes 835592 | tf_op jit(solution)/shard_map/ppermute | solution.py:481
  34.5 5.7 %collective-permute-start = (f32[8,68,128]{2,1,0:T(8,128)S(1)}, f32[8,68,128]{2,1,0:T(8,128)S(1)}, u32[]{:S(2)}, u32[]{:S(2)}) collective-permute-start(f32[8,68,128]{2,1,0:T(8,128)S(1)} %all_to_all.66.refs_0_.own_ref), channel_id=1, source_target_pairs={{0,126},{1,127},{2,0},{3,1},{4,2},{5,3},{6,4},{7,5},{8,6},{9,7},{1... | collective-permute-start | bytes 835592 | tf_op jit(solution)/shard_map/ppermute | solution.py:482
  40.9 2.7 %all-to-all-done.1.refs_0_ = f32[64,4,128]{2,1,0:T(4,128)S(1)} async-done(((f32[64,4,128]{2,1,0:T(4,128)}), f32[64,4,128]{2,1,0:T(4,128)S(1)}, u32[]{:S(2)}, u32[]{:S(2)}) %all-to-all-start.1) | async-done | bytes 131104 | tf_op jit(solution)/shard_map/all_to_all | solution.py:31
  44.3 5.3 %all-to-all-start.2 = ((f32[8,4,128]{2,1,0:T(4,128)}), f32[8,4,128]{2,1,0:T(4,128)S(1)}, u32[]{:S(2)}, u32[]{:S(2)}) async-start(f32[8,4,128]{2,1,0:T(4,128)} %sum_copies.7), calls=%async_computation.2 | async-start | bytes 32768 | tf_op jit(solution)/shard_map/all_to_all | solution.py:31
  50.3 4.0 %all-to-all-done.2 = f32[8,4,128]{2,1,0:T(4,128)S(1)} async-done(((f32[8,4,128]{2,1,0:T(4,128)}), f32[8,4,128]{2,1,0:T(4,128)S(1)}, u32[]{:S(2)}, u32[]{:S(2)}) %all-to-all-start.2) | async-done | bytes 16416 | tf_op jit(solution)/shard_map/all_to_all | solution.py:31
  54.3 4.6 %start_step.1 = (f32[64,128]{1,0:T(8,128)S(1)}, f32[12,64,128]{2,1,0:T(8,128)S(1)}, f32[64,128]{1,0:T(8,128)S(1)}, f32[8,68,128]{2,1,0:T(8,128)S(1)}) custom-call(f32[12]{0:T(128)S(1)} %compare_select_fusion.2.weight_ref.refs_0_, s32[12]{0:T(128)S(1)} %fusion.4.index_ref.refs_1_, f32[8,68,128]{2,1,0:T(8,128)S(1)} %all_to_all.66.refs_0_.own_ref, ...), custom_call_target="tpu_custom_call" | custom-call | tf_op jit(solution)/shard_map/start_step/pallas_call | solution.py:39
  58.9 10.5 %all_to_all.67.refs_0_.refs_2_ = f32[8,68,128]{2,1,0:T(8,128)S(1)} all-to-all(f32[8,68,128]{2,1,0:T(8,128)S(1)} %get-tuple-element.27), channel_id=1, replica_groups={{0,1,128,129,256,257,384,385},{2,3,130,131,258,259,386,387},{4,5,132,13..., dimensions={0} | all-to-all | bytes 557056 | tf_op jit(solution)/shard_map/all_to_all | solution.py:31
  69.3 2.1 collective-permute-start.3
  71.4 6.5 %collective-permute-start.2 = (f32[8,68,128]{2,1,0:T(8,128)S(1)}, f32[8,68,128]{2,1,0:T(8,128)S(1)}, u32[]{:S(2)}, u32[]{:S(2)}) collective-permute-start(f32[8,68,128]{2,1,0:T(8,128)S(1)} %all_to_all.67.refs_0_.refs_2_), channel_id=1, source_target_pairs={{0,126},{1,127},{2,0},{3,1},{4,2},{5,3},{6,4},{7,5},{8,6},{9,7},{1... | collective-permute-start | bytes 835592 | tf_op jit(solution)/shard_map/ppermute | solution.py:482
  78.0 16.3 %all_to_all.68.refs_0_ = f32[64,4,128]{2,1,0:T(4,128)S(1)} all-to-all(f32[64,4,128]{2,1,0:T(4,128)S(1)} %sum_copies.8), channel_id=1, replica_groups={{0,2,4,6,8,10,12,14,16,18,20,22,24,26,28,30,32,34,36,38,40,42,44,46,48,..., dimensions={0} | all-to-all | bytes 262144 | tf_op jit(solution)/shard_map/all_to_all | solution.py:31
  94.2 9.6 %all_to_all.69 = f32[8,4,128]{2,1,0:T(4,128)S(1)} all-to-all(f32[8,4,128]{2,1,0:T(4,128)S(1)} %sum_copies.9), channel_id=1, replica_groups={{0,1,128,129,256,257,384,385},{2,3,130,131,258,259,386,387},{4,5,132,13..., dimensions={0} | all-to-all | bytes 32768 | tf_op jit(solution)/shard_map/all_to_all | solution.py:31
  103.9 3.2 %first_residual.1 = (f32[64,64]{1,0:T(8,128)S(1)}, f32[64,64]{1,0:T(8,128)}, f32[64,128]{1,0:T(8,128)S(1)}, f32[12,64,128]{2,1,0:T(8,128)S(1)}, f32[64,128]{1,0:...) custom-call(f32[12]{0:T(128)S(1)} %compare_select_fusion.2.weight_ref.refs_0_, ...), custom_call_target="tpu_custom_call" | custom-call | tf_op jit(solution)/shard_map/first_residual/pallas_call | solution.py:39
  107.0 10.6 %all_to_all.70.refs_0_.own_ref = f32[8,73,128]{2,1,0:T(8,128)S(1)} all-to-all(f32[8,73,128]{2,1,0:T(8,128)S(1)} %get-tuple-element.32), channel_id=1, replica_groups={{0,1,128,129,256,257,384,385},{2,3,130,131,258,259,386,387},{4,5,132,13..., dimensions={0} | all-to-all | bytes 598016 | tf_op jit(solution)/shard_map/all_to_all | solution.py:31
  117.6 0.8 sum_copies.10
  118.4 4.6 %all-to-all-start.7 = ((f32[64,9,128]{2,1,0:T(8,128)}), f32[64,9,128]{2,1,0:T(8,128)S(1)}, u32[]{:S(2)}, u32[]{:S(2)}) async-start(f32[64,9,128]{2,1,0:T(8,128)} %sum_copies.10), calls=%async_computation.7 | async-start | bytes 1048576 | tf_op jit(solution)/shard_map/all_to_all | solution.py:31
  123.1 2.8 %collective-permute-start.5 = (f32[8,73,128]{2,1,0:T(8,128)S(1)}, f32[8,73,128]{2,1,0:T(8,128)S(1)}, u32[]{:S(2)}, u32[]{:S(2)}) collective-permute-start(f32[8,73,128]{2,1,0:T(8,128)S(1)} %all_to_all.70.refs_0_.own_ref), channel_id=1, source_target_pairs={{0,2},{1,3},{2,4},{3,5},{4,6},{5,7},{6,8},{7,9},{8,10},{9,11},{10,... | collective-permute-start | bytes 897032 | tf_op jit(solution)/shard_map/ppermute | solution.py:481
  125.9 5.8 %collective-permute-start.4 = (f32[8,73,128]{2,1,0:T(8,128)S(1)}, f32[8,73,128]{2,1,0:T(8,128)S(1)}, u32[]{:S(2)}, u32[]{:S(2)}) collective-permute-start(f32[8,73,128]{2,1,0:T(8,128)S(1)} %all_to_all.70.refs_0_.own_ref), channel_id=1, source_target_pairs={{0,126},{1,127},{2,0},{3,1},{4,2},{5,3},{6,4},{7,5},{8,6},{9,7},{1... | collective-permute-start | bytes 897032 | tf_op jit(solution)/shard_map/ppermute | solution.py:482
  131.7 8.7 %all-to-all-done.7.refs_0_ = f32[64,9,128]{2,1,0:T(8,128)S(1)} async-done(((f32[64,9,128]{2,1,0:T(8,128)}), f32[64,9,128]{2,1,0:T(8,128)S(1)}, u32[]{:S(2)}, u32[]{:S(2)}) %all-to-all-start.7) | async-done | bytes 294944 | tf_op jit(solution)/shard_map/all_to_all | solution.py:31
  140.4 0.7 sum_copies.11
  141.1 7.9 %all-to-all-start.8 = ((f32[8,9,128]{2,1,0:T(8,128)}), f32[8,9,128]{2,1,0:T(8,128)S(1)}, u32[]{:S(2)}, u32[]{:S(2)}) async-start(f32[8,9,128]{2,1,0:T(8,128)} %sum_copies.11), calls=%async_computation.8 | async-start | bytes 131072 | tf_op jit(solution)/shard_map/all_to_all | solution.py:31
  148.9 4.9 %all-to-all-done.8.grams_ref = f32[8,9,128]{2,1,0:T(8,128)S(1)} async-done(((f32[8,9,128]{2,1,0:T(8,128)}), f32[8,9,128]{2,1,0:T(8,128)S(1)}, u32[]{:S(2)}, u32[]{:S(2)}) %all-to-all-start.8) | async-done | bytes 36896 | tf_op jit(solution)/shard_map/all_to_all | solution.py:31
  153.8 10.8 %second_step.1 = (f32[128,128]{1,0:T(8,128)S(1)}, f32[64,64]{1,0:T(8,128)S(1)}, f32[192,128]{1,0:T(8,128)S(1)}, f32[128,192]{1,0:T(8,128)S(1)}) custom-call(f32[12]{0:T(128)S(1)} %compare_select_fusion.2.weight_ref.refs_0_, s32[12]{0:T(128)S(1)} %fusion.4.index_ref.refs_1_, f32[8,73,128]{2,1,0:T(8,128)S(1)} %all_to_all.70.refs_0_.own_ref, ...), custom_call_target="tpu_custom_call" | custom-call | tf_op jit(solution)/shard_map/second_step/pallas_call | solution.py:39
  164.7 18.3 %all_to_all.71.parts_ref = f32[128,1,192]{2,1,0:T(1,128)S(1)} all-to-all(f32[128,1,192]{2,1,0:T(1,128)S(1)} %copy.12), channel_id=1, replica_groups=mesh['grp'=4,'node'=128] {'node'}, dimensions={0} | all-to-all | bytes 196608 | tf_op jit(solution)/shard_map/all_to_all | solution.py:567
  183.1 0.7 row_sum.1
  183.8 3.5 %all-to-all-start.10 = ((f32[4,1,192]{2,1,0:T(1,128)}), f32[4,1,192]{2,1,0:T(1,128)S(1)}, u32[]{:S(2)}, u32[]{:S(2)}) async-start(f32[4,1,192]{2,1,0:T(1,128)} %row_sum.1), calls=%async_computation.10 | async-start | bytes 8192 | tf_op jit(solution)/shard_map/all_to_all | solution.py:567
  188.0 3.8 %carry.1 = (f32[256,128]{1,0:T(8,128)S(1)}, f32[128,192]{1,0:T(8,128)S(1)}) custom-call(f32[128,128]{1,0:T(8,128)S(1)} %get-tuple-element.41.coeffs_ref, f32[8,9,128]{2,1,0:T(8,128)S(1)} %all-to-all-done.8.grams_ref, f32[64,64]{1,0:T(8,128)S(1)} %get-tuple-element.34.overlap_ref, f32[64,64]{1,0:T(8,128)S(1)} %get-tuple-element.35.theta_ref, ...), custom_call_target="tpu_custom_call" | custom-call | tf_op jit(solution)/shard_map/carry/pallas_call | solution.py:39
  192.0 19.6 %all_to_all.72 = f32[128,1,384]{2,1,0:T(1,128)S(1)} all-to-all(f32[128,1,384]{2,1,0:T(1,128)S(1)} %copy.13), channel_id=1, replica_groups=mesh['grp'=4,'node'=128] {'node'}, dimensions={0} | all-to-all | bytes 393216 | tf_op jit(solution)/shard_map/all_to_all | solution.py:567
  211.7 9.5 %last_step.1 = (f32[64,64]{1,0:T(8,128)}, f32[64,128]{1,0:T(8,128)}) custom-call(f32[128,384]{1,0:T(8,128)S(1)} %bitcast.30, f32[256,128]{1,0:T(8,128)S(1)} %get-tuple-element.44.refs_1_, f32[64,64]{1,0:T(8,128)S(1)} %get-tuple-element.45.refs_2_), custom_call_target="tpu_custom_call" | custom-call | tf_op jit(solution)/shard_map/last_step/pallas_call | solution.py:39
  (28 shorter events, 2.7 us)
Async XLA Ops:
  0.6 0.8 copy-start.1
  18.2 36.1 %copy-start = (bf16[1,12,128,128]{3,2,1,0:T(8,128)(2,1)S(1)}, bf16[1,12,128,128]{3,2,1,0:T(8,128)(2,1)}, u32[]{:S(2)}) copy-start(bf16[1,12,128,128]{3,2,1,0:T(8,128)(2,1)} %param.7) | copy-start | bytes 1179652
  18.9 24.8 %all-to-all-start.1 = ((f32[64,4,128]{2,1,0:T(4,128)}), f32[64,4,128]{2,1,0:T(4,128)S(1)}, u32[]{:S(2)}, u32[]{:S(2)}) async-start(f32[64,4,128]{2,1,0:T(4,128)} %sum_copies.6), calls=%async_computation.1 | async-start | bytes 262144 | tf_op jit(solution)/shard_map/all_to_all | solution.py:31
  31.6 8.6 %copy-start.4 = (s32[1,12]{1,0:T(1,128)S(1)}, s32[1,12]{1,0:T(1,128)}, u32[]{:S(2)}) copy-start(s32[1,12]{1,0:T(1,128)} %param.9) | copy-start | bytes 148
  31.6 22.7 %collective-permute-start.1 = (f32[8,68,128]{2,1,0:T(8,128)S(1)}, f32[8,68,128]{2,1,0:T(8,128)S(1)}, u32[]{:S(2)}, u32[]{:S(2)}) collective-permute-start(f32[8,68,128]{2,1,0:T(8,128)S(1)} %all_to_all.66.refs_0_.own_ref), channel_id=1, source_target_pairs={{0,2},{1,3},{2,4},{3,5},{4,6},{5,7},{6,8},{7,9},{8,10},{9,11},{10,... | collective-permute-start | bytes 835592 | tf_op jit(solution)/shard_map/ppermute | solution.py:481
  34.5 19.8 %collective-permute-start = (f32[8,68,128]{2,1,0:T(8,128)S(1)}, f32[8,68,128]{2,1,0:T(8,128)S(1)}, u32[]{:S(2)}, u32[]{:S(2)}) collective-permute-start(f32[8,68,128]{2,1,0:T(8,128)S(1)} %all_to_all.66.refs_0_.own_ref), channel_id=1, source_target_pairs={{0,126},{1,127},{2,0},{3,1},{4,2},{5,3},{6,4},{7,5},{8,6},{9,7},{1... | collective-permute-start | bytes 835592 | tf_op jit(solution)/shard_map/ppermute | solution.py:482
  44.3 10.0 %copy-start.2 = (f32[64,128]{1,0:T(8,128)S(1)}, f32[64,128]{1,0:T(8,128)}, u32[]{:S(2)}) copy-start(f32[64,128]{1,0:T(8,128)} %start_ref.3) | copy-start | bytes 98308
  44.3 10.0 %all-to-all-start.2 = ((f32[8,4,128]{2,1,0:T(4,128)}), f32[8,4,128]{2,1,0:T(4,128)S(1)}, u32[]{:S(2)}, u32[]{:S(2)}) async-start(f32[8,4,128]{2,1,0:T(4,128)} %sum_copies.7), calls=%async_computation.2 | async-start | bytes 32768 | tf_op jit(solution)/shard_map/all_to_all | solution.py:31
  49.6 0.7 copy-start.5
  69.3 34.5 %collective-permute-start.3 = (f32[8,68,128]{2,1,0:T(8,128)S(1)}, f32[8,68,128]{2,1,0:T(8,128)S(1)}, u32[]{:S(2)}, u32[]{:S(2)}) collective-permute-start(f32[8,68,128]{2,1,0:T(8,128)S(1)} %all_to_all.67.refs_0_.refs_2_), channel_id=1, source_target_pairs={{0,2},{1,3},{2,4},{3,5},{4,6},{5,7},{6,8},{7,9},{8,10},{9,11},{10,... | collective-permute-start | bytes 835592 | tf_op jit(solution)/shard_map/ppermute | solution.py:481
  71.4 32.4 %collective-permute-start.2 = (f32[8,68,128]{2,1,0:T(8,128)S(1)}, f32[8,68,128]{2,1,0:T(8,128)S(1)}, u32[]{:S(2)}, u32[]{:S(2)}) collective-permute-start(f32[8,68,128]{2,1,0:T(8,128)S(1)} %all_to_all.67.refs_0_.refs_2_), channel_id=1, source_target_pairs={{0,126},{1,127},{2,0},{3,1},{4,2},{5,3},{6,4},{7,5},{8,6},{9,7},{1... | collective-permute-start | bytes 835592 | tf_op jit(solution)/shard_map/ppermute | solution.py:482
  118.4 22.0 %all-to-all-start.7 = ((f32[64,9,128]{2,1,0:T(8,128)}), f32[64,9,128]{2,1,0:T(8,128)S(1)}, u32[]{:S(2)}, u32[]{:S(2)}) async-start(f32[64,9,128]{2,1,0:T(8,128)} %sum_copies.10), calls=%async_computation.7 | async-start | bytes 1048576 | tf_op jit(solution)/shard_map/all_to_all | solution.py:31
  123.1 25.9 %collective-permute-start.5 = (f32[8,73,128]{2,1,0:T(8,128)S(1)}, f32[8,73,128]{2,1,0:T(8,128)S(1)}, u32[]{:S(2)}, u32[]{:S(2)}) collective-permute-start(f32[8,73,128]{2,1,0:T(8,128)S(1)} %all_to_all.70.refs_0_.own_ref), channel_id=1, source_target_pairs={{0,2},{1,3},{2,4},{3,5},{4,6},{5,7},{6,8},{7,9},{8,10},{9,11},{10,... | collective-permute-start | bytes 897032 | tf_op jit(solution)/shard_map/ppermute | solution.py:481
  125.9 23.0 %collective-permute-start.4 = (f32[8,73,128]{2,1,0:T(8,128)S(1)}, f32[8,73,128]{2,1,0:T(8,128)S(1)}, u32[]{:S(2)}, u32[]{:S(2)}) collective-permute-start(f32[8,73,128]{2,1,0:T(8,128)S(1)} %all_to_all.70.refs_0_.own_ref), channel_id=1, source_target_pairs={{0,126},{1,127},{2,0},{3,1},{4,2},{5,3},{6,4},{7,5},{8,6},{9,7},{1... | collective-permute-start | bytes 897032 | tf_op jit(solution)/shard_map/ppermute | solution.py:482
  141.1 12.7 %all-to-all-start.8 = ((f32[8,9,128]{2,1,0:T(8,128)}), f32[8,9,128]{2,1,0:T(8,128)S(1)}, u32[]{:S(2)}, u32[]{:S(2)}) async-start(f32[8,9,128]{2,1,0:T(8,128)} %sum_copies.11), calls=%async_computation.8 | async-start | bytes 131072 | tf_op jit(solution)/shard_map/all_to_all | solution.py:31
  183.8 7.9 %all-to-all-start.10 = ((f32[4,1,192]{2,1,0:T(1,128)}), f32[4,1,192]{2,1,0:T(1,128)S(1)}, u32[]{:S(2)}, u32[]{:S(2)}) async-start(f32[4,1,192]{2,1,0:T(1,128)} %row_sum.1), calls=%async_computation.10 | async-start | bytes 8192 | tf_op jit(solution)/shard_map/all_to_all | solution.py:567
  187.3 0.7 copy-start.3
